TPU v7x, 256 devices: a whole 4x4x8 slice. The times are simulated.
256 devices in a mesh: dom: 16 (over y, z_lo, core), dir: 16 (over x, z_hi).
Axes of the slice: x: 4, y: 4, z: 8 (z_hi: 4, z_lo: 2; z = z_hi * 2 + z_lo), core: 2. Of those that a mesh axis runs over, the one named last changes fastest.
Arguments:
- coefficients: bfloat16 [2, 70, 32768], P(None, None, ('dom', 'dir')), may hold values from -6 to 6
- positions: float32 [3, 32768], P(None, ('dom', 'dir')), may hold values from -50 to 50
- polar: float32 [10240], P('dir'), may hold values from 0 to 1.4
- azimuth: float32 [10240], P('dir'), may hold values from -3.140625 to 3.140625
- weights: float32 [10240], P('dir'), may hold values from -4 to 4
- farmap: float32 [2, 2, 70, 10240], P(None, None, None, 'dir'), may hold values from -0.00390625 to 0.00390625
Outputs:
- coef_grad: float32 [2, 70, 32768], P(None, None, ('dom', 'dir'))
- place_grad: float32 [3, 32768], P(None, ('dom', 'dir'))
All inputs are finite; a program needn't handle non-finite values.
Results may differ from a plain program's by a relative error of at most 0.0052.
Values may be sent and summed in bfloat16 or wider, within the bound.
A program may use at most 64 MiB of HBM per device.

v0:
```python
import jax
import jax.numpy as jnp
from jax import lax
from jax.sharding import PartitionSpec as P

C = 70


def unit_vectors(polar, azimuth):
    sine_polar = jnp.sin(polar)
    return jnp.stack([sine_polar * jnp.cos(azimuth), sine_polar * jnp.sin(azimuth), jnp.cos(polar)])


def phase_tile(places, vectors):
    angles = (
        places[0][:, None] * vectors[0][None, :]
        + places[1][:, None] * vectors[1][None, :]
        + places[2][:, None] * vectors[2][None, :]
    )
    return (jnp.cos(angles).astype(jnp.bfloat16), jnp.sin(angles).astype(jnp.bfloat16))


def field_terms(coef_block, cos_tile, sin_tile):
    order_count = coef_block.shape[0] // 2
    real_rows = coef_block[:order_count]
    imag_rows = coef_block[order_count:]
    top_rows = jnp.concatenate([real_rows, imag_rows], axis=1)
    low_rows = jnp.concatenate([imag_rows, -real_rows], axis=1)
    left_side = jnp.concatenate([top_rows, low_rows], axis=0)
    right_side = jnp.concatenate([cos_tile, sin_tile], axis=0)
    return jnp.dot(left_side, right_side, preferred_element_type=jnp.float32)


def adjoint_terms(stacked, cos_tile, sin_tile):
    order_count = stacked.shape[0] // 2
    real_rows = stacked[:order_count]
    imag_rows = stacked[order_count:]
    top_rows = jnp.concatenate([real_rows, imag_rows], axis=1)
    low_rows = jnp.concatenate([imag_rows, -real_rows], axis=1)
    left_side = jnp.concatenate([top_rows, low_rows], axis=0)
    right_side = jnp.concatenate([cos_tile, sin_tile], axis=1)
    return lax.dot_general(
        left_side, right_side, (((1,), (1,)), ((), ())), preferred_element_type=jnp.float32
    )


def amplitude_parts(fields, farmap):
    order_count = fields.shape[0] // 2
    field_real = fields[:order_count][None]
    field_imag = fields[order_count:][None]
    map_real = farmap[:, 0]
    map_imag = farmap[:, 1]
    amp_real = jnp.sum(map_real * field_real - map_imag * field_imag, axis=1)
    amp_imag = jnp.sum(map_real * field_imag + map_imag * field_real, axis=1)
    return (amp_real, amp_imag)


def cotangent_from(amp_real, amp_imag, farmap, weights):
    map_real = farmap[:, 0]
    map_imag = farmap[:, 1]
    cot_real = weights * jnp.sum(
        amp_real[:, None] * map_real + amp_imag[:, None] * map_imag, axis=0
    )
    cot_imag = weights * jnp.sum(
        amp_real[:, None] * map_imag - amp_imag[:, None] * map_real, axis=0
    )
    return jnp.concatenate([cot_real, cot_imag], axis=0).astype(jnp.bfloat16)


def cotangent_rows(fields, farmap, weights):
    amp_real, amp_imag = amplitude_parts(fields, farmap)
    return cotangent_from(amp_real, amp_imag, farmap, weights)


def stacked_rows(adjoint, vectors):
    order_count = adjoint.shape[0] // 2
    widened = adjoint.astype(jnp.float32)
    scaled = [(vectors[axis_id][None, :] * widened).astype(jnp.bfloat16) for axis_id in range(3)]
    real_parts = [adjoint[:order_count]] + [item[:order_count] for item in scaled]
    imag_parts = [adjoint[order_count:]] + [item[order_count:] for item in scaled]
    return jnp.concatenate(real_parts + imag_parts, axis=0)


def gradients(output, coef_block):
    order_count = coef_block.shape[0] // 2
    real_out = output[: 4 * order_count]
    imag_out = output[4 * order_count :]
    coef_term = jnp.concatenate(
        [2.0 * real_out[:order_count], -2.0 * imag_out[:order_count]], axis=0
    )
    coef_real = coef_block[:order_count].astype(jnp.float32)
    coef_imag = coef_block[order_count:].astype(jnp.float32)
    place_terms = []
    for axis_id in range(3):
        lower_row = (axis_id + 1) * order_count
        upper_row = (axis_id + 2) * order_count
        place_terms.append(
            2.0
            * jnp.sum(
                coef_real * imag_out[lower_row:upper_row]
                + coef_imag * real_out[lower_row:upper_row],
                axis=0,
            )
        )
    return (coef_term, jnp.stack(place_terms))


def body(coefficients, positions, polar, azimuth, weights, farmap):
    own_count = coefficients.shape[2]
    own_rows = coefficients.reshape(2 * C, own_count)
    domain_rows = lax.all_gather(own_rows, "dir", axis=1, tiled=True)
    domain_places = lax.all_gather(positions, "dir", axis=1, tiled=True)
    vectors = unit_vectors(polar, azimuth)
    width_all = domain_rows.shape[1]
    width_block = 512
    blocks = width_all // width_block

    def forward_block(block_id, totals):
        offset = block_id * width_block
        coef_block = lax.dynamic_slice_in_dim(domain_rows, offset, width_block, 1)
        place_block = lax.dynamic_slice_in_dim(domain_places, offset, width_block, 1)
        cos_tile, sin_tile = phase_tile(place_block, vectors)
        return totals + field_terms(coef_block, cos_tile, sin_tile)

    partial_fields = lax.fori_loop(
        0, blocks, forward_block, jnp.zeros((2 * C, polar.shape[0]), jnp.float32)
    )
    fields = lax.psum(partial_fields, "dom")
    adjoint = cotangent_rows(fields, farmap, weights)
    stacked = stacked_rows(adjoint, vectors)

    def backward_block(block_id):
        offset = block_id * width_block
        coef_block = lax.dynamic_slice_in_dim(domain_rows, offset, width_block, 1)
        place_block = lax.dynamic_slice_in_dim(domain_places, offset, width_block, 1)
        cos_tile, sin_tile = phase_tile(place_block, vectors)
        return gradients(adjoint_terms(stacked, cos_tile, sin_tile), coef_block)

    coef_parts, place_parts = lax.map(backward_block, jnp.arange(blocks, dtype=jnp.int32))
    coef_part = jnp.moveaxis(coef_parts, 0, 1).reshape(2 * C, width_all)
    place_part = jnp.moveaxis(place_parts, 0, 1).reshape(3, width_all)
    coef_grad, place_grad = (
        lax.psum_scatter(coef_part, "dir", scatter_dimension=1, tiled=True),
        lax.psum_scatter(place_part, "dir", scatter_dimension=1, tiled=True),
    )
    return (coef_grad.reshape(2, C, own_count), place_grad)


def solution(mesh):
    placed = (
        P(None, None, ("dom", "dir")),
        P(None, ("dom", "dir")),
        P("dir"),
        P("dir"),
        P("dir"),
        P(None, None, None, "dir"),
    )
    return jax.shard_map(
        body,
        mesh=mesh,
        in_specs=placed,
        out_specs=(P(None, None, ("dom", "dir")), P(None, ("dom", "dir"))),
        check_vma=False,
    )
```

profile of v0, /device:TPU:32, one launch (start us, length us, event | category | flops | bytes accessed | tf_op | source)
XLA Modules:
  0.0 477.6 jit_solution(2724014570653692775)
XLA Ops:
  7.2 0.7 fusion.36
  7.9 0.7 sine_multiply_fusion
  8.7 0.8 copy.18
  9.5 49.2 %all_gather.7 = bf16[140,2048]{1,0:T(8,128)(2,1)S(1)} all-gather(bf16[140,128]{1,0:T(8,128)(2,1)S(1)} %reshape.65), channel_id=1, replica_groups=mesh['dom'=16,'dir'=16] {'dir'}, dimensions={1}, use_global_device_ids=true | all-gather | bytes 609280 | tf_op jit(solution)/shard_map/all_gather | solution.py:111
  58.8 38.4 %all_gather.6 = f32[3,2048]{1,0:T(4,128)S(1)} all-gather(f32[3,128]{1,0:T(4,128)} %param.11), channel_id=1, replica_groups=mesh['dom'=16,'dir'=16] {'dir'}, dimensions={1}, use_global_device_ids=true | all-gather | bytes 26112 | tf_op jit(solution)/shard_map/all_gather | solution.py:112
  97.2 24.7 %while.29 = (s32[]{:T(128)}, f32[140,640]{1,0:T(8,128)S(1)}, bf16[140,2048]{1,0:T(8,128)(2,1)S(1)}, f32[3,2048]{1,0:T(4,128)S(1)}, f32[1,640]{1,0:T(1,128)S(1)},...) while((s32[]{:T(128)}, f32[140,640]{1,0:T(8,128)S(1)}, ...), condition=%wide.region_1.0_spmd.clone, body=%wide.region_0.0_spmd.clone.sunk | while | flops 189849616 | bytes 3953417 | solution.py:125
  97.3 5.4 %cosine_convert_fusion.5 = (bf16[512,640]{1,0:T(8,128)(2,1)S(1)}, bf16[512,640]{1,0:T(8,128)(2,1)S(1)}) fusion(f32[640]{0:T(1024)S(1)} %reduce.15, f32[512]{0:T(512)S(1)} %bitcast.83, f32[640]{0:T(1024)S(1)} %reduce.16, f32[512]{0:T(512)S(1)} %bitcast.82, f32[640]{0:T(1024)S(1)} %reduce.17, f32[512]{0:T(512)S(1)} %bitcast.81), kind=kLoop, calls=%fused_computation.35.clone.1 | loop fusion | flops 2293760 | bytes 1324544 | tf_op jit(solution)/shard_map/while/body/eval_jaxpr/convert_element_type | solution.py:20
  102.8 0.1 fusion.54
  102.9 0.4 fusion.55
  103.3 0.1 constant_dynamic-slice_fusion.7
  103.5 5.4 %cosine_convert_fusion.5 = (bf16[512,640]{1,0:T(8,128)(2,1)S(1)}, bf16[512,640]{1,0:T(8,128)(2,1)S(1)}) fusion(f32[640]{0:T(1024)S(1)} %reduce.15, f32[512]{0:T(512)S(1)} %bitcast.83, f32[640]{0:T(1024)S(1)} %reduce.16, f32[512]{0:T(512)S(1)} %bitcast.82, f32[640]{0:T(1024)S(1)} %reduce.17, f32[512]{0:T(512)S(1)} %bitcast.81), kind=kLoop, calls=%fused_computation.35.clone.1 | loop fusion | flops 2293760 | bytes 1324544 | tf_op jit(solution)/shard_map/while/body/eval_jaxpr/convert_element_type | solution.py:20
  108.9 0.1 fusion.54
  109.1 0.4 fusion.55
  109.5 0.1 constant_dynamic-slice_fusion.7
  109.7 5.4 %cosine_convert_fusion.5 = (bf16[512,640]{1,0:T(8,128)(2,1)S(1)}, bf16[512,640]{1,0:T(8,128)(2,1)S(1)}) fusion(f32[640]{0:T(1024)S(1)} %reduce.15, f32[512]{0:T(512)S(1)} %bitcast.83, f32[640]{0:T(1024)S(1)} %reduce.16, f32[512]{0:T(512)S(1)} %bitcast.82, f32[640]{0:T(1024)S(1)} %reduce.17, f32[512]{0:T(512)S(1)} %bitcast.81), kind=kLoop, calls=%fused_computation.35.clone.1 | loop fusion | flops 2293760 | bytes 1324544 | tf_op jit(solution)/shard_map/while/body/eval_jaxpr/convert_element_type | solution.py:20
  115.1 0.1 fusion.54
  115.2 0.4 fusion.55
  115.7 0.1 constant_dynamic-slice_fusion.7
  115.8 5.4 %cosine_convert_fusion.5 = (bf16[512,640]{1,0:T(8,128)(2,1)S(1)}, bf16[512,640]{1,0:T(8,128)(2,1)S(1)}) fusion(f32[640]{0:T(1024)S(1)} %reduce.15, f32[512]{0:T(512)S(1)} %bitcast.83, f32[640]{0:T(1024)S(1)} %reduce.16, f32[512]{0:T(512)S(1)} %bitcast.82, f32[640]{0:T(1024)S(1)} %reduce.17, f32[512]{0:T(512)S(1)} %bitcast.81), kind=kLoop, calls=%fused_computation.35.clone.1 | loop fusion | flops 2293760 | bytes 1324544 | tf_op jit(solution)/shard_map/while/body/eval_jaxpr/convert_element_type | solution.py:20
  121.3 0.1 fusion.54
  121.4 0.4 fusion.55
  121.9 0.7 copy-done.1
  122.6 0.2 reduce-scatter.7.cloned.1.call-start
  122.9 0.6 fusion.31
  123.4 116.2 %all-reduce.2.cloned.1.call-done = f32[140,640]{1,0:T(8,128)} async-done(((f32[140,640]{1,0:T(8,128)}), f32[140,640]{1,0:T(8,128)}) %all-reduce.2.cloned.1.call-update) | async-done | bytes 358416 | tf_op jit(solution)/shard_map/psum | solution.py:128
  239.7 1.0 fusion.32
  240.7 0.1 subtract_reduce_fusion.1
  240.9 0.1 add_reduce_fusion
  241.0 0.1 fusion.27
  241.2 0.1 maximum_negate_fusion
  241.3 14.7 %maximum_maximum_fusion = bf16[560,1280]{1,0:T(8,128)(2,1)S(1)} fusion(bf16[280,640]{1,0:T(8,128)(2,1)S(1)} %maximum_negate_fusion, bf16[70,640]{1,0:T(8,128)(2,1)S(1)} %get-tuple-element.343, bf16[70,640]{1,0:T(8,128)(2,1)S(1)} %get-tuple-element.355, bf16[70,640]{1,0:T(8,128)(2,1)S(1)} %get-tuple-element.339, bf16[70,640]{1,0:T(8,128)(2,1)S(1)} %get-tuple-element.351, ...), kind=kLoop, calls=%fused_computation.48 | loop fusion | flops 18636800 | bytes 2508800 | tf_op jit(solution)/shard_map/while/body/eval_jaxpr/concatenate | solution.py:40
  256.0 35.1 %while.28 = (s32[]{:T(128)}, f32[4,140,512]{2,1,0:T(8,128)}, f32[4,3,512]{2,1,0:T(4,128)S(1)}, s32[4]{0:T(128)S(1)}, f32[3,2048]{1,0:T(4,128)S(1)}, /*index=5*/f...) while((s32[]{:T(128)}, f32[4,140,512]{2,1,0:T(8,128)}, ...), condition=%wide.region_11.12_spmd, body=%wide.region_7.11_spmd.sunk | while | flops 739566592 | bytes 7435559 | solution.py:139
  256.1 0.6 dynamic_slice.33
  257.4 5.4 %cosine_convert_fusion.4 = (bf16[512,640]{1,0:T(8,128)(2,1)S(1)}, bf16[512,640]{1,0:T(8,128)(2,1)S(1)}) fusion(f32[640]{0:T(1024)S(1)} %reduce.12, f32[512]{0:T(512)S(1)} %bitcast.86, f32[640]{0:T(1024)S(1)} %reduce.13, f32[512]{0:T(512)S(1)} %bitcast.85, f32[640]{0:T(1024)S(1)} %reduce.14, f32[512]{0:T(512)S(1)} %bitcast.84), kind=kLoop, calls=%fused_computation.5.clone.1 | loop fusion | flops 2293760 | bytes 1324544 | tf_op jit(solution)/shard_map/while/body/eval_jaxpr/convert_element_type | solution.py:20
  262.9 0.9 convolution_bitcast_fusion.2
  263.8 0.2 fusion.49
  264.1 0.7 fusion.50
  264.8 0.6 dynamic_slice.33
  266.1 0.1 constant_dynamic-slice_fusion.6
  266.2 5.4 %cosine_convert_fusion.4 = (bf16[512,640]{1,0:T(8,128)(2,1)S(1)}, bf16[512,640]{1,0:T(8,128)(2,1)S(1)}) fusion(f32[640]{0:T(1024)S(1)} %reduce.12, f32[512]{0:T(512)S(1)} %bitcast.86, f32[640]{0:T(1024)S(1)} %reduce.13, f32[512]{0:T(512)S(1)} %bitcast.85, f32[640]{0:T(1024)S(1)} %reduce.14, f32[512]{0:T(512)S(1)} %bitcast.84), kind=kLoop, calls=%fused_computation.5.clone.1 | loop fusion | flops 2293760 | bytes 1324544 | tf_op jit(solution)/shard_map/while/body/eval_jaxpr/convert_element_type | solution.py:20
  271.7 0.9 convolution_bitcast_fusion.2
  272.6 0.2 fusion.49
  272.9 0.7 fusion.50
  273.6 0.6 dynamic_slice.33
  274.9 0.1 constant_dynamic-slice_fusion.6
  275.0 5.4 %cosine_convert_fusion.4 = (bf16[512,640]{1,0:T(8,128)(2,1)S(1)}, bf16[512,640]{1,0:T(8,128)(2,1)S(1)}) fusion(f32[640]{0:T(1024)S(1)} %reduce.12, f32[512]{0:T(512)S(1)} %bitcast.86, f32[640]{0:T(1024)S(1)} %reduce.13, f32[512]{0:T(512)S(1)} %bitcast.85, f32[640]{0:T(1024)S(1)} %reduce.14, f32[512]{0:T(512)S(1)} %bitcast.84), kind=kLoop, calls=%fused_computation.5.clone.1 | loop fusion | flops 2293760 | bytes 1324544 | tf_op jit(solution)/shard_map/while/body/eval_jaxpr/convert_element_type | solution.py:20
  280.5 0.9 convolution_bitcast_fusion.2
  281.4 0.2 fusion.49
  281.7 0.7 fusion.50
  282.4 0.6 dynamic_slice.33
  283.6 0.1 constant_dynamic-slice_fusion.6
  283.8 5.4 %cosine_convert_fusion.4 = (bf16[512,640]{1,0:T(8,128)(2,1)S(1)}, bf16[512,640]{1,0:T(8,128)(2,1)S(1)}) fusion(f32[640]{0:T(1024)S(1)} %reduce.12, f32[512]{0:T(512)S(1)} %bitcast.86, f32[640]{0:T(1024)S(1)} %reduce.13, f32[512]{0:T(512)S(1)} %bitcast.85, f32[640]{0:T(1024)S(1)} %reduce.14, f32[512]{0:T(512)S(1)} %bitcast.84), kind=kLoop, calls=%fused_computation.5.clone.1 | loop fusion | flops 2293760 | bytes 1324544 | tf_op jit(solution)/shard_map/while/body/eval_jaxpr/convert_element_type | solution.py:20
  289.2 0.9 convolution_bitcast_fusion.2
  290.2 0.2 fusion.49
  290.4 0.7 fusion.50
  291.2 1.4 copy.23
  292.7 2.0 copy.20
  294.7 0.2 pad.32
  294.9 1.4 copy.27
  296.3 84.7 %reduce-scatter.7.cloned.1.call-done = f32[128,3]{1,0:T(8,128)} async-done(((f32[2048,3]{1,0:T(8,128)}), f32[128,3]{1,0:T(8,128)}) %reduce-scatter.7.cloned.1.call-update) | async-done | bytes 1552
  381.0 1.5 copy.24
  382.5 87.0 %reduce-scatter.5.cloned.1.call-done = f32[140,128]{1,0:T(8,128)} async-done(((f32[140,2048]{1,0:T(8,128)}), f32[140,128]{1,0:T(8,128)}) %reduce-scatter.5.cloned.1.call-update) | async-done | bytes 71696 | tf_op jit(solution)/shard_map/reduce_scatter | solution.py:143
  469.5 0.9 reshape.67
  470.4 0.7 copy.22
  (59 shorter events, 0.9 us)
Async XLA Ops:
  7.2 232.5 %all-reduce.2.cloned.1.call-start = ((), (), s32[]{:S(2)}) async-start(), calls=%async_computation.2 | async-start | bytes 737280 | tf_op jit(solution)/shard_map/psum | solution.py:128
  97.2 25.7 %copy-start = (f32[2,2,70,640]{3,1,2,0:T(2,128)S(1)}, f32[2,2,70,640]{3,1,2,0:T(2,128)}, u32[]{:S(2)}) copy-start(f32[2,2,70,640]{3,1,2,0:T(2,128)} %param.15) | copy-start | bytes 2150404
  121.8 0.7 copy-start.1
  122.6 258.4 %reduce-scatter.7.cloned.1.call-start = ((), (), s32[]{:S(2)}) async-start(), calls=%async_computation.4 | async-start | bytes 1114112
  123.4 117.6 %copy-start.2 = (f32[640]{0:T(1024)S(1)}, f32[640]{0:T(1024)}, u32[]{:S(2)}) copy-start(f32[640]{0:T(1024)} %param.14) | copy-start | bytes 7684
  292.6 176.9 %reduce-scatter.5.cloned.1.call-start = ((), (), s32[]{:S(2)}) async-start(), calls=%async_computation.3 | async-start | bytes 1253376 | tf_op jit(solution)/shard_map/reduce_scatter | solution.py:143
Sparse Core Ops, SparseCore 0:
  122.7 116.9 all-reduce.1
  292.7 88.2 reduce-scatter.6
  384.6 84.9 reduce-scatter.4
where the time goes:
time: 479 us; the launch traced here: 478 us
  waiting for transfers between devices  288 us (60%)
  blocking collectives  87.7 us (18%)
  other arithmetic  64.2 us (13%)
  local copies, waits for them, and re-layouts  15 us (3%)
  between operations  13.9 us (3%)
  matrix products  5.45 us (1%)
    psum x1, waiting for transfers between devices, body(): fields = lax.psum(partial_fields, 'dom')  116 us
    reduce_scatter x1, waiting for transfers between devices, body(): lax.psum_scatter(coef_part, 'dir', scatter_dimension=1, tiled=True)  87 us
    unnamed x4, waiting for transfers between devices  84.8 us
    all_gather x1, blocking collectives, body(): domain_rows = lax.all_gather(own_rows, 'dir', axis=1, tiled=True)  49.2 us
    convert_element_type x8, other arithmetic, phase_tile(): jnp.cos(angles).astype(jnp.bfloat16)  43.5 us
    all_gather x1, blocking collectives, body(): domain_places = lax.all_gather(positions, 'dir', axis=1, tiled=True)  38.4 us
    concatenate x1, other arithmetic, adjoint_terms(): left_side = jnp.concatenate([top_rows, low_rows], axis=0)  14.7 us
  transfers between devices with their start and end apart: 3, of which 3 were waited for; matrix products, arithmetic and copies ran while one was open for 1% of the time, Pallas kernels for 0%

commit v1 on v0

--- a/solution.py
+++ b/solution.py
@@ -1,3 +1,5 @@
+import functools
+
 import jax
 import jax.numpy as jnp
 from jax import lax
@@ -105,45 +107,48 @@
     return (coef_term, jnp.stack(place_terms))
 
 
-def body(coefficients, positions, polar, azimuth, weights, farmap):
+def xor_pairs(size, mask):
+    return [(index, index ^ mask) for index in range(size)]
+
+
+def step_masks(size, nearest_last):
+    masks = [1 << bit for bit in range(size.bit_length() - 1)]
+    assert 1 << len(masks) == size
+    if nearest_last and size == 16:
+        masks = [2, 8, 1, 4]
+    return masks
+
+
+def body(coefficients, positions, polar, azimuth, weights, farmap, dir_size, dom_size):
     own_count = coefficients.shape[2]
-    own_rows = coefficients.reshape(2 * C, own_count)
-    domain_rows = lax.all_gather(own_rows, "dir", axis=1, tiled=True)
-    domain_places = lax.all_gather(positions, "dir", axis=1, tiled=True)
+    dir_masks = step_masks(dir_size, True)
+    dom_masks = step_masks(dom_size, False)
+    own_rows = jnp.concatenate(
+        [coefficients.reshape(2 * C, own_count).astype(jnp.float32), positions], axis=0
+    )
+    gathered = own_rows
+    for mask in dir_masks:
+        gathered = jnp.concatenate(
+            [gathered, lax.ppermute(gathered, "dir", xor_pairs(dir_size, mask))], axis=1
+        )
+    domain_rows = gathered[: 2 * C].astype(jnp.bfloat16)
+    domain_places = gathered[2 * C :]
     vectors = unit_vectors(polar, azimuth)
-    width_all = domain_rows.shape[1]
-    width_block = 512
-    blocks = width_all // width_block
-
-    def forward_block(block_id, totals):
-        offset = block_id * width_block
-        coef_block = lax.dynamic_slice_in_dim(domain_rows, offset, width_block, 1)
-        place_block = lax.dynamic_slice_in_dim(domain_places, offset, width_block, 1)
-        cos_tile, sin_tile = phase_tile(place_block, vectors)
-        return totals + field_terms(coef_block, cos_tile, sin_tile)
-
-    partial_fields = lax.fori_loop(
-        0, blocks, forward_block, jnp.zeros((2 * C, polar.shape[0]), jnp.float32)
-    )
-    fields = lax.psum(partial_fields, "dom")
+    cos_tile, sin_tile = phase_tile(domain_places, vectors)
+    fields = field_terms(domain_rows, cos_tile, sin_tile)
+    for mask in dom_masks:
+        fields = fields + lax.ppermute(fields, "dom", xor_pairs(dom_size, mask))
     adjoint = cotangent_rows(fields, farmap, weights)
     stacked = stacked_rows(adjoint, vectors)
-
-    def backward_block(block_id):
-        offset = block_id * width_block
-        coef_block = lax.dynamic_slice_in_dim(domain_rows, offset, width_block, 1)
-        place_block = lax.dynamic_slice_in_dim(domain_places, offset, width_block, 1)
-        cos_tile, sin_tile = phase_tile(place_block, vectors)
-        return gradients(adjoint_terms(stacked, cos_tile, sin_tile), coef_block)
-
-    coef_parts, place_parts = lax.map(backward_block, jnp.arange(blocks, dtype=jnp.int32))
-    coef_part = jnp.moveaxis(coef_parts, 0, 1).reshape(2 * C, width_all)
-    place_part = jnp.moveaxis(place_parts, 0, 1).reshape(3, width_all)
-    coef_grad, place_grad = (
-        lax.psum_scatter(coef_part, "dir", scatter_dimension=1, tiled=True),
-        lax.psum_scatter(place_part, "dir", scatter_dimension=1, tiled=True),
-    )
-    return (coef_grad.reshape(2, C, own_count), place_grad)
+    coef_part, place_part = gradients(adjoint_terms(stacked, cos_tile, sin_tile), domain_rows)
+    part = jnp.concatenate([coef_part, place_part], axis=0)
+    for step in reversed(range(len(dir_masks))):
+        half = own_count << step
+        received = lax.ppermute(
+            part[:, half : 2 * half], "dir", xor_pairs(dir_size, dir_masks[step])
+        )
+        part = part[:, :half] + received
+    return (part[: 2 * C].reshape(2, C, own_count), part[2 * C :])
 
 
 def solution(mesh):
@@ -156,7 +161,7 @@
         P(None, None, None, "dir"),
     )
     return jax.shard_map(
-        body,
+        functools.partial(body, dir_size=mesh.shape["dir"], dom_size=mesh.shape["dom"]),
         mesh=mesh,
         in_specs=placed,
         out_specs=(P(None, None, ("dom", "dir")), P(None, ("dom", "dir"))),

time: 479 us -> 154 us (0.32)
  waiting for transfers between devices: 288 us -> 82.5 us
  blocking collectives: 87.7 us -> 0 us
  other arithmetic: 64.2 us -> 26 us
  starting transfers between devices: 0.3 us -> 33.3 us
  between operations: 13.9 us -> 0.89 us
  local copies, waits for them, and re-layouts: 15 us -> 4.26 us
    psum x1 -> x0, waiting for transfers between devices: 116 us -> none  [body(): fields = lax.psum(partial_fields, 'dom')]
    all_gather x2 -> x0, blocking collectives: 87.7 us -> none  [the longest x1 49.2 us: body(): domain_rows = lax.all_gather(own_rows, 'dir', axis=1, tiled=True)]
    reduce_scatter x1 -> x0, waiting for transfers between devices: 87 us -> none  [body(): lax.psum_scatter(coef_part, 'dir', scatter_dimension=1, tiled=True)]
    unnamed x4 -> x0, waiting for transfers between devices: 84.8 us -> none
    ppermute x0 -> x12, waiting for transfers between devices: none -> 82.5 us  [the longest x4 28.4 us: body(): lax.ppermute(gathered, 'dir', xor_pairs(dir_size, mask))]
    ppermute x0 -> x12, starting transfers between devices: none -> 33.3 us  [the longest x4 12.9 us: body(): lax.ppermute(gathered, 'dir', xor_pairs(dir_size, mask))]
    convert_element_type x8 -> x1, other arithmetic: 43.5 us -> 20.8 us  [phase_tile(): jnp.cos(angles).astype(jnp.bfloat16)]
    concatenate x1 -> x3, other arithmetic: 14.7 us -> 2.12 us  [body(): jnp.concatenate([gathered, lax.ppermute(gathered, 'dir', xor_pairs(dir_si...]
  transfers between devices with their start and end apart: 3 -> 12, of which waited for: 3 -> 12; matrix products, arithmetic and copies ran while one was open for 1% -> 1% of each run, Pallas kernels for 0% -> 0%
where the time goes in v1:
time: 154 us; the launch traced here: 151 us
  waiting for transfers between devices  82.5 us (54%)
  starting transfers between devices  33.3 us (22%)
  other arithmetic  26 us (17%)
  matrix products  4.27 us (3%)
  local copies, waits for them, and re-layouts  4.26 us (3%)
    ppermute x4, waiting for transfers between devices, body(): lax.ppermute(gathered, 'dir', xor_pairs(dir_size, mask))  28.4 us
    ppermute x4, waiting for transfers between devices, body(): lax.ppermute(part[:, half:2 * half], 'dir', xor_pairs(dir_size, dir_masks...  28.1 us
    ppermute x4, waiting for transfers between devices, body(): fields = fields + lax.ppermute(fields, 'dom', xor_pairs(dom_size, mask))  26 us
    convert_element_type x1, other arithmetic, phase_tile(): jnp.cos(angles).astype(jnp.bfloat16)  20.8 us
    ppermute x4, starting transfers between devices, body(): lax.ppermute(gathered, 'dir', xor_pairs(dir_size, mask))  12.9 us
    ppermute x4, starting transfers between devices, body(): lax.ppermute(part[:, half:2 * half], 'dir', xor_pairs(dir_size, dir_masks...  11.6 us
    ppermute x4, starting transfers between devices, body(): fields = fields + lax.ppermute(fields, 'dom', xor_pairs(dom_size, mask))  8.78 us
    dot_general x1, matrix products, adjoint_terms(): lax.dot_general(left_side, right_side, (((1,), (1,)), ((), ())), preferre...  3.17 us
  transfers between devices with their start and end apart: 12, of which 12 were waited for; matrix products, arithmetic and copies ran while one was open for 1% of the time, Pallas kernels for 0%

profile of v1, /device:TPU:32, one launch (start us, length us, event | category | flops | bytes accessed | tf_op | source)
XLA Modules:
  0.0 151.3 jit_solution(15041413710017215848)
XLA Ops:
  0.6 0.8 copy.12
  1.4 0.7 constant_dynamic-update-slice_fusion.4
  2.1 6.4 %collective-permute-start = (f32[143,128]{1,0:T(8,128)S(1)}, f32[143,128]{1,0:T(8,128)S(1)}, u32[]{:S(2)}, u32[]{:S(2)}) collective-permute-start(f32[143,128]{1,0:T(8,128)S(1)} %get-tuple-element.14), channel_id=1, source_target_pairs={{0,2},{1,3},{2,0},{3,1},{4,6},{5,7},{6,4},{7,5},{8,10},{9,11},{10,... | collective-permute-start | bytes 219656 | tf_op jit(solution)/shard_map/ppermute | solution.py:132
  8.5 3.5 %collective-permute-done = f32[143,128]{1,0:T(8,128)S(1)} collective-permute-done((f32[143,128]{1,0:T(8,128)S(1)}, f32[143,128]{1,0:T(8,128)S(1)}, u32[]{:S(2)}, u32[]{:S(2)}) %collective-permute-start) | collective-permute-done | bytes 73248 | tf_op jit(solution)/shard_map/ppermute | solution.py:132
  12.0 0.7 pad_maximum_fusion.3
  12.6 3.1 %collective-permute-start.1 = (f32[143,256]{1,0:T(8,128)S(1)}, f32[143,256]{1,0:T(8,128)S(1)}, u32[]{:S(2)}, u32[]{:S(2)}) collective-permute-start(f32[143,256]{1,0:T(8,128)S(1)} %pad_maximum_fusion.3), channel_id=1, source_target_pairs={{0,8},{1,9},{2,10},{3,11},{4,12},{5,13},{6,14},{7,15},{8,0},{9,1},... | collective-permute-start | bytes 439304 | tf_op jit(solution)/shard_map/ppermute | solution.py:132
  15.8 3.6 %collective-permute-done.1 = f32[143,256]{1,0:T(8,128)S(1)} collective-permute-done((f32[143,256]{1,0:T(8,128)S(1)}, f32[143,256]{1,0:T(8,128)S(1)}, u32[]{:S(2)}, u32[]{:S(2)}) %collective-permute-start.1) | collective-permute-done | bytes 146464 | tf_op jit(solution)/shard_map/ppermute | solution.py:132
  19.4 0.7 pad_maximum_fusion.1
  20.1 1.9 %collective-permute-start.2 = (f32[143,512]{1,0:T(8,128)S(1)}, f32[143,512]{1,0:T(8,128)S(1)}, u32[]{:S(2)}, u32[]{:S(2)}) collective-permute-start(f32[143,512]{1,0:T(8,128)S(1)} %pad_maximum_fusion.1), channel_id=1, source_target_pairs={{0,1},{1,0},{2,3},{3,2},{4,5},{5,4},{6,7},{7,6},{8,9},{9,8},{10,11... | collective-permute-start | bytes 878600 | tf_op jit(solution)/shard_map/ppermute | solution.py:132
  22.0 10.3 %collective-permute-done.2 = f32[143,512]{1,0:T(8,128)S(1)} collective-permute-done((f32[143,512]{1,0:T(8,128)S(1)}, f32[143,512]{1,0:T(8,128)S(1)}, u32[]{:S(2)}, u32[]{:S(2)}) %collective-permute-start.2) | collective-permute-done | bytes 292896 | tf_op jit(solution)/shard_map/ppermute | solution.py:132
  32.2 0.7 pad_maximum_fusion
  33.0 1.6 %collective-permute-start.3 = (f32[143,1024]{1,0:T(8,128)S(1)}, f32[143,1024]{1,0:T(8,128)S(1)}, u32[]{:S(2)}, u32[]{:S(2)}) collective-permute-start(f32[143,1024]{1,0:T(8,128)S(1)} %pad_maximum_fusion), channel_id=1, source_target_pairs={{0,4},{1,5},{2,6},{3,7},{4,0},{5,1},{6,2},{7,3},{8,12},{9,13},{10,... | collective-permute-start | bytes 1757192 | tf_op jit(solution)/shard_map/ppermute | solution.py:132
  34.5 0.7 fusion.58
  35.3 0.7 cosine_multiply_fusion
  36.1 11.0 %collective-permute-done.3 = f32[143,1024]{1,0:T(8,128)S(1)} collective-permute-done((f32[143,1024]{1,0:T(8,128)S(1)}, f32[143,1024]{1,0:T(8,128)S(1)}, u32[]{:S(2)}, u32[]{:S(2)}) %collective-permute-start.3) | collective-permute-done | bytes 585760 | tf_op jit(solution)/shard_map/ppermute | solution.py:132
  47.1 0.1 convert.6
  47.2 0.1 fusion.53
  47.3 20.8 %cosine_convert_fusion = (bf16[2048,640]{1,0:T(8,128)(2,1)S(1)}, bf16[2048,640]{1,0:T(8,128)(2,1)S(1)}) fusion(f32[640]{0:T(1024)S(1)} %get-tuple-element.43, f32[2048]{0:T(1024)S(1)} %bitcast.32, f32[640]{0:T(1024)S(1)} %get-tuple-element.39, f32[2048]{0:T(1024)S(1)} %bitcast.33, f32[640]{0:T(1024)S(1)} %get-tuple-element.38, f32[2048]{0:T(1024)S(1)} %bitcast.31), kind=kLoop, calls=%fused_computation.9 | loop fusion | flops 9175040 | bytes 5275136 | tf_op jit(solution)/shard_map/convert_element_type | solution.py:22
  68.1 1.1 fusion
  69.2 0.0 copy-start
  69.2 0.1 collective-permute-start.4
  69.3 1.7 %collective-permute-done.4 = f32[140,640]{1,0:T(8,128)S(1)} collective-permute-done((f32[140,640]{1,0:T(8,128)S(1)}, f32[140,640]{1,0:T(8,128)S(1)}, u32[]{:S(2)}, u32[]{:S(2)}) %collective-permute-start.4) | collective-permute-done | bytes 358432 | tf_op jit(solution)/shard_map/ppermute | solution.py:140
  71.0 0.1 add.47
  71.0 3.6 %collective-permute-start.5 = (f32[140,640]{1,0:T(8,128)S(1)}, f32[140,640]{1,0:T(8,128)S(1)}, u32[]{:S(2)}, u32[]{:S(2)}) collective-permute-start(f32[140,640]{1,0:T(8,128)S(1)} %add.47), channel_id=1, source_target_pairs={{0,32},{16,48},{32,0},{48,16},{64,96},{80,112},{96,64},{112,80},{1... | collective-permute-start | bytes 1075208 | tf_op jit(solution)/shard_map/ppermute | solution.py:140
  74.6 8.9 %collective-permute-done.5 = f32[140,640]{1,0:T(8,128)S(1)} collective-permute-done((f32[140,640]{1,0:T(8,128)S(1)}, f32[140,640]{1,0:T(8,128)S(1)}, u32[]{:S(2)}, u32[]{:S(2)}) %collective-permute-start.5) | collective-permute-done | bytes 358432 | tf_op jit(solution)/shard_map/ppermute | solution.py:140
  83.5 1.7 %collective-permute-start.6 = (f32[140,640]{1,0:T(8,128)S(1)}, f32[140,640]{1,0:T(8,128)S(1)}, u32[]{:S(2)}, u32[]{:S(2)}) collective-permute-start(f32[140,640]{1,0:T(8,128)S(1)} %add.48), channel_id=1, source_target_pairs={{0,64},{16,80},{32,96},{48,112},{64,0},{80,16},{96,32},{112,48},{1... | collective-permute-start | bytes 1075208 | tf_op jit(solution)/shard_map/ppermute | solution.py:140
  85.2 8.5 %collective-permute-done.6 = f32[140,640]{1,0:T(8,128)S(1)} collective-permute-done((f32[140,640]{1,0:T(8,128)S(1)}, f32[140,640]{1,0:T(8,128)S(1)}, u32[]{:S(2)}, u32[]{:S(2)}) %collective-permute-start.6) | collective-permute-done | bytes 358432 | tf_op jit(solution)/shard_map/ppermute | solution.py:140
  93.7 0.1 add.49
  93.7 0.0 copy-start.1
  93.7 3.5 %collective-permute-start.7 = (f32[140,640]{1,0:T(8,128)S(1)}, f32[140,640]{1,0:T(8,128)S(1)}, u32[]{:S(2)}, u32[]{:S(2)}) collective-permute-start(f32[140,640]{1,0:T(8,128)S(1)} %add.49), channel_id=1, source_target_pairs={{0,128},{16,144},{32,160},{48,176},{64,192},{80,208},{96,224},{112... | collective-permute-start | bytes 1075208 | tf_op jit(solution)/shard_map/ppermute | solution.py:140
  97.2 0.0 copy-done
  97.2 0.6 fusion.52
  97.8 7.0 %collective-permute-done.7 = f32[140,640]{1,0:T(8,128)S(1)} collective-permute-done((f32[140,640]{1,0:T(8,128)S(1)}, f32[140,640]{1,0:T(8,128)S(1)}, u32[]{:S(2)}, u32[]{:S(2)}) %collective-permute-start.7) | collective-permute-done | bytes 358432 | tf_op jit(solution)/shard_map/ppermute | solution.py:140
  104.8 0.1 subtract_reduce_fusion.1
  104.9 0.1 add_reduce_fusion
  105.0 0.0 copy-done.1
  105.1 0.1 fusion.46
  105.2 0.1 fusion.55
  105.3 0.1 maximum_negate_fusion
  105.4 3.2 %fusion.4 = f32[560,2048]{1,0:T(8,128)S(1)} fusion(bf16[2048,640]{1,0:T(8,128)(2,1)S(1)} %get-tuple-element.37, bf16[2048,640]{1,0:T(8,128)(2,1)S(1)} %get-tuple-element.36, bf16[280,640]{1,0:T(8,128)(2,1)S(1)} %maximum_negate_fusion, bf16[70,640]{1,0:T(8,128)(2,1)S(1)} %get-tuple-element.31, bf16[70,640]{1,0:T(8,128)(2,1)S(1)} %get-tuple-element.45, ...), kind=kOutput, calls=%fused_computation.4 | convolution fusion | flops 2965135360 | bytes 10905600 | tf_op jit(solution)/shard_map/dot_general | solution.py:44
  108.6 0.7 fusion.45
  109.3 0.6 concatenate.72
  110.0 1.6 %collective-permute-start.8 = (f32[143,1024]{1,0:T(8,128)S(1)}, f32[143,1024]{1,0:T(8,128)S(1)}, u32[]{:S(2)}, u32[]{:S(2)}) collective-permute-start(f32[143,1024]{1,0:T(8,128)S(1)} %slice.188), channel_id=1, source_target_pairs={{0,4},{1,5},{2,6},{3,7},{4,0},{5,1},{6,2},{7,3},{8,12},{9,13},{10,... | collective-permute-start | bytes 1757192 | tf_op jit(solution)/shard_map/ppermute | solution.py:147
  111.6 11.6 %collective-permute-done.8 = f32[143,1024]{1,0:T(8,128)S(1)} collective-permute-done((f32[143,1024]{1,0:T(8,128)S(1)}, f32[143,1024]{1,0:T(8,128)S(1)}, u32[]{:S(2)}, u32[]{:S(2)}) %collective-permute-start.8) | collective-permute-done | bytes 585760 | tf_op jit(solution)/shard_map/ppermute | solution.py:147
  123.2 0.1 slice_add_fusion
  123.3 0.9 collective-permute-start.9
  124.2 9.5 %collective-permute-done.9 = f32[143,512]{1,0:T(8,128)S(1)} collective-permute-done((f32[143,512]{1,0:T(8,128)S(1)}, f32[143,512]{1,0:T(8,128)S(1)}, u32[]{:S(2)}, u32[]{:S(2)}) %collective-permute-start.9) | collective-permute-done | bytes 292896 | tf_op jit(solution)/shard_map/ppermute | solution.py:147
  133.6 0.1 slice_add_fusion.1
  133.7 2.9 %collective-permute-start.10 = (f32[143,256]{1,0:T(8,128)S(1)}, f32[143,256]{1,0:T(8,128)S(1)}, u32[]{:S(2)}, u32[]{:S(2)}) collective-permute-start(f32[143,256]{1,0:T(8,128)S(1)} %slice.192), channel_id=1, source_target_pairs={{0,8},{1,9},{2,10},{3,11},{4,12},{5,13},{6,14},{7,15},{8,0},{9,1},... | collective-permute-start | bytes 439304 | tf_op jit(solution)/shard_map/ppermute | solution.py:147
  136.6 3.9 %collective-permute-done.10 = f32[143,256]{1,0:T(8,128)S(1)} collective-permute-done((f32[143,256]{1,0:T(8,128)S(1)}, f32[143,256]{1,0:T(8,128)S(1)}, u32[]{:S(2)}, u32[]{:S(2)}) %collective-permute-start.10) | collective-permute-done | bytes 146464 | tf_op jit(solution)/shard_map/ppermute | solution.py:147
  140.5 6.3 %collective-permute-start.11 = (f32[143,128]{1,0:T(8,128)S(1)}, f32[143,128]{1,0:T(8,128)S(1)}, u32[]{:S(2)}, u32[]{:S(2)}) collective-permute-start(f32[143,128]{1,0:T(8,128)S(1)} %slice.194), channel_id=1, source_target_pairs={{0,2},{1,3},{2,0},{3,1},{4,6},{5,7},{6,4},{7,5},{8,10},{9,11},{10,... | collective-permute-start | bytes 219656 | tf_op jit(solution)/shard_map/ppermute | solution.py:147
  146.8 3.2 %collective-permute-done.11 = f32[143,128]{1,0:T(8,128)S(1)} collective-permute-done((f32[143,128]{1,0:T(8,128)S(1)}, f32[143,128]{1,0:T(8,128)S(1)}, u32[]{:S(2)}, u32[]{:S(2)}) %collective-permute-start.11) | collective-permute-done | bytes 73248 | tf_op jit(solution)/shard_map/ppermute | solution.py:147
  150.0 0.6 slice.196
  150.6 0.7 copy.14
  (21 shorter events, 0.4 us)
Async XLA Ops:
  2.1 9.8 %collective-permute-start = (f32[143,128]{1,0:T(8,128)S(1)}, f32[143,128]{1,0:T(8,128)S(1)}, u32[]{:S(2)}, u32[]{:S(2)}) collective-permute-start(f32[143,128]{1,0:T(8,128)S(1)} %get-tuple-element.14), channel_id=1, source_target_pairs={{0,2},{1,3},{2,0},{3,1},{4,6},{5,7},{6,4},{7,5},{8,10},{9,11},{10,... | collective-permute-start | bytes 219656 | tf_op jit(solution)/shard_map/ppermute | solution.py:132
  12.6 6.7 %collective-permute-start.1 = (f32[143,256]{1,0:T(8,128)S(1)}, f32[143,256]{1,0:T(8,128)S(1)}, u32[]{:S(2)}, u32[]{:S(2)}) collective-permute-start(f32[143,256]{1,0:T(8,128)S(1)} %pad_maximum_fusion.3), channel_id=1, source_target_pairs={{0,8},{1,9},{2,10},{3,11},{4,12},{5,13},{6,14},{7,15},{8,0},{9,1},... | collective-permute-start | bytes 439304 | tf_op jit(solution)/shard_map/ppermute | solution.py:132
  20.1 12.2 %collective-permute-start.2 = (f32[143,512]{1,0:T(8,128)S(1)}, f32[143,512]{1,0:T(8,128)S(1)}, u32[]{:S(2)}, u32[]{:S(2)}) collective-permute-start(f32[143,512]{1,0:T(8,128)S(1)} %pad_maximum_fusion.1), channel_id=1, source_target_pairs={{0,1},{1,0},{2,3},{3,2},{4,5},{5,4},{6,7},{7,6},{8,9},{9,8},{10,11... | collective-permute-start | bytes 878600 | tf_op jit(solution)/shard_map/ppermute | solution.py:132
  33.0 14.1 %collective-permute-start.3 = (f32[143,1024]{1,0:T(8,128)S(1)}, f32[143,1024]{1,0:T(8,128)S(1)}, u32[]{:S(2)}, u32[]{:S(2)}) collective-permute-start(f32[143,1024]{1,0:T(8,128)S(1)} %pad_maximum_fusion), channel_id=1, source_target_pairs={{0,4},{1,5},{2,6},{3,7},{4,0},{5,1},{6,2},{7,3},{8,12},{9,13},{10,... | collective-permute-start | bytes 1757192 | tf_op jit(solution)/shard_map/ppermute | solution.py:132
  69.2 28.0 %copy-start = (f32[2,2,70,640]{3,1,2,0:T(2,128)S(1)}, f32[2,2,70,640]{3,1,2,0:T(2,128)}, u32[]{:S(2)}) copy-start(f32[2,2,70,640]{3,1,2,0:T(2,128)} %param.11) | copy-start | bytes 2150404
  69.2 1.8 %collective-permute-start.4 = (f32[140,640]{1,0:T(8,128)S(1)}, f32[140,640]{1,0:T(8,128)S(1)}, u32[]{:S(2)}, u32[]{:S(2)}) collective-permute-start(f32[140,640]{1,0:T(8,128)S(1)} %fusion), channel_id=1, source_target_pairs={{0,16},{16,0},{32,48},{48,32},{64,80},{80,64},{96,112},{112,96},{1... | collective-permute-start | bytes 1075208 | tf_op jit(solution)/shard_map/ppermute | solution.py:140
  71.0 12.4 %collective-permute-start.5 = (f32[140,640]{1,0:T(8,128)S(1)}, f32[140,640]{1,0:T(8,128)S(1)}, u32[]{:S(2)}, u32[]{:S(2)}) collective-permute-start(f32[140,640]{1,0:T(8,128)S(1)} %add.47), channel_id=1, source_target_pairs={{0,32},{16,48},{32,0},{48,16},{64,96},{80,112},{96,64},{112,80},{1... | collective-permute-start | bytes 1075208 | tf_op jit(solution)/shard_map/ppermute | solution.py:140
  83.5 10.1 %collective-permute-start.6 = (f32[140,640]{1,0:T(8,128)S(1)}, f32[140,640]{1,0:T(8,128)S(1)}, u32[]{:S(2)}, u32[]{:S(2)}) collective-permute-start(f32[140,640]{1,0:T(8,128)S(1)} %add.48), channel_id=1, source_target_pairs={{0,64},{16,80},{32,96},{48,112},{64,0},{80,16},{96,32},{112,48},{1... | collective-permute-start | bytes 1075208 | tf_op jit(solution)/shard_map/ppermute | solution.py:140
  93.7 11.3 %copy-start.1 = (f32[640]{0:T(1024)S(1)}, f32[640]{0:T(1024)}, u32[]{:S(2)}) copy-start(f32[640]{0:T(1024)} %param.10) | copy-start | bytes 7684
  93.7 11.0 %collective-permute-start.7 = (f32[140,640]{1,0:T(8,128)S(1)}, f32[140,640]{1,0:T(8,128)S(1)}, u32[]{:S(2)}, u32[]{:S(2)}) collective-permute-start(f32[140,640]{1,0:T(8,128)S(1)} %add.49), channel_id=1, source_target_pairs={{0,128},{16,144},{32,160},{48,176},{64,192},{80,208},{96,224},{112... | collective-permute-start | bytes 1075208 | tf_op jit(solution)/shard_map/ppermute | solution.py:140
  110.0 13.2 %collective-permute-start.8 = (f32[143,1024]{1,0:T(8,128)S(1)}, f32[143,1024]{1,0:T(8,128)S(1)}, u32[]{:S(2)}, u32[]{:S(2)}) collective-permute-start(f32[143,1024]{1,0:T(8,128)S(1)} %slice.188), channel_id=1, source_target_pairs={{0,4},{1,5},{2,6},{3,7},{4,0},{5,1},{6,2},{7,3},{8,12},{9,13},{10,... | collective-permute-start | bytes 1757192 | tf_op jit(solution)/shard_map/ppermute | solution.py:147
  123.3 10.4 %collective-permute-start.9 = (f32[143,512]{1,0:T(8,128)S(1)}, f32[143,512]{1,0:T(8,128)S(1)}, u32[]{:S(2)}, u32[]{:S(2)}) collective-permute-start(f32[143,512]{1,0:T(8,128)S(1)} %slice.190), channel_id=1, source_target_pairs={{0,1},{1,0},{2,3},{3,2},{4,5},{5,4},{6,7},{7,6},{8,9},{9,8},{10,11... | collective-permute-start | bytes 878600 | tf_op jit(solution)/shard_map/ppermute | solution.py:147
  133.7 6.7 %collective-permute-start.10 = (f32[143,256]{1,0:T(8,128)S(1)}, f32[143,256]{1,0:T(8,128)S(1)}, u32[]{:S(2)}, u32[]{:S(2)}) collective-permute-start(f32[143,256]{1,0:T(8,128)S(1)} %slice.192), channel_id=1, source_target_pairs={{0,8},{1,9},{2,10},{3,11},{4,12},{5,13},{6,14},{7,15},{8,0},{9,1},... | collective-permute-start | bytes 439304 | tf_op jit(solution)/shard_map/ppermute | solution.py:147
  140.5 9.5 %collective-permute-start.11 = (f32[143,128]{1,0:T(8,128)S(1)}, f32[143,128]{1,0:T(8,128)S(1)}, u32[]{:S(2)}, u32[]{:S(2)}) collective-permute-start(f32[143,128]{1,0:T(8,128)S(1)} %slice.194), channel_id=1, source_target_pairs={{0,2},{1,3},{2,0},{3,1},{4,6},{5,7},{6,4},{7,5},{8,10},{9,11},{10,... | collective-permute-start | bytes 219656 | tf_op jit(solution)/shard_map/ppermute | solution.py:147

commit v2 on v1

--- a/solution.py
+++ b/solution.py
@@ -107,48 +107,42 @@
     return (coef_term, jnp.stack(place_terms))
 
 
-def xor_pairs(size, mask):
-    return [(index, index ^ mask) for index in range(size)]
+def gather_blocks(block, axis_name, size):
+    spread = jnp.broadcast_to(block[None], (size,) + block.shape)
+    return lax.all_to_all(spread, axis_name, 0, 0, tiled=True)
 
 
-def step_masks(size, nearest_last):
-    masks = [1 << bit for bit in range(size.bit_length() - 1)]
-    assert 1 << len(masks) == size
-    if nearest_last and size == 16:
-        masks = [2, 8, 1, 4]
-    return masks
+def scatter_sum(part, axis_name, size):
+    rows, width = part.shape
+    split = part.reshape(rows, size, width // size)
+    received = lax.all_to_all(split, axis_name, 1, 1, tiled=True)
+    return jnp.sum(received, axis=1)
 
 
 def body(coefficients, positions, polar, azimuth, weights, farmap, dir_size, dom_size):
     own_count = coefficients.shape[2]
-    dir_masks = step_masks(dir_size, True)
-    dom_masks = step_masks(dom_size, False)
-    own_rows = jnp.concatenate(
-        [coefficients.reshape(2 * C, own_count).astype(jnp.float32), positions], axis=0
-    )
-    gathered = own_rows
-    for mask in dir_masks:
-        gathered = jnp.concatenate(
-            [gathered, lax.ppermute(gathered, "dir", xor_pairs(dir_size, mask))], axis=1
-        )
-    domain_rows = gathered[: 2 * C].astype(jnp.bfloat16)
-    domain_places = gathered[2 * C :]
+    own_rows = coefficients.reshape(2 * C, own_count)
+    coef_blocks = gather_blocks(own_rows, "dir", dir_size)
+    place_blocks = gather_blocks(positions, "dir", dir_size)
+    domain_rows = jnp.moveaxis(coef_blocks, 0, 1).reshape(2 * C, dir_size * own_count)
+    domain_places = jnp.moveaxis(place_blocks, 0, 1).reshape(3, dir_size * own_count)
     vectors = unit_vectors(polar, azimuth)
     cos_tile, sin_tile = phase_tile(domain_places, vectors)
-    fields = field_terms(domain_rows, cos_tile, sin_tile)
-    for mask in dom_masks:
-        fields = fields + lax.ppermute(fields, "dom", xor_pairs(dom_size, mask))
-    adjoint = cotangent_rows(fields, farmap, weights)
+    partial_fields = field_terms(domain_rows, cos_tile, sin_tile)
+    dir_count = polar.shape[0]
+    slice_width = dir_count // dom_size
+    fields_slice = scatter_sum(partial_fields, "dom", dom_size)
+    offset = lax.axis_index("dom") * slice_width
+    farmap_slice = lax.dynamic_slice_in_dim(farmap, offset, slice_width, 3)
+    weights_slice = lax.dynamic_slice_in_dim(weights, offset, slice_width, 0)
+    adjoint_slice = cotangent_rows(fields_slice, farmap_slice, weights_slice)
+    adjoint_blocks = gather_blocks(adjoint_slice, "dom", dom_size)
+    adjoint = jnp.moveaxis(adjoint_blocks, 0, 1).reshape(2 * C, dir_count)
     stacked = stacked_rows(adjoint, vectors)
     coef_part, place_part = gradients(adjoint_terms(stacked, cos_tile, sin_tile), domain_rows)
     part = jnp.concatenate([coef_part, place_part], axis=0)
-    for step in reversed(range(len(dir_masks))):
-        half = own_count << step
-        received = lax.ppermute(
-            part[:, half : 2 * half], "dir", xor_pairs(dir_size, dir_masks[step])
-        )
-        part = part[:, :half] + received
-    return (part[: 2 * C].reshape(2, C, own_count), part[2 * C :])
+    reduced = scatter_sum(part, "dir", dir_size)
+    return (reduced[: 2 * C].reshape(2, C, own_count), reduced[2 * C :])
 
 
 def solution(mesh):

time: 154 us -> 138 us (0.90); the launches traced: 151 us -> 137 us
  waiting for transfers between devices: 82.5 us -> 18.1 us
  blocking collectives: 0 us -> 53.6 us
  starting transfers between devices: 33.3 us -> 19.7 us
  local copies, waits for them, and re-layouts: 4.26 us -> 11.1 us
  matrix products: 4.27 us -> 7.82 us
    ppermute x12 -> x0, waiting for transfers between devices: 82.5 us -> none  [the longest x4 28.4 us: body(): lax.ppermute(gathered, 'dir', xor_pairs(dir_size, mask))]
    all_to_all x0 -> x2, blocking collectives: none -> 53.6 us  [the longest x1 42.2 us: scatter_sum(): received = lax.all_to_all(split, axis_name, 1, 1, tiled=True)]
    ppermute x12 -> x0, starting transfers between devices: 33.3 us -> none  [the longest x4 12.9 us: body(): lax.ppermute(gathered, 'dir', xor_pairs(dir_size, mask))]
    all_to_all x0 -> x3, starting transfers between devices: none -> 19.7 us  [the longest x2 13.7 us: gather_blocks(): return lax.all_to_all(spread, axis_name, 0, 0, tiled=True)]
    all_to_all x0 -> x3, waiting for transfers between devices: none -> 18.1 us  [the longest x2 9.23 us: gather_blocks(): return lax.all_to_all(spread, axis_name, 0, 0, tiled=True)]
    unnamed x8 -> x14, local copies, waits for them, and re-layouts: 0.72 us -> 3.29 us
    broadcast_in_dim x0 -> x4, local copies, waits for them, and re-layouts: none -> 2.25 us  [gather_blocks(): spread = jnp.broadcast_to(block[None], (size,) + block.shape)]
    concatenate x3 -> x1, other arithmetic: 2.12 us -> 0.08 us  [cotangent_from(): return jnp.concatenate([cot_real, cot_imag], axis=0).astype(jnp.bfloat16)]
  transfers between devices with their start and end apart: 12 -> 3, of which waited for: 12 -> 2; matrix products, arithmetic and copies ran while one was open for 1% -> 20% of each run, Pallas kernels for 0% -> 0%
where the time goes in v2:
time: 138 us; the launch traced here: 137 us
  blocking collectives  53.6 us (39%)
  other arithmetic  26.3 us (19%)
  starting transfers between devices  19.7 us (14%)
  waiting for transfers between devices  18.1 us (13%)
  local copies, waits for them, and re-layouts  11.1 us (8%)
  matrix products  7.82 us (6%)
    all_to_all x1, blocking collectives, scatter_sum(): received = lax.all_to_all(split, axis_name, 1, 1, tiled=True)  42.2 us
    convert_element_type x1, other arithmetic, phase_tile(): jnp.cos(angles).astype(jnp.bfloat16)  22.5 us
    all_to_all x2, starting transfers between devices, gather_blocks(): return lax.all_to_all(spread, axis_name, 0, 0, tiled=True)  13.7 us
    all_to_all x1, blocking collectives, gather_blocks(): return lax.all_to_all(spread, axis_name, 0, 0, tiled=True)  11.4 us
    all_to_all x2, waiting for transfers between devices, gather_blocks(): return lax.all_to_all(spread, axis_name, 0, 0, tiled=True)  9.23 us
    all_to_all x1, waiting for transfers between devices, scatter_sum(): received = lax.all_to_all(split, axis_name, 1, 1, tiled=True)  8.85 us
    all_to_all x1, starting transfers between devices, scatter_sum(): received = lax.all_to_all(split, axis_name, 1, 1, tiled=True)  5.95 us
    dot_general x1, matrix products, adjoint_terms(): lax.dot_general(left_side, right_side, (((1,), (1,)), ((), ())), preferre...  4.77 us
  transfers between devices with their start and end apart: 3, of which 2 were waited for; matrix products, arithmetic and copies ran while one was open for 20% of the time, Pallas kernels for 0%

profile of v2, /device:TPU:32, one launch (start us, length us, event | category | flops | bytes accessed | tf_op | source)
XLA Modules:
  0.0 137.4 jit_solution(18096370921419156442)
XLA Ops:
  0.6 1.3 broadcast_in_dim.10
  1.9 10.1 %all-to-all-start.1 = ((f32[16,3,128]{2,1,0:T(4,128)}), f32[16,3,128]{2,1,0:T(4,128)S(1)}, u32[]{:S(2)}, u32[]{:S(2)}) async-start(f32[16,3,128]{2,1,0:T(4,128)} %broadcast_in_dim.10), calls=%async_computation.1 | async-start | bytes 65536 | tf_op jit(solution)/shard_map/all_to_all | solution.py:112
  12.1 0.8 copy.14
  12.9 9.2 %all-to-all-done.1 = f32[16,3,128]{2,1,0:T(4,128)S(1)} async-done(((f32[16,3,128]{2,1,0:T(4,128)}), f32[16,3,128]{2,1,0:T(4,128)S(1)}, u32[]{:S(2)}, u32[]{:S(2)}) %all-to-all-start.1) | async-done | bytes 24608 | tf_op jit(solution)/shard_map/all_to_all | solution.py:112
  22.1 0.9 broadcast_in_dim.9
  23.0 3.6 %all-to-all-start = ((bf16[16,140,128]{2,1,0:T(8,128)(2,1)}), bf16[16,140,128]{2,1,0:T(8,128)(2,1)S(1)}, u32[]{:S(2)}, u32[]{:S(2)}) async-start(bf16[16,140,128]{2,1,0:T(8,128)(2,1)} %broadcast_in_dim.9), calls=%async_computation | async-start | bytes 1179648 | tf_op jit(solution)/shard_map/all_to_all | solution.py:112
  26.6 0.7 fusion.66
  27.3 0.7 cosine_multiply_fusion
  28.1 22.5 %cosine_convert_fusion = (bf16[2048,640]{1,0:T(8,128)(2,1)S(1)}, bf16[2048,640]{1,0:T(8,128)(2,1)}) fusion(f32[640]{0:T(1024)S(1)} %get-tuple-element.40, f32[2048]{0:T(1024)S(1)} %bitcast.88, f32[640]{0:T(1024)S(1)} %get-tuple-element.38, f32[2048]{0:T(1024)S(1)} %bitcast.89, f32[640]{0:T(1024)S(1)} %get-tuple-element.37, f32[2048]{0:T(1024)S(1)} %bitcast.87), kind=kLoop, calls=%fused_computation.9 | loop fusion | flops 9175040 | bytes 5275136 | tf_op jit(solution)/shard_map/convert_element_type | solution.py:22
  50.6 0.0 all-to-all-done
  50.6 0.0 copy-start
  50.6 0.1 fusion.59
  50.8 0.1 copy.26
  50.9 0.1 copy.25
  51.0 0.1 neg.6
  51.1 1.3 copy-done
  52.3 3.1 %fusion = f32[140,640]{0,1:T(8,128)} fusion(bf16[2048,640]{1,0:T(8,128)(2,1)S(1)} %copy-done, bf16[2048,640]{1,0:T(8,128)(2,1)S(1)} %get-tuple-element.32, bf16[70,2048]{1,0:T(8,128)(2,1)S(1)} %neg.6, bf16[70,2048]{1,0:T(8,128)(2,1)S(1)} %bitcast.74, bf16[70,2048]{1,0:T(8,128)(2,1)S(1)} %bitcast.67), kind=kOutput, calls=%fused_computation | convolution fusion | flops 749076480 | bytes 6461440 | tf_op jit(solution)/shard_map/dot_general | solution.py:33
  55.4 5.9 %all-to-all-start.2 = ((f32[140,16,40]{0,2,1:T(8,128)}), f32[140,16,40]{0,2,1:T(8,128)}, u32[]{:S(2)}, u32[]{:S(2)}) async-start(f32[140,16,40]{0,2,1:T(8,128)} %bitcast.80), calls=%async_computation.2 | async-start | bytes 1310720 | tf_op jit(solution)/shard_map/all_to_all | solution.py:118
  61.3 0.8 dynamic_slice.6
  62.1 1.4 %constant_dynamic-slice_fusion = (f32[2,1,70,40]{3,1,2,0:T(1,128)S(1)}, f32[2,1,70,40]{3,1,2,0:T(1,128)S(1)}) fusion(f32[2,2,70,640]{3,1,2,0:T(2,128)} %param.11, s32[]{:T(128)S(6)} %select_n.4, s32[]{:T(128)S(6)} %add.33), kind=kLoop, calls=%fused_computation.88 | loop fusion | bytes 89608 | tf_op jit(solution)/shard_map/slice | solution.py:53
  63.5 0.1 copy.23
  63.6 0.1 copy.24
  63.7 8.9 %all-to-all-done.2 = f32[140,16,40]{0,2,1:T(8,128)} async-done(((f32[140,16,40]{0,2,1:T(8,128)}), f32[140,16,40]{0,2,1:T(8,128)}, u32[]{:S(2)}, u32[]{:S(2)}) %all-to-all-start.2) | async-done | bytes 358432 | tf_op jit(solution)/shard_map/all_to_all | solution.py:118
  72.5 1.1 reduce_sum.81
  73.7 0.0 copy-start.1
  73.7 0.1 fusion.64
  73.8 0.1 fusion.50
  73.9 0.1 fusion.54
  74.0 0.1 multiply_convert_fusion.1
  74.1 0.1 pad_maximum_fusion
  74.2 11.4 %all_to_all.25 = bf16[16,140,40]{1,2,0:T(8,128)(2,1)S(1)} all-to-all(bf16[16,140,40]{1,2,0:T(8,128)(2,1)S(1)} %broadcast_in_dim.11), channel_id=1, replica_groups=mesh['dom'=16,'dir'=16] {'dom'}, dimensions={0} | all-to-all | bytes 358400 | tf_op jit(solution)/shard_map/all_to_all | solution.py:112
  85.6 0.1 fusion.60
  85.7 0.3 fusion.40
  86.0 0.1 fusion.63
  86.1 0.2 fusion.61
  86.3 0.4 maximum_negate_fusion
  86.7 0.0 copy-done.1
  86.7 4.8 %fusion.4 = f32[560,2048]{1,0:T(8,128)S(1)} fusion(bf16[2048,640]{1,0:T(8,128)(2,1)S(1)} %copy-done.1, bf16[2048,640]{1,0:T(8,128)(2,1)S(1)} %get-tuple-element.32, bf16[280,640]{0,1:T(8,128)(2,1)S(1)} %maximum_negate_fusion, bf16[70,640]{0,1:T(8,128)(2,1)S(1)} %get-tuple-element.25, bf16[70,640]{0,1:T(8,128)(2,1)S(1)} %get-tuple-element.44, ...), kind=kOutput, calls=%fused_computation.4 | convolution fusion | flops 2965135360 | bytes 10905600 | tf_op jit(solution)/shard_map/dot_general | solution.py:44
  91.5 0.7 fusion.48
  92.2 0.1 copy.28
  92.4 0.2 copy.19
  92.6 0.1 copy.27
  92.8 0.2 copy.18
  93.0 1.0 concatenate.60
  93.9 42.2 %all_to_all.26 = f32[143,16,128]{2,0,1:T(8,128)S(1)} all-to-all(f32[143,16,128]{2,0,1:T(8,128)S(1)} %concatenate.60), channel_id=1, replica_groups=mesh['dom'=16,'dir'=16] {'dir'}, dimensions={1} | all-to-all | bytes 2342912 | tf_op jit(solution)/shard_map/all_to_all | solution.py:118
  136.1 0.1 reduce_sum.89
  136.2 0.6 slice.169
  136.8 0.7 copy.20
  (13 shorter events, 0.3 us)
Async XLA Ops:
  1.9 20.2 %all-to-all-start.1 = ((f32[16,3,128]{2,1,0:T(4,128)}), f32[16,3,128]{2,1,0:T(4,128)S(1)}, u32[]{:S(2)}, u32[]{:S(2)}) async-start(f32[16,3,128]{2,1,0:T(4,128)} %broadcast_in_dim.10), calls=%async_computation.1 | async-start | bytes 65536 | tf_op jit(solution)/shard_map/all_to_all | solution.py:112
  23.0 27.6 %all-to-all-start = ((bf16[16,140,128]{2,1,0:T(8,128)(2,1)}), bf16[16,140,128]{2,1,0:T(8,128)(2,1)S(1)}, u32[]{:S(2)}, u32[]{:S(2)}) async-start(bf16[16,140,128]{2,1,0:T(8,128)(2,1)} %broadcast_in_dim.9), calls=%async_computation | async-start | bytes 1179648 | tf_op jit(solution)/shard_map/all_to_all | solution.py:112
  50.6 1.7 %copy-start = (bf16[2048,640]{1,0:T(8,128)(2,1)S(1)}, bf16[2048,640]{1,0:T(8,128)(2,1)}, u32[]{:S(2)}) copy-start(bf16[2048,640]{1,0:T(8,128)(2,1)} %get-tuple-element.33) | copy-start | bytes 7864324
  55.4 17.2 %all-to-all-start.2 = ((f32[140,16,40]{0,2,1:T(8,128)}), f32[140,16,40]{0,2,1:T(8,128)}, u32[]{:S(2)}, u32[]{:S(2)}) async-start(f32[140,16,40]{0,2,1:T(8,128)} %bitcast.80), calls=%async_computation.2 | async-start | bytes 1310720 | tf_op jit(solution)/shard_map/all_to_all | solution.py:118
  73.7 13.0 %copy-start.1 = (bf16[2048,640]{1,0:T(8,128)(2,1)S(1)}, bf16[2048,640]{1,0:T(8,128)(2,1)}, u32[]{:S(2)}) copy-start(bf16[2048,640]{1,0:T(8,128)(2,1)} %get-tuple-element.33) | copy-start | bytes 7864324

commit v3 on v2

--- a/solution.py
+++ b/solution.py
@@ -107,6 +107,10 @@
     return (coef_term, jnp.stack(place_terms))
 
 
+DOM_AXES = ("y", "z_lo", "core")
+DIR_AXES = ("x", "z_hi")
+
+
 def gather_blocks(block, axis_name, size):
     spread = jnp.broadcast_to(block[None], (size,) + block.shape)
     return lax.all_to_all(spread, axis_name, 0, 0, tiled=True)
@@ -119,45 +123,69 @@
     return jnp.sum(received, axis=1)
 
 
-def body(coefficients, positions, polar, azimuth, weights, farmap, dir_size, dom_size):
+def gather_dir(block, sizes):
+    inner = gather_blocks(block, DIR_AXES[1], sizes[1])
+    outer = gather_blocks(inner, DIR_AXES[0], sizes[0])
+    rows, width = block.shape
+    return jnp.moveaxis(outer.reshape(sizes[0] * sizes[1], rows, width), 0, 1).reshape(
+        rows, sizes[0] * sizes[1] * width
+    )
+
+
+def scatter_dir(part, sizes):
+    rows, width = part.shape
+    split = part.reshape(rows, sizes[0], sizes[1] * width // (sizes[0] * sizes[1]))
+    outer = jnp.sum(lax.all_to_all(split, DIR_AXES[0], 1, 1, tiled=True), axis=1)
+    return scatter_sum(outer, DIR_AXES[1], sizes[1])
+
+
+def body(coefficients, positions, polar, azimuth, weights, farmap, dir_sizes, dom_size):
     own_count = coefficients.shape[2]
     own_rows = coefficients.reshape(2 * C, own_count)
-    coef_blocks = gather_blocks(own_rows, "dir", dir_size)
-    place_blocks = gather_blocks(positions, "dir", dir_size)
-    domain_rows = jnp.moveaxis(coef_blocks, 0, 1).reshape(2 * C, dir_size * own_count)
-    domain_places = jnp.moveaxis(place_blocks, 0, 1).reshape(3, dir_size * own_count)
+    domain_rows = gather_dir(own_rows, dir_sizes)
+    domain_places = gather_dir(positions, dir_sizes)
     vectors = unit_vectors(polar, azimuth)
     cos_tile, sin_tile = phase_tile(domain_places, vectors)
     partial_fields = field_terms(domain_rows, cos_tile, sin_tile)
     dir_count = polar.shape[0]
     slice_width = dir_count // dom_size
-    fields_slice = scatter_sum(partial_fields, "dom", dom_size)
-    offset = lax.axis_index("dom") * slice_width
+    fields_slice = scatter_sum(partial_fields, DOM_AXES, dom_size)
+    offset = lax.axis_index(DOM_AXES) * slice_width
     farmap_slice = lax.dynamic_slice_in_dim(farmap, offset, slice_width, 3)
     weights_slice = lax.dynamic_slice_in_dim(weights, offset, slice_width, 0)
     adjoint_slice = cotangent_rows(fields_slice, farmap_slice, weights_slice)
-    adjoint_blocks = gather_blocks(adjoint_slice, "dom", dom_size)
+    adjoint_blocks = gather_blocks(adjoint_slice, DOM_AXES, dom_size)
     adjoint = jnp.moveaxis(adjoint_blocks, 0, 1).reshape(2 * C, dir_count)
     stacked = stacked_rows(adjoint, vectors)
     coef_part, place_part = gradients(adjoint_terms(stacked, cos_tile, sin_tile), domain_rows)
     part = jnp.concatenate([coef_part, place_part], axis=0)
-    reduced = scatter_sum(part, "dir", dir_size)
+    reduced = scatter_dir(part, dir_sizes)
     return (reduced[: 2 * C].reshape(2, C, own_count), reduced[2 * C :])
 
 
 def solution(mesh):
+    dom_size = mesh.shape["dom"]
+    dir_size = mesh.shape["dir"]
+    chips_z = 2 if dom_size % 4 == 0 else 1
+    dom_sizes = (dom_size // (2 * chips_z), chips_z, 2)
+    x_size = 4 if dir_size % 4 == 0 else dir_size
+    dir_sizes = (x_size, dir_size // x_size)
+    fine = jax.sharding.Mesh(
+        mesh.devices.reshape(dom_sizes + dir_sizes), DOM_AXES + DIR_AXES
+    )
+    every = DOM_AXES + DIR_AXES
     placed = (
-        P(None, None, ("dom", "dir")),
-        P(None, ("dom", "dir")),
-        P("dir"),
-        P("dir"),
-        P("dir"),
-        P(None, None, None, "dir"),
+        P(None, None, every),
+        P(None, every),
+        P(DIR_AXES),
+        P(DIR_AXES),
+        P(DIR_AXES),
+        P(None, None, None, DIR_AXES),
     )
     return jax.shard_map(
-        functools.partial(body, dir_size=mesh.shape["dir"], dom_size=mesh.shape["dom"]),
-        mesh=mesh,
+        functools.partial(body, dir_sizes=dir_sizes, dom_size=dom_size),
+        mesh=fine,
         in_specs=placed,
-        out_specs=(P(None, None, ("dom", "dir")), P(None, ("dom", "dir"))),
+        out_specs=(P(None, None, every), P(None, every)),
         check_vma=False,
     )

time: 138 us -> 148 us (1.072)
  waiting for transfers between devices: 18.1 us -> 28.1 us
  blocking collectives: 53.6 us -> 45.8 us
  starting transfers between devices: 19.7 us -> 24.6 us
  local copies, waits for them, and re-layouts: 11.1 us -> 12.8 us
    all_to_all x1, blocking collectives: 42.2 us -> 13.2 us  [scatter_sum(): received = lax.all_to_all(split, axis_name, 1, 1, tiled=True)]
    all_to_all x0 -> x1, blocking collectives: none -> 21.2 us  [scatter_dir(): lax.all_to_all(split, DIR_AXES[0], 1, 1, tiled=True)]
    all_to_all x2 -> x4, waiting for transfers between devices: 9.23 us -> 19.3 us  [gather_blocks(): return lax.all_to_all(spread, axis_name, 0, 0, tiled=True)]
    all_to_all x2 -> x4, starting transfers between devices: 13.7 us -> 18.7 us  [gather_blocks(): return lax.all_to_all(spread, axis_name, 0, 0, tiled=True)]
    broadcast_in_dim x4 -> x6, local copies, waits for them, and re-layouts: 2.25 us -> 3.57 us  [gather_blocks(): spread = jnp.broadcast_to(block[None], (size,) + block.shape)]
    unnamed x14 -> x12, local copies, waits for them, and re-layouts: 3.29 us -> 2.99 us
  transfers between devices with their start and end apart: 3 -> 5, of which waited for: 2 -> 4; matrix products, arithmetic and copies ran while one was open for 20% -> 19% of each run, Pallas kernels for 0% -> 0%
where the time goes in v3:
time: 148 us; the launch traced here: 147 us
  blocking collectives  45.8 us (31%)
  waiting for transfers between devices  28.1 us (19%)
  other arithmetic  26.4 us (18%)
  starting transfers between devices  24.6 us (17%)
  local copies, waits for them, and re-layouts  12.8 us (9%)
  matrix products  7.95 us (5%)
    convert_element_type x1, other arithmetic, phase_tile(): jnp.cos(angles).astype(jnp.bfloat16)  22.6 us
    all_to_all x1, blocking collectives, scatter_dir(): lax.all_to_all(split, DIR_AXES[0], 1, 1, tiled=True)  21.2 us
    all_to_all x4, waiting for transfers between devices, gather_blocks(): return lax.all_to_all(spread, axis_name, 0, 0, tiled=True)  19.3 us
    all_to_all x4, starting transfers between devices, gather_blocks(): return lax.all_to_all(spread, axis_name, 0, 0, tiled=True)  18.7 us
    all_to_all x1, blocking collectives, scatter_sum(): received = lax.all_to_all(split, axis_name, 1, 1, tiled=True)  13.2 us
    all_to_all x1, blocking collectives, gather_blocks(): return lax.all_to_all(spread, axis_name, 0, 0, tiled=True)  11.4 us
    all_to_all x1, waiting for transfers between devices, scatter_sum(): received = lax.all_to_all(split, axis_name, 1, 1, tiled=True)  8.83 us
    all_to_all x1, starting transfers between devices, scatter_sum(): received = lax.all_to_all(split, axis_name, 1, 1, tiled=True)  5.94 us
  transfers between devices with their start and end apart: 5, of which 4 were waited for; matrix products, arithmetic and copies ran while one was open for 19% of the time, Pallas kernels for 0%

profile of v3, /device:TPU:32, one launch (start us, length us, event | category | flops | bytes accessed | tf_op | source)
XLA Modules:
  0.0 146.6 jit_solution(6410262738144650423)
XLA Ops:
  0.6 1.3 broadcast_in_dim.15
  1.9 7.6 %all-to-all-start.2 = ((f32[4,3,128]{2,1,0:T(4,128)}), f32[4,3,128]{2,1,0:T(4,128)S(1)}, u32[]{:S(2)}, u32[]{:S(2)}) async-start(f32[4,3,128]{2,1,0:T(4,128)} %broadcast_in_dim.15), calls=%async_computation.2 | async-start | bytes 16384 | tf_op jit(solution)/shard_map/all_to_all | solution.py:116
  9.5 0.7 fusion.65
  10.2 7.0 %all-to-all-done.2 = f32[4,3,128]{2,1,0:T(4,128)S(1)} async-done(((f32[4,3,128]{2,1,0:T(4,128)}), f32[4,3,128]{2,1,0:T(4,128)S(1)}, u32[]{:S(2)}, u32[]{:S(2)}) %all-to-all-start.2) | async-done | bytes 6176 | tf_op jit(solution)/shard_map/all_to_all | solution.py:116
  17.2 0.6 broadcast_in_dim.16
  17.8 4.3 %all-to-all-start.3 = ((f32[4,4,3,128]{3,1,2,0:T(4,128)}), f32[4,4,3,128]{3,1,2,0:T(4,128)S(1)}, u32[]{:S(2)}, u32[]{:S(2)}) async-start(f32[4,4,3,128]{3,1,2,0:T(4,128)} %broadcast_in_dim.16), calls=%async_computation.3 | async-start | bytes 49152 | tf_op jit(solution)/shard_map/all_to_all | solution.py:116
  22.1 0.7 cosine_multiply_fusion
  22.8 0.8 copy.33
  23.6 3.9 %all-to-all-done.3 = f32[4,4,3,128]{3,1,2,0:T(4,128)S(1)} async-done(((f32[4,4,3,128]{3,1,2,0:T(4,128)}), f32[4,4,3,128]{3,1,2,0:T(4,128)S(1)}, u32[]{:S(2)}, u32[]{:S(2)}) %all-to-all-start.3) | async-done | bytes 24608 | tf_op jit(solution)/shard_map/all_to_all | solution.py:116
  27.5 0.7 broadcast_in_dim.13
  28.2 3.3 %all-to-all-start = ((bf16[4,140,128]{2,1,0:T(8,128)(2,1)}), bf16[4,140,128]{2,1,0:T(8,128)(2,1)S(1)}, u32[]{:S(2)}, u32[]{:S(2)}) async-start(bf16[4,140,128]{2,1,0:T(8,128)(2,1)} %broadcast_in_dim.13), calls=%async_computation | async-start | bytes 294912 | tf_op jit(solution)/shard_map/all_to_all | solution.py:116
  31.6 8.4 %all-to-all-done = bf16[4,140,128]{2,1,0:T(8,128)(2,1)S(1)} async-done(((bf16[4,140,128]{2,1,0:T(8,128)(2,1)}), bf16[4,140,128]{2,1,0:T(8,128)(2,1)S(1)}, u32[]{:S(2)}, u32[]{:S(2)}) %all-to-all-start) | async-done | bytes 143392 | tf_op jit(solution)/shard_map/all_to_all | solution.py:116
  40.0 0.1 copy.34
  40.0 1.0 broadcast_in_dim.14
  41.0 3.5 %all-to-all-start.1 = ((bf16[4,4,140,128]{3,1,2,0:T(4,128)(2,1)}), bf16[4,4,140,128]{3,1,2,0:T(4,128)(2,1)S(1)}, u32[]{:S(2)}, u32[]{:S(2)}) async-start(bf16[4,4,140,128]{3,1,2,0:T(4,128)(2,1)} %broadcast_in_dim.14), calls=%async_computation.1 | async-start | bytes 1146880 | tf_op jit(solution)/shard_map/all_to_all | solution.py:116
  44.5 22.6 %cosine_convert_fusion = (bf16[2048,640]{1,0:T(8,128)(2,1)S(1)}, bf16[2048,640]{1,0:T(8,128)(2,1)}) fusion(f32[640]{0:T(1024)S(1)} %get-tuple-element.44, f32[2048]{0:T(1024)S(1)} %get-tuple-element.39, f32[640]{0:T(1024)S(1)} %get-tuple-element.42, f32[2048]{0:T(1024)S(1)} %get-tuple-element.40, f32[640]{0:T(1024)S(1)} %get-tuple-element.41, ...), kind=kLoop, calls=%fused_computation.9 | loop fusion | flops 9175040 | bytes 5275136 | tf_op jit(solution)/shard_map/convert_element_type | solution.py:22
  67.1 0.0 all-to-all-done.1
  67.1 0.0 copy-start
  67.1 0.1 copy.35
  67.1 0.1 fusion.59
  67.3 0.1 copy.50
  67.5 0.1 copy.49
  67.6 0.1 neg.6
  67.6 1.2 copy-done
  68.8 3.1 %fusion = f32[140,640]{0,1:T(8,128)} fusion(bf16[2048,640]{1,0:T(8,128)(2,1)S(1)} %copy-done, bf16[2048,640]{1,0:T(8,128)(2,1)S(1)} %get-tuple-element.36, bf16[70,2048]{1,0:T(8,128)(2,1)S(1)} %neg.6, bf16[70,2048]{1,0:T(8,128)(2,1)S(1)} %bitcast.71, bf16[70,2048]{1,0:T(8,128)(2,1)S(1)} %bitcast.68), kind=kOutput, calls=%fused_computation | convolution fusion | flops 749076480 | bytes 6461440 | tf_op jit(solution)/shard_map/dot_general | solution.py:33
  71.9 5.9 %all-to-all-start.4 = ((f32[140,16,40]{0,2,1:T(8,128)}), f32[140,16,40]{0,2,1:T(8,128)}, u32[]{:S(2)}, u32[]{:S(2)}) async-start(f32[140,16,40]{0,2,1:T(8,128)} %bitcast.77), calls=%async_computation.4 | async-start | bytes 1310720 | tf_op jit(solution)/shard_map/all_to_all | solution.py:122
  77.8 0.8 dynamic_slice.6
  78.6 1.5 constant_dynamic-slice_fusion
  80.0 0.1 copy.47
  80.1 0.1 copy.48
  80.2 8.8 %all-to-all-done.4 = f32[140,16,40]{0,2,1:T(8,128)} async-done(((f32[140,16,40]{0,2,1:T(8,128)}), f32[140,16,40]{0,2,1:T(8,128)}, u32[]{:S(2)}, u32[]{:S(2)}) %all-to-all-start.4) | async-done | bytes 358432 | tf_op jit(solution)/shard_map/all_to_all | solution.py:122
  89.0 1.1 reduce_sum.90
  90.2 0.0 copy-start.1
  90.2 0.1 fusion.64
  90.3 0.1 fusion.50
  90.4 0.1 fusion.54
  90.5 0.1 multiply_convert_fusion.1
  90.5 0.1 pad_maximum_fusion
  90.7 11.4 %all_to_all.40 = bf16[16,140,40]{1,2,0:T(8,128)(2,1)S(1)} all-to-all(bf16[16,140,40]{1,2,0:T(8,128)(2,1)S(1)} %broadcast_in_dim.17), channel_id=1, replica_groups=mesh['y'=4,'z_lo'=2,'core'=2,'x'=4,'z_hi'=4] {'y','z_lo','core'}, dimensions={0} | all-to-all | bytes 358400 | tf_op jit(solution)/shard_map/all_to_all | solution.py:116
  102.0 0.1 fusion.60
  102.2 0.3 fusion.40
  102.5 0.1 fusion.63
  102.6 0.2 fusion.61
  102.8 0.4 maximum_negate_fusion
  103.2 0.0 copy-done.1
  103.2 4.9 %fusion.4 = f32[560,2048]{1,0:T(8,128)S(1)} fusion(bf16[2048,640]{1,0:T(8,128)(2,1)S(1)} %copy-done.1, bf16[2048,640]{1,0:T(8,128)(2,1)S(1)} %get-tuple-element.36, bf16[280,640]{0,1:T(8,128)(2,1)S(1)} %maximum_negate_fusion, bf16[70,640]{0,1:T(8,128)(2,1)S(1)} %get-tuple-element.29, bf16[70,640]{0,1:T(8,128)(2,1)S(1)} %get-tuple-element.48, ...), kind=kOutput, calls=%fused_computation.4 | convolution fusion | flops 2965135360 | bytes 10905600 | tf_op jit(solution)/shard_map/dot_general | solution.py:44
  108.1 0.7 fusion.48
  108.8 0.4 concatenate.59
  109.2 0.2 copy.42
  109.4 0.4 concatenate.58
  109.8 0.2 copy.41
  110.0 0.6 concatenate.60
  110.6 21.2 %all_to_all.41 = f32[143,4,512]{2,0,1:T(8,128)S(1)} all-to-all(f32[143,4,512]{2,0,1:T(8,128)S(1)} %concatenate.60), channel_id=1, replica_groups=mesh['y'=4,'z_lo'=2,'core'=2,'x'=4,'z_hi'=4] {'x'}, dimensions={1} | all-to-all | bytes 2342912 | tf_op jit(solution)/shard_map/all_to_all | solution.py:138
  131.8 0.1 reduce_sum.98
  131.9 0.1 reshape.126
  132.1 13.2 %all_to_all.42 = f32[143,4,128]{2,0,1:T(8,128)S(1)} all-to-all(f32[143,4,128]{2,0,1:T(8,128)S(1)} %copy.43), channel_id=1, replica_groups=mesh['y'=4,'z_lo'=2,'core'=2,'x'=4,'z_hi'=4] {'z_hi'}, dimensions={1} | all-to-all | bytes 585728 | tf_op jit(solution)/shard_map/all_to_all | solution.py:122
  145.3 0.6 slice.169
  145.9 0.7 copy.44
  (15 shorter events, 0.2 us)
Async XLA Ops:
  1.9 15.3 %all-to-all-start.2 = ((f32[4,3,128]{2,1,0:T(4,128)}), f32[4,3,128]{2,1,0:T(4,128)S(1)}, u32[]{:S(2)}, u32[]{:S(2)}) async-start(f32[4,3,128]{2,1,0:T(4,128)} %broadcast_in_dim.15), calls=%async_computation.2 | async-start | bytes 16384 | tf_op jit(solution)/shard_map/all_to_all | solution.py:116
  17.8 9.7 %all-to-all-start.3 = ((f32[4,4,3,128]{3,1,2,0:T(4,128)}), f32[4,4,3,128]{3,1,2,0:T(4,128)S(1)}, u32[]{:S(2)}, u32[]{:S(2)}) async-start(f32[4,4,3,128]{3,1,2,0:T(4,128)} %broadcast_in_dim.16), calls=%async_computation.3 | async-start | bytes 49152 | tf_op jit(solution)/shard_map/all_to_all | solution.py:116
  28.2 11.8 %all-to-all-start = ((bf16[4,140,128]{2,1,0:T(8,128)(2,1)}), bf16[4,140,128]{2,1,0:T(8,128)(2,1)S(1)}, u32[]{:S(2)}, u32[]{:S(2)}) async-start(bf16[4,140,128]{2,1,0:T(8,128)(2,1)} %broadcast_in_dim.13), calls=%async_computation | async-start | bytes 294912 | tf_op jit(solution)/shard_map/all_to_all | solution.py:116
  41.0 26.1 %all-to-all-start.1 = ((bf16[4,4,140,128]{3,1,2,0:T(4,128)(2,1)}), bf16[4,4,140,128]{3,1,2,0:T(4,128)(2,1)S(1)}, u32[]{:S(2)}, u32[]{:S(2)}) async-start(bf16[4,4,140,128]{3,1,2,0:T(4,128)(2,1)} %broadcast_in_dim.14), calls=%async_computation.1 | async-start | bytes 1146880 | tf_op jit(solution)/shard_map/all_to_all | solution.py:116
  67.1 1.7 %copy-start = (bf16[2048,640]{1,0:T(8,128)(2,1)S(1)}, bf16[2048,640]{1,0:T(8,128)(2,1)}, u32[]{:S(2)}) copy-start(bf16[2048,640]{1,0:T(8,128)(2,1)} %get-tuple-element.37) | copy-start | bytes 7864324
  71.9 17.2 %all-to-all-start.4 = ((f32[140,16,40]{0,2,1:T(8,128)}), f32[140,16,40]{0,2,1:T(8,128)}, u32[]{:S(2)}, u32[]{:S(2)}) async-start(f32[140,16,40]{0,2,1:T(8,128)} %bitcast.77), calls=%async_computation.4 | async-start | bytes 1310720 | tf_op jit(solution)/shard_map/all_to_all | solution.py:122
  90.2 13.0 %copy-start.1 = (bf16[2048,640]{1,0:T(8,128)(2,1)S(1)}, bf16[2048,640]{1,0:T(8,128)(2,1)}, u32[]{:S(2)}) copy-start(bf16[2048,640]{1,0:T(8,128)(2,1)} %get-tuple-element.37) | copy-start | bytes 7864324

commit v4 on v2

--- a/solution.py
+++ b/solution.py
@@ -122,26 +122,28 @@
 def body(coefficients, positions, polar, azimuth, weights, farmap, dir_size, dom_size):
     own_count = coefficients.shape[2]
     own_rows = coefficients.reshape(2 * C, own_count)
-    coef_blocks = gather_blocks(own_rows, "dir", dir_size)
-    place_blocks = gather_blocks(positions, "dir", dir_size)
-    domain_rows = jnp.moveaxis(coef_blocks, 0, 1).reshape(2 * C, dir_size * own_count)
-    domain_places = jnp.moveaxis(place_blocks, 0, 1).reshape(3, dir_size * own_count)
-    vectors = unit_vectors(polar, azimuth)
+    coef_blocks = gather_blocks(own_rows, "dom", dom_size)
+    place_blocks = gather_blocks(positions, "dom", dom_size)
+    domain_rows = jnp.moveaxis(coef_blocks, 0, 1).reshape(2 * C, dom_size * own_count)
+    domain_places = jnp.moveaxis(place_blocks, 0, 1).reshape(3, dom_size * own_count)
+    slice_width = polar.shape[0] // dom_size
+    offset = lax.axis_index("dom") * slice_width
+    own_angles = lax.dynamic_slice_in_dim(jnp.stack([polar, azimuth]), offset, slice_width, 1)
+    angle_blocks = gather_blocks(own_angles, "dir", dir_size)
+    set_angles = jnp.moveaxis(angle_blocks, 0, 1).reshape(2, dir_size * slice_width)
+    vectors = unit_vectors(set_angles[0], set_angles[1])
     cos_tile, sin_tile = phase_tile(domain_places, vectors)
     partial_fields = field_terms(domain_rows, cos_tile, sin_tile)
-    dir_count = polar.shape[0]
-    slice_width = dir_count // dom_size
-    fields_slice = scatter_sum(partial_fields, "dom", dom_size)
-    offset = lax.axis_index("dom") * slice_width
+    fields_slice = scatter_sum(partial_fields, "dir", dir_size)
     farmap_slice = lax.dynamic_slice_in_dim(farmap, offset, slice_width, 3)
     weights_slice = lax.dynamic_slice_in_dim(weights, offset, slice_width, 0)
     adjoint_slice = cotangent_rows(fields_slice, farmap_slice, weights_slice)
-    adjoint_blocks = gather_blocks(adjoint_slice, "dom", dom_size)
-    adjoint = jnp.moveaxis(adjoint_blocks, 0, 1).reshape(2 * C, dir_count)
+    adjoint_blocks = gather_blocks(adjoint_slice, "dir", dir_size)
+    adjoint = jnp.moveaxis(adjoint_blocks, 0, 1).reshape(2 * C, dir_size * slice_width)
     stacked = stacked_rows(adjoint, vectors)
     coef_part, place_part = gradients(adjoint_terms(stacked, cos_tile, sin_tile), domain_rows)
     part = jnp.concatenate([coef_part, place_part], axis=0)
-    reduced = scatter_sum(part, "dir", dir_size)
+    reduced = scatter_sum(part, "dom", dom_size)
     return (reduced[: 2 * C].reshape(2, C, own_count), reduced[2 * C :])
 
 

time: 138 us -> 148 us (1.072); the launches traced: 137 us -> 146 us
  blocking collectives: 53.6 us -> 60.4 us
  waiting for transfers between devices: 18.1 us -> 23.5 us
  starting transfers between devices: 19.7 us -> 15 us
    all_to_all x1 -> x2, blocking collectives: 11.4 us -> 38 us  [gather_blocks(): return lax.all_to_all(spread, axis_name, 0, 0, tiled=True)]
    all_to_all x1, blocking collectives: 42.2 us -> 22.4 us  [scatter_sum(): received = lax.all_to_all(split, axis_name, 1, 1, tiled=True)]
    all_to_all x1, waiting for transfers between devices: 8.85 us -> 19.5 us  [scatter_sum(): received = lax.all_to_all(split, axis_name, 1, 1, tiled=True)]
    all_to_all x2, waiting for transfers between devices: 9.23 us -> 4.01 us  [gather_blocks(): return lax.all_to_all(spread, axis_name, 0, 0, tiled=True)]
    all_to_all x2, starting transfers between devices: 13.7 us -> 10.7 us  [gather_blocks(): return lax.all_to_all(spread, axis_name, 0, 0, tiled=True)]
    all_to_all x1, starting transfers between devices: 5.95 us -> 4.25 us  [scatter_sum(): received = lax.all_to_all(split, axis_name, 1, 1, tiled=True)]
  transfers between devices with their start and end apart: 3 -> 3, of which waited for: 2 -> 2; matrix products, arithmetic and copies ran while one was open for 20% -> 18% of each run, Pallas kernels for 0% -> 0%
where the time goes in v4:
time: 148 us; the launch traced here: 146 us
  blocking collectives  60.4 us (41%)
  other arithmetic  26.1 us (18%)
  waiting for transfers between devices  23.5 us (16%)
  starting transfers between devices  15 us (10%)
  local copies, waits for them, and re-layouts  12 us (8%)
  matrix products  7.83 us (5%)
    all_to_all x2, blocking collectives, gather_blocks(): return lax.all_to_all(spread, axis_name, 0, 0, tiled=True)  38 us
    convert_element_type x1, other arithmetic, phase_tile(): jnp.cos(angles).astype(jnp.bfloat16)  22.5 us
    all_to_all x1, blocking collectives, scatter_sum(): received = lax.all_to_all(split, axis_name, 1, 1, tiled=True)  22.4 us
    all_to_all x1, waiting for transfers between devices, scatter_sum(): received = lax.all_to_all(split, axis_name, 1, 1, tiled=True)  19.5 us
    all_to_all x2, starting transfers between devices, gather_blocks(): return lax.all_to_all(spread, axis_name, 0, 0, tiled=True)  10.7 us
    dot_general x1, matrix products, adjoint_terms(): lax.dot_general(left_side, right_side, (((1,), (1,)), ((), ())), preferre...  4.77 us
    all_to_all x1, starting transfers between devices, scatter_sum(): received = lax.all_to_all(split, axis_name, 1, 1, tiled=True)  4.25 us
    all_to_all x2, waiting for transfers between devices, gather_blocks(): return lax.all_to_all(spread, axis_name, 0, 0, tiled=True)  4.01 us
  transfers between devices with their start and end apart: 3, of which 2 were waited for; matrix products, arithmetic and copies ran while one was open for 18% of the time, Pallas kernels for 0%

profile of v4, /device:TPU:32, one launch (start us, length us, event | category | flops | bytes accessed | tf_op | source)
XLA Modules:
  0.0 145.7 jit_solution(3739812071987932066)
XLA Ops:
  0.6 0.7 stack.6
  1.3 0.7 stack.7
  2.0 0.1 fusion.57
  2.1 19.9 %all_to_all.30 = f32[16,2,40]{2,1,0:T(2,128)S(1)} all-to-all(f32[16,2,40]{2,1,0:T(2,128)S(1)} %broadcast_in_dim.13), channel_id=1, replica_groups=mesh['dom'=16,'dir'=16] {'dir'}, dimensions={0} | all-to-all | bytes 10240 | tf_op jit(solution)/shard_map/all_to_all | solution.py:112
  22.0 1.3 broadcast_in_dim.12
  23.3 5.9 %all-to-all-start.1 = ((f32[16,3,128]{2,1,0:T(4,128)}), f32[16,3,128]{2,1,0:T(4,128)S(1)}, u32[]{:S(2)}, u32[]{:S(2)}) async-start(f32[16,3,128]{2,1,0:T(4,128)} %broadcast_in_dim.12), calls=%async_computation.1 | async-start | bytes 65536 | tf_op jit(solution)/shard_map/all_to_all | solution.py:112
  29.3 0.8 copy.14
  30.1 4.0 %all-to-all-done.1 = f32[16,3,128]{2,1,0:T(4,128)S(1)} async-done(((f32[16,3,128]{2,1,0:T(4,128)}), f32[16,3,128]{2,1,0:T(4,128)S(1)}, u32[]{:S(2)}, u32[]{:S(2)}) %all-to-all-start.1) | async-done | bytes 24608 | tf_op jit(solution)/shard_map/all_to_all | solution.py:112
  34.1 0.9 broadcast_in_dim.11
  35.0 4.8 %all-to-all-start = ((bf16[16,140,128]{2,1,0:T(8,128)(2,1)}), bf16[16,140,128]{2,1,0:T(8,128)(2,1)S(1)}, u32[]{:S(2)}, u32[]{:S(2)}) async-start(bf16[16,140,128]{2,1,0:T(8,128)(2,1)} %broadcast_in_dim.11), calls=%async_computation | async-start | bytes 1179648 | tf_op jit(solution)/shard_map/all_to_all | solution.py:112
  39.7 0.5 multiply_reduce_fusion.1
  40.3 0.1 mul.243
  40.4 0.1 mul.249
  40.5 0.1 cos.23
  40.6 22.5 %cosine_convert_fusion = (bf16[2048,640]{1,0:T(8,128)(2,1)S(1)}, bf16[2048,640]{1,0:T(8,128)(2,1)}) fusion(f32[640]{0:T(1024)S(1)} %cos.23, f32[2048]{0:T(1024)S(1)} %bitcast.90, f32[640]{0:T(1024)S(1)} %mul.249, f32[2048]{0:T(1024)S(1)} %bitcast.91, f32[640]{0:T(1024)S(1)} %mul.243, f32[2048]{0:T(1024)S(1)} %bitcast.89), kind=kLoop, calls=%fused_computation.9 | loop fusion | flops 9175040 | bytes 5275136 | tf_op jit(solution)/shard_map/convert_element_type | solution.py:22
  63.1 0.0 all-to-all-done
  63.1 0.0 copy-start
  63.1 0.1 fusion.60
  63.3 0.1 copy.26
  63.4 0.1 copy.25
  63.5 0.1 neg.6
  63.6 1.3 copy-done
  64.8 3.1 %fusion = f32[140,640]{0,1:T(8,128)} fusion(bf16[2048,640]{1,0:T(8,128)(2,1)S(1)} %copy-done, bf16[2048,640]{1,0:T(8,128)(2,1)S(1)} %get-tuple-element.35, bf16[70,2048]{1,0:T(8,128)(2,1)S(1)} %neg.6, bf16[70,2048]{1,0:T(8,128)(2,1)S(1)} %bitcast.75, bf16[70,2048]{1,0:T(8,128)(2,1)S(1)} %bitcast.68), kind=kOutput, calls=%fused_computation | convolution fusion | flops 749076480 | bytes 6461440 | tf_op jit(solution)/shard_map/dot_general | solution.py:33
  67.9 4.3 %all-to-all-start.3 = ((f32[140,16,40]{0,2,1:T(8,128)}), f32[140,16,40]{0,2,1:T(8,128)}, u32[]{:S(2)}, u32[]{:S(2)}) async-start(f32[140,16,40]{0,2,1:T(8,128)} %bitcast.81), calls=%async_computation.3 | async-start | bytes 1310720 | tf_op jit(solution)/shard_map/all_to_all | solution.py:118
  72.2 0.8 dynamic_slice.9
  72.9 1.4 constant_dynamic-slice_fusion
  74.4 0.1 copy.23
  74.4 0.1 copy.24
  74.5 19.5 %all-to-all-done.3 = f32[140,16,40]{0,2,1:T(8,128)} async-done(((f32[140,16,40]{0,2,1:T(8,128)}), f32[140,16,40]{0,2,1:T(8,128)}, u32[]{:S(2)}, u32[]{:S(2)}) %all-to-all-start.3) | async-done | bytes 358432 | tf_op jit(solution)/shard_map/all_to_all | solution.py:118
  94.0 1.1 reduce_sum.81
  95.1 0.0 copy-start.1
  95.1 0.1 fusion.65
  95.2 0.1 fusion.50
  95.3 0.1 fusion.54
  95.4 0.1 multiply_convert_fusion.1
  95.5 0.1 pad_maximum_fusion
  95.6 18.1 %all_to_all.31 = bf16[16,140,40]{1,2,0:T(8,128)(2,1)S(1)} all-to-all(bf16[16,140,40]{1,2,0:T(8,128)(2,1)S(1)} %broadcast_in_dim.14), channel_id=1, replica_groups=mesh['dom'=16,'dir'=16] {'dir'}, dimensions={0} | all-to-all | bytes 358400 | tf_op jit(solution)/shard_map/all_to_all | solution.py:112
  113.7 0.1 fusion.61
  113.8 0.3 fusion.40
  114.1 0.1 fusion.64
  114.3 0.2 fusion.62
  114.4 0.4 maximum_negate_fusion
  114.8 0.0 copy-done.1
  114.8 4.8 %fusion.4 = f32[560,2048]{1,0:T(8,128)S(1)} fusion(bf16[2048,640]{1,0:T(8,128)(2,1)S(1)} %copy-done.1, bf16[2048,640]{1,0:T(8,128)(2,1)S(1)} %get-tuple-element.35, bf16[280,640]{0,1:T(8,128)(2,1)S(1)} %maximum_negate_fusion, bf16[70,640]{0,1:T(8,128)(2,1)S(1)} %get-tuple-element.28, bf16[70,640]{0,1:T(8,128)(2,1)S(1)} %get-tuple-element.43, ...), kind=kOutput, calls=%fused_computation.4 | convolution fusion | flops 2965135360 | bytes 10905600 | tf_op jit(solution)/shard_map/dot_general | solution.py:44
  119.6 0.7 fusion.48
  120.3 0.1 copy.28
  120.5 0.2 copy.19
  120.7 0.1 copy.27
  120.8 0.2 copy.18
  121.0 1.0 concatenate.60
  122.0 22.4 %all_to_all.32 = f32[143,16,128]{2,0,1:T(8,128)S(1)} all-to-all(f32[143,16,128]{2,0,1:T(8,128)S(1)} %concatenate.60), channel_id=1, replica_groups=mesh['dom'=16,'dir'=16] {'dom'}, dimensions={1} | all-to-all | bytes 2342912 | tf_op jit(solution)/shard_map/all_to_all | solution.py:118
  144.4 0.1 reduce_sum.89
  144.5 0.6 slice.181
  145.1 0.7 copy.20
  (14 shorter events, 0.3 us)
Async XLA Ops:
  23.3 10.7 %all-to-all-start.1 = ((f32[16,3,128]{2,1,0:T(4,128)}), f32[16,3,128]{2,1,0:T(4,128)S(1)}, u32[]{:S(2)}, u32[]{:S(2)}) async-start(f32[16,3,128]{2,1,0:T(4,128)} %broadcast_in_dim.12), calls=%async_computation.1 | async-start | bytes 65536 | tf_op jit(solution)/shard_map/all_to_all | solution.py:112
  35.0 28.1 %all-to-all-start = ((bf16[16,140,128]{2,1,0:T(8,128)(2,1)}), bf16[16,140,128]{2,1,0:T(8,128)(2,1)S(1)}, u32[]{:S(2)}, u32[]{:S(2)}) async-start(bf16[16,140,128]{2,1,0:T(8,128)(2,1)} %broadcast_in_dim.11), calls=%async_computation | async-start | bytes 1179648 | tf_op jit(solution)/shard_map/all_to_all | solution.py:112
  63.1 1.7 %copy-start = (bf16[2048,640]{1,0:T(8,128)(2,1)S(1)}, bf16[2048,640]{1,0:T(8,128)(2,1)}, u32[]{:S(2)}) copy-start(bf16[2048,640]{1,0:T(8,128)(2,1)} %get-tuple-element.36) | copy-start | bytes 7864324
  67.9 26.1 %all-to-all-start.3 = ((f32[140,16,40]{0,2,1:T(8,128)}), f32[140,16,40]{0,2,1:T(8,128)}, u32[]{:S(2)}, u32[]{:S(2)}) async-start(f32[140,16,40]{0,2,1:T(8,128)} %bitcast.81), calls=%async_computation.3 | async-start | bytes 1310720 | tf_op jit(solution)/shard_map/all_to_all | solution.py:118
  95.1 19.7 %copy-start.1 = (bf16[2048,640]{1,0:T(8,128)(2,1)S(1)}, bf16[2048,640]{1,0:T(8,128)(2,1)}, u32[]{:S(2)}) copy-start(bf16[2048,640]{1,0:T(8,128)(2,1)} %get-tuple-element.36) | copy-start | bytes 7864324

commit v5 on v3

--- a/solution.py
+++ b/solution.py
@@ -123,15 +123,6 @@
     return jnp.sum(received, axis=1)
 
 
-def gather_dir(block, sizes):
-    inner = gather_blocks(block, DIR_AXES[1], sizes[1])
-    outer = gather_blocks(inner, DIR_AXES[0], sizes[0])
-    rows, width = block.shape
-    return jnp.moveaxis(outer.reshape(sizes[0] * sizes[1], rows, width), 0, 1).reshape(
-        rows, sizes[0] * sizes[1] * width
-    )
-
-
 def scatter_dir(part, sizes):
     rows, width = part.shape
     split = part.reshape(rows, sizes[0], sizes[1] * width // (sizes[0] * sizes[1]))
@@ -141,9 +132,13 @@
 
 def body(coefficients, positions, polar, azimuth, weights, farmap, dir_sizes, dom_size):
     own_count = coefficients.shape[2]
+    dir_size = dir_sizes[0] * dir_sizes[1]
     own_rows = coefficients.reshape(2 * C, own_count)
-    domain_rows = gather_dir(own_rows, dir_sizes)
-    domain_places = gather_dir(positions, dir_sizes)
+    place_blocks = gather_blocks(positions, DIR_AXES, dir_size)
+    domain_places = jnp.moveaxis(place_blocks, 0, 1).reshape(3, dir_size * own_count)
+    own_rows, domain_places = lax.optimization_barrier((own_rows, domain_places))
+    coef_blocks = gather_blocks(own_rows, DIR_AXES, dir_size)
+    domain_rows = jnp.moveaxis(coef_blocks, 0, 1).reshape(2 * C, dir_size * own_count)
     vectors = unit_vectors(polar, azimuth)
     cos_tile, sin_tile = phase_tile(domain_places, vectors)
     partial_fields = field_terms(domain_rows, cos_tile, sin_tile)

time: 148 us -> 135 us (0.912)
  waiting for transfers between devices: 28.1 us -> 17.3 us
  starting transfers between devices: 24.6 us -> 19.7 us
  blocking collectives: 45.8 us -> 49.7 us
    all_to_all x4 -> x2, waiting for transfers between devices: 19.3 us -> 8.5 us  [gather_blocks(): return lax.all_to_all(spread, axis_name, 0, 0, tiled=True)]
    all_to_all x4 -> x2, starting transfers between devices: 18.7 us -> 13.7 us  [gather_blocks(): return lax.all_to_all(spread, axis_name, 0, 0, tiled=True)]
    all_to_all x1, blocking collectives: 13.2 us -> 17.1 us  [scatter_sum(): received = lax.all_to_all(split, axis_name, 1, 1, tiled=True)]
    broadcast_in_dim x6 -> x3, local copies, waits for them, and re-layouts: 3.57 us -> 2.23 us  [gather_blocks(): spread = jnp.broadcast_to(block[None], (size,) + block.shape)]
  transfers between devices with their start and end apart: 5 -> 3, of which waited for: 4 -> 2; matrix products, arithmetic and copies ran while one was open for 19% -> 20% of each run, Pallas kernels for 0% -> 0%
where the time goes in v5:
time: 135 us; the launch traced here: 133 us
  blocking collectives  49.7 us (37%)
  other arithmetic  26.4 us (20%)
  starting transfers between devices  19.7 us (15%)
  waiting for transfers between devices  17.3 us (13%)
  local copies, waits for them, and re-layouts  11.4 us (8%)
  matrix products  7.97 us (6%)
    convert_element_type x1, other arithmetic, phase_tile(): jnp.cos(angles).astype(jnp.bfloat16)  22.6 us
    all_to_all x1, blocking collectives, scatter_dir(): lax.all_to_all(split, DIR_AXES[0], 1, 1, tiled=True)  21.2 us
    all_to_all x1, blocking collectives, scatter_sum(): received = lax.all_to_all(split, axis_name, 1, 1, tiled=True)  17.1 us
    all_to_all x2, starting transfers between devices, gather_blocks(): return lax.all_to_all(spread, axis_name, 0, 0, tiled=True)  13.7 us
    all_to_all x1, blocking collectives, gather_blocks(): return lax.all_to_all(spread, axis_name, 0, 0, tiled=True)  11.4 us
    all_to_all x1, waiting for transfers between devices, scatter_sum(): received = lax.all_to_all(split, axis_name, 1, 1, tiled=True)  8.85 us
    all_to_all x2, waiting for transfers between devices, gather_blocks(): return lax.all_to_all(spread, axis_name, 0, 0, tiled=True)  8.5 us
    all_to_all x1, starting transfers between devices, scatter_sum(): received = lax.all_to_all(split, axis_name, 1, 1, tiled=True)  5.94 us
  transfers between devices with their start and end apart: 3, of which 2 were waited for; matrix products, arithmetic and copies ran while one was open for 20% of the time, Pallas kernels for 0%

profile of v5, /device:TPU:32, one launch (start us, length us, event | category | flops | bytes accessed | tf_op | source)
XLA Modules:
  0.0 133.4 jit_solution(12954478252862845767)
XLA Ops:
  0.6 1.3 broadcast_in_dim.6
  1.9 10.1 %all-to-all-start = ((f32[16,3,128]{2,1,0:T(4,128)}), f32[16,3,128]{2,1,0:T(4,128)S(1)}, u32[]{:S(2)}, u32[]{:S(2)}) async-start(f32[16,3,128]{2,1,0:T(4,128)} %broadcast_in_dim.6), calls=%async_computation | async-start | bytes 65536 | tf_op jit(solution)/shard_map/all_to_all | solution.py:116
  12.1 0.7 fusion.66
  12.8 0.8 copy.22
  13.6 8.5 %all-to-all-done = f32[16,3,128]{2,1,0:T(4,128)S(1)} async-done(((f32[16,3,128]{2,1,0:T(4,128)}), f32[16,3,128]{2,1,0:T(4,128)S(1)}, u32[]{:S(2)}, u32[]{:S(2)}) %all-to-all-start) | async-done | bytes 24608 | tf_op jit(solution)/shard_map/all_to_all | solution.py:116
  22.1 0.9 broadcast_in_dim.7
  23.0 3.6 %all-to-all-start.1 = ((bf16[16,140,128]{2,1,0:T(8,128)(2,1)}), bf16[16,140,128]{2,1,0:T(8,128)(2,1)S(1)}, u32[]{:S(2)}, u32[]{:S(2)}) async-start(bf16[16,140,128]{2,1,0:T(8,128)(2,1)} %broadcast_in_dim.7), calls=%async_computation.1 | async-start | bytes 1179648 | tf_op jit(solution)/shard_map/all_to_all | solution.py:116
  26.6 0.7 cosine_multiply_fusion
  27.3 22.6 %cosine_convert_fusion = (bf16[2048,640]{1,0:T(8,128)(2,1)S(1)}, bf16[2048,640]{1,0:T(8,128)(2,1)}) fusion(f32[640]{0:T(1024)S(1)} %get-tuple-element.46, f32[2048]{0:T(1024)S(1)} %bitcast.80, f32[640]{0:T(1024)S(1)} %get-tuple-element.44, f32[2048]{0:T(1024)S(1)} %bitcast.81, f32[640]{0:T(1024)S(1)} %get-tuple-element.43, f32[2048]{0:T(1024)S(1)} %bitcast.79), kind=kLoop, calls=%fused_computation.9 | loop fusion | flops 9175040 | bytes 5275136 | tf_op jit(solution)/shard_map/convert_element_type | solution.py:22
  49.9 0.0 all-to-all-done.1
  49.9 0.0 copy-start
  49.9 0.1 fusion.59
  50.1 0.1 copy.35
  50.2 0.1 copy.34
  50.3 0.1 neg.6
  50.4 1.3 copy-done
  51.7 3.1 %fusion = f32[140,640]{0,1:T(8,128)} fusion(bf16[2048,640]{1,0:T(8,128)(2,1)S(1)} %copy-done, bf16[2048,640]{1,0:T(8,128)(2,1)S(1)} %get-tuple-element.38, bf16[70,2048]{1,0:T(8,128)(2,1)S(1)} %neg.6, bf16[70,2048]{1,0:T(8,128)(2,1)S(1)} %bitcast.66, bf16[70,2048]{1,0:T(8,128)(2,1)S(1)} %bitcast.63), kind=kOutput, calls=%fused_computation | convolution fusion | flops 749076480 | bytes 6461440 | tf_op jit(solution)/shard_map/dot_general | solution.py:33
  54.7 5.9 %all-to-all-start.2 = ((f32[140,16,40]{0,2,1:T(8,128)}), f32[140,16,40]{0,2,1:T(8,128)}, u32[]{:S(2)}, u32[]{:S(2)}) async-start(f32[140,16,40]{0,2,1:T(8,128)} %bitcast.72), calls=%async_computation.2 | async-start | bytes 1310720 | tf_op jit(solution)/shard_map/all_to_all | solution.py:122
  60.7 0.8 dynamic_slice.6
  61.5 1.4 %constant_dynamic-slice_fusion = (f32[2,1,70,40]{3,1,2,0:T(1,128)S(1)}, f32[2,1,70,40]{3,1,2,0:T(1,128)S(1)}) fusion(f32[2,2,70,640]{3,1,2,0:T(2,128)} %param.11, s32[]{:T(128)S(6)} %select_n.4, s32[]{:T(128)S(6)} %add.41), kind=kLoop, calls=%fused_computation.88 | loop fusion | bytes 89608 | tf_op jit(solution)/shard_map/slice | solution.py:53
  62.9 0.1 copy.32
  63.0 0.1 copy.33
  63.0 8.9 %all-to-all-done.2 = f32[140,16,40]{0,2,1:T(8,128)} async-done(((f32[140,16,40]{0,2,1:T(8,128)}), f32[140,16,40]{0,2,1:T(8,128)}, u32[]{:S(2)}, u32[]{:S(2)}) %all-to-all-start.2) | async-done | bytes 358432 | tf_op jit(solution)/shard_map/all_to_all | solution.py:122
  71.9 1.1 reduce_sum.90
  73.0 0.0 copy-start.1
  73.1 0.1 fusion.64
  73.1 0.1 fusion.50
  73.2 0.1 fusion.54
  73.3 0.1 multiply_convert_fusion.1
  73.4 0.1 pad_maximum_fusion
  73.5 11.4 %all_to_all.30 = bf16[16,140,40]{1,2,0:T(8,128)(2,1)S(1)} all-to-all(bf16[16,140,40]{1,2,0:T(8,128)(2,1)S(1)} %broadcast_in_dim.8), channel_id=1, replica_groups=mesh['y'=4,'z_lo'=2,'core'=2,'x'=4,'z_hi'=4] {'y','z_lo','core'}, dimensions={0} | all-to-all | bytes 358400 | tf_op jit(solution)/shard_map/all_to_all | solution.py:116
  84.9 0.1 fusion.60
  85.0 0.3 fusion.40
  85.4 0.1 fusion.63
  85.5 0.2 fusion.61
  85.7 0.4 maximum_negate_fusion
  86.1 0.0 copy-done.1
  86.1 4.9 %fusion.4 = f32[560,2048]{1,0:T(8,128)S(1)} fusion(bf16[2048,640]{1,0:T(8,128)(2,1)S(1)} %copy-done.1, bf16[2048,640]{1,0:T(8,128)(2,1)S(1)} %get-tuple-element.38, bf16[280,640]{0,1:T(8,128)(2,1)S(1)} %maximum_negate_fusion, bf16[70,640]{0,1:T(8,128)(2,1)S(1)} %get-tuple-element.31, bf16[70,640]{0,1:T(8,128)(2,1)S(1)} %get-tuple-element.50, ...), kind=kOutput, calls=%fused_computation.4 | convolution fusion | flops 2965135360 | bytes 10905600 | tf_op jit(solution)/shard_map/dot_general | solution.py:44
  91.0 0.7 fusion.48
  91.7 0.4 concatenate.59
  92.0 0.2 copy.27
  92.2 0.4 concatenate.58
  92.6 0.2 copy.26
  92.8 0.6 concatenate.60
  93.5 21.2 %all_to_all.31 = f32[143,4,512]{2,0,1:T(8,128)S(1)} all-to-all(f32[143,4,512]{2,0,1:T(8,128)S(1)} %concatenate.60), channel_id=1, replica_groups=mesh['y'=4,'z_lo'=2,'core'=2,'x'=4,'z_hi'=4] {'x'}, dimensions={1} | all-to-all | bytes 2342912 | tf_op jit(solution)/shard_map/all_to_all | solution.py:129
  114.7 0.1 reduce_sum.98
  114.8 0.1 reshape.117
  114.9 17.1 %all_to_all.32 = f32[143,4,128]{2,0,1:T(8,128)S(1)} all-to-all(f32[143,4,128]{2,0,1:T(8,128)S(1)} %copy.28), channel_id=1, replica_groups=mesh['y'=4,'z_lo'=2,'core'=2,'x'=4,'z_hi'=4] {'z_hi'}, dimensions={1} | all-to-all | bytes 585728 | tf_op jit(solution)/shard_map/all_to_all | solution.py:122
  132.1 0.6 slice.163
  132.7 0.7 copy.29
  (13 shorter events, 0.2 us)
Async XLA Ops:
  1.9 20.2 %all-to-all-start = ((f32[16,3,128]{2,1,0:T(4,128)}), f32[16,3,128]{2,1,0:T(4,128)S(1)}, u32[]{:S(2)}, u32[]{:S(2)}) async-start(f32[16,3,128]{2,1,0:T(4,128)} %broadcast_in_dim.6), calls=%async_computation | async-start | bytes 65536 | tf_op jit(solution)/shard_map/all_to_all | solution.py:116
  23.0 26.9 %all-to-all-start.1 = ((bf16[16,140,128]{2,1,0:T(8,128)(2,1)}), bf16[16,140,128]{2,1,0:T(8,128)(2,1)S(1)}, u32[]{:S(2)}, u32[]{:S(2)}) async-start(bf16[16,140,128]{2,1,0:T(8,128)(2,1)} %broadcast_in_dim.7), calls=%async_computation.1 | async-start | bytes 1179648 | tf_op jit(solution)/shard_map/all_to_all | solution.py:116
  49.9 1.7 %copy-start = (bf16[2048,640]{1,0:T(8,128)(2,1)S(1)}, bf16[2048,640]{1,0:T(8,128)(2,1)}, u32[]{:S(2)}) copy-start(bf16[2048,640]{1,0:T(8,128)(2,1)} %get-tuple-element.39) | copy-start | bytes 7864324
  54.7 17.2 %all-to-all-start.2 = ((f32[140,16,40]{0,2,1:T(8,128)}), f32[140,16,40]{0,2,1:T(8,128)}, u32[]{:S(2)}, u32[]{:S(2)}) async-start(f32[140,16,40]{0,2,1:T(8,128)} %bitcast.72), calls=%async_computation.2 | async-start | bytes 1310720 | tf_op jit(solution)/shard_map/all_to_all | solution.py:122
  73.0 13.0 %copy-start.1 = (bf16[2048,640]{1,0:T(8,128)(2,1)S(1)}, bf16[2048,640]{1,0:T(8,128)(2,1)}, u32[]{:S(2)}) copy-start(bf16[2048,640]{1,0:T(8,128)(2,1)} %get-tuple-element.39) | copy-start | bytes 7864324

commit v6 on v5

--- a/solution.py
+++ b/solution.py
@@ -126,8 +126,25 @@
 def scatter_dir(part, sizes):
     rows, width = part.shape
     split = part.reshape(rows, sizes[0], sizes[1] * width // (sizes[0] * sizes[1]))
-    outer = jnp.sum(lax.all_to_all(split, DIR_AXES[0], 1, 1, tiled=True), axis=1)
-    return scatter_sum(outer, DIR_AXES[1], sizes[1])
+    received = lax.all_to_all(narrow_rows(split), DIR_AXES[0], 1, 1, tiled=True)
+    outer = jnp.sum(widen_rows(received), axis=1)
+    inner = outer.reshape(rows, sizes[1], width // (sizes[0] * sizes[1]))
+    received = lax.all_to_all(narrow_rows(inner), DIR_AXES[1], 1, 1, tiled=True)
+    return jnp.sum(widen_rows(received), axis=1)
+
+
+def narrow_rows(part):
+    coef_rows = part[: 2 * C].astype(jnp.bfloat16)
+    place_high = part[2 * C :].astype(jnp.bfloat16)
+    place_low = (part[2 * C :] - place_high.astype(jnp.float32)).astype(jnp.bfloat16)
+    return jnp.concatenate([coef_rows, place_high, place_low], axis=0)
+
+
+def widen_rows(packed):
+    wide = packed.astype(jnp.float32)
+    place_count = (packed.shape[0] - 2 * C) // 2
+    place_rows = wide[2 * C : 2 * C + place_count] + wide[2 * C + place_count :]
+    return jnp.concatenate([wide[: 2 * C], place_rows], axis=0)
 
 
 def body(coefficients, positions, polar, azimuth, weights, farmap, dir_sizes, dom_size):

time: 135 us -> 126 us (0.933)
  blocking collectives: 49.7 us -> 41.6 us
    all_to_all x2, blocking collectives: 38.4 us -> 30.2 us  [the longest x1 15.2 us: scatter_dir(): received = lax.all_to_all(narrow_rows(split), DIR_AXES[0], 1, 1, tiled=True)]
    concatenate x5 -> x1, local copies, waits for them, and re-layouts: 1.78 us -> 0.02 us  [narrow_rows(): return jnp.concatenate([coef_rows, place_high, place_low], axis=0)]
  transfers between devices with their start and end apart: 3 -> 3, of which waited for: 2 -> 2; matrix products, arithmetic and copies ran while one was open for 20% -> 22% of each run, Pallas kernels for 0% -> 0%
where the time goes in v6:
time: 126 us; the launch traced here: 125 us
  blocking collectives  41.6 us (33%)
  other arithmetic  26.9 us (21%)
  starting transfers between devices  19.7 us (16%)
  waiting for transfers between devices  17.3 us (14%)
  local copies, waits for them, and re-layouts  10.2 us (8%)
  matrix products  7.95 us (6%)
    convert_element_type x1, other arithmetic, phase_tile(): jnp.cos(angles).astype(jnp.bfloat16)  22.5 us
    all_to_all x1, blocking collectives, scatter_dir(): received = lax.all_to_all(narrow_rows(split), DIR_AXES[0], 1, 1, tiled=True)  15.2 us
    all_to_all x1, blocking collectives, scatter_dir(): received = lax.all_to_all(narrow_rows(inner), DIR_AXES[1], 1, 1, tiled=True)  15 us
    all_to_all x2, starting transfers between devices, gather_blocks(): return lax.all_to_all(spread, axis_name, 0, 0, tiled=True)  13.7 us
    all_to_all x1, blocking collectives, gather_blocks(): return lax.all_to_all(spread, axis_name, 0, 0, tiled=True)  11.4 us
    all_to_all x1, waiting for transfers between devices, scatter_sum(): received = lax.all_to_all(split, axis_name, 1, 1, tiled=True)  8.85 us
    all_to_all x2, waiting for transfers between devices, gather_blocks(): return lax.all_to_all(spread, axis_name, 0, 0, tiled=True)  8.5 us
    all_to_all x1, starting transfers between devices, scatter_sum(): received = lax.all_to_all(split, axis_name, 1, 1, tiled=True)  5.94 us
  transfers between devices with their start and end apart: 3, of which 2 were waited for; matrix products, arithmetic and copies ran while one was open for 22% of the time, Pallas kernels for 0%

profile of v6, /device:TPU:32, one launch (start us, length us, event | category | flops | bytes accessed | tf_op | source)
XLA Modules:
  0.0 124.6 jit_solution(17234707402181179199)
XLA Ops:
  0.6 1.3 %broadcast_in_dim.6 = f32[16,3,128]{2,1,0:T(4,128)} broadcast(f32[3,128]{1,0:T(4,128)} %param.7), dimensions={1,2} | broadcast | bytes 26112 | tf_op jit(solution)/shard_map/broadcast_in_dim | solution.py:115
  1.9 10.1 %all-to-all-start = ((f32[16,3,128]{2,1,0:T(4,128)}), f32[16,3,128]{2,1,0:T(4,128)S(1)}, u32[]{:S(2)}, u32[]{:S(2)}) async-start(f32[16,3,128]{2,1,0:T(4,128)} %broadcast_in_dim.6), calls=%async_computation | async-start | bytes 65536 | tf_op jit(solution)/shard_map/all_to_all | solution.py:116
  12.1 0.7 fusion.69
  12.8 0.8 copy.21
  13.6 8.5 %all-to-all-done = f32[16,3,128]{2,1,0:T(4,128)S(1)} async-done(((f32[16,3,128]{2,1,0:T(4,128)}), f32[16,3,128]{2,1,0:T(4,128)S(1)}, u32[]{:S(2)}, u32[]{:S(2)}) %all-to-all-start) | async-done | bytes 24608 | tf_op jit(solution)/shard_map/all_to_all | solution.py:116
  22.1 0.9 broadcast_in_dim.7
  23.0 3.6 %all-to-all-start.1 = ((bf16[16,140,128]{2,1,0:T(8,128)(2,1)}), bf16[16,140,128]{2,1,0:T(8,128)(2,1)S(1)}, u32[]{:S(2)}, u32[]{:S(2)}) async-start(bf16[16,140,128]{2,1,0:T(8,128)(2,1)} %broadcast_in_dim.7), calls=%async_computation.1 | async-start | bytes 1179648 | tf_op jit(solution)/shard_map/all_to_all | solution.py:116
  26.6 0.7 cosine_multiply_fusion
  27.3 22.5 %cosine_convert_fusion = (bf16[2048,640]{1,0:T(8,128)(2,1)S(1)}, bf16[2048,640]{1,0:T(8,128)(2,1)}) fusion(f32[640]{0:T(1024)S(1)} %get-tuple-element.48, f32[2048]{0:T(1024)S(1)} %bitcast.83, f32[640]{0:T(1024)S(1)} %get-tuple-element.46, f32[2048]{0:T(1024)S(1)} %bitcast.84, f32[640]{0:T(1024)S(1)} %get-tuple-element.45, f32[2048]{0:T(1024)S(1)} %bitcast.82), kind=kLoop, calls=%fused_computation.9 | loop fusion | flops 9175040 | bytes 5275136 | tf_op jit(solution)/shard_map/convert_element_type | solution.py:22
  49.9 0.0 all-to-all-done.1
  49.9 0.0 copy-start
  49.9 0.1 fusion.62
  50.1 0.1 copy.33
  50.2 0.1 copy.32
  50.3 0.1 neg.6
  50.4 1.3 %copy-done = bf16[2048,640]{1,0:T(8,128)(2,1)S(1)} copy-done((bf16[2048,640]{1,0:T(8,128)(2,1)S(1)}, bf16[2048,640]{1,0:T(8,128)(2,1)}, u32[]{:S(2)}) %copy-start) | copy-done | bytes 2621464
  51.6 3.1 %fusion = f32[140,640]{0,1:T(8,128)} fusion(bf16[2048,640]{1,0:T(8,128)(2,1)S(1)} %copy-done, bf16[2048,640]{1,0:T(8,128)(2,1)S(1)} %get-tuple-element.40, bf16[70,2048]{1,0:T(8,128)(2,1)S(1)} %neg.6, bf16[70,2048]{1,0:T(8,128)(2,1)S(1)} %bitcast.66, bf16[70,2048]{1,0:T(8,128)(2,1)S(1)} %bitcast.63), kind=kOutput, calls=%fused_computation | convolution fusion | flops 749076480 | bytes 6461440 | tf_op jit(solution)/shard_map/dot_general | solution.py:33
  54.7 5.9 %all-to-all-start.2 = ((f32[140,16,40]{0,2,1:T(8,128)}), f32[140,16,40]{0,2,1:T(8,128)}, u32[]{:S(2)}, u32[]{:S(2)}) async-start(f32[140,16,40]{0,2,1:T(8,128)} %bitcast.72), calls=%async_computation.2 | async-start | bytes 1310720 | tf_op jit(solution)/shard_map/all_to_all | solution.py:122
  60.7 0.8 dynamic_slice.6
  61.4 1.4 %constant_dynamic-slice_fusion = (f32[2,1,70,40]{3,1,2,0:T(1,128)S(1)}, f32[2,1,70,40]{3,1,2,0:T(1,128)S(1)}) fusion(f32[2,2,70,640]{3,1,2,0:T(2,128)} %param.11, s32[]{:T(128)S(6)} %select_n.4, s32[]{:T(128)S(6)} %add.49), kind=kLoop, calls=%fused_computation.102 | loop fusion | bytes 89608 | tf_op jit(solution)/shard_map/slice | solution.py:53
  62.9 0.1 copy.30
  62.9 0.1 copy.31
  63.0 8.9 %all-to-all-done.2 = f32[140,16,40]{0,2,1:T(8,128)} async-done(((f32[140,16,40]{0,2,1:T(8,128)}), f32[140,16,40]{0,2,1:T(8,128)}, u32[]{:S(2)}, u32[]{:S(2)}) %all-to-all-start.2) | async-done | bytes 358432 | tf_op jit(solution)/shard_map/all_to_all | solution.py:122
  71.9 1.1 reduce_sum.90
  73.0 0.0 copy-start.1
  73.0 0.1 fusion.67
  73.1 0.1 fusion.52
  73.2 0.1 fusion.56
  73.3 0.1 multiply_convert_fusion.1
  73.4 0.1 pad_maximum_fusion.4
  73.5 11.4 %all_to_all.30 = bf16[16,140,40]{1,2,0:T(8,128)(2,1)S(1)} all-to-all(bf16[16,140,40]{1,2,0:T(8,128)(2,1)S(1)} %broadcast_in_dim.8), channel_id=1, replica_groups=mesh['y'=4,'z_lo'=2,'core'=2,'x'=4,'z_hi'=4] {'y','z_lo','core'}, dimensions={0} | all-to-all | bytes 358400 | tf_op jit(solution)/shard_map/all_to_all | solution.py:116
  84.9 0.1 fusion.63
  85.0 0.3 fusion.40
  85.3 0.1 fusion.66
  85.5 0.2 fusion.64
  85.6 0.4 maximum_negate_fusion
  86.0 0.0 copy-done.1
  86.0 4.9 %fusion.4 = f32[560,2048]{1,0:T(8,128)S(1)} fusion(bf16[2048,640]{1,0:T(8,128)(2,1)S(1)} %copy-done.1, bf16[2048,640]{1,0:T(8,128)(2,1)S(1)} %get-tuple-element.40, bf16[280,640]{0,1:T(8,128)(2,1)S(1)} %maximum_negate_fusion, bf16[70,640]{0,1:T(8,128)(2,1)S(1)} %get-tuple-element.33, bf16[70,640]{0,1:T(8,128)(2,1)S(1)} %get-tuple-element.52, ...), kind=kOutput, calls=%fused_computation.4 | convolution fusion | flops 2965135360 | bytes 10905600 | tf_op jit(solution)/shard_map/dot_general | solution.py:44
  90.9 0.7 fusion.44
  91.7 0.1 pad_maximum_fusion.1
  91.8 0.3 convert_element_type.71
  92.1 0.1 copy.25
  92.2 0.1 pad_maximum_fusion
  92.3 15.2 %all_to_all.31 = bf16[146,4,512]{2,0,1:T(8,128)(2,1)S(1)} all-to-all(bf16[146,4,512]{2,0,1:T(8,128)(2,1)S(1)} %pad_maximum_fusion), channel_id=1, replica_groups=mesh['y'=4,'z_lo'=2,'core'=2,'x'=4,'z_hi'=4] {'x'}, dimensions={1} | all-to-all | bytes 1196032 | tf_op jit(solution)/shard_map/all_to_all | solution.py:129
  107.6 0.1 convert_element_type.77
  107.7 0.1 slice.208
  107.9 0.1 maximum_reduce_fusion
  108.1 0.1 pad_maximum_fusion.2
  108.3 15.0 %all_to_all.32 = bf16[146,4,128]{2,0,1:T(8,128)(2,1)S(1)} all-to-all(bf16[146,4,128]{2,0,1:T(8,128)(2,1)S(1)} %copy.26), channel_id=1, replica_groups=mesh['y'=4,'z_lo'=2,'core'=2,'x'=4,'z_hi'=4] {'z_hi'}, dimensions={1} | all-to-all | bytes 299008 | tf_op jit(solution)/shard_map/all_to_all | solution.py:132
  123.3 0.6 slice.217
  123.9 0.7 copy.27
  (24 shorter events, 0.5 us)
Async XLA Ops:
  1.9 20.2 %all-to-all-start = ((f32[16,3,128]{2,1,0:T(4,128)}), f32[16,3,128]{2,1,0:T(4,128)S(1)}, u32[]{:S(2)}, u32[]{:S(2)}) async-start(f32[16,3,128]{2,1,0:T(4,128)} %broadcast_in_dim.6), calls=%async_computation | async-start | bytes 65536 | tf_op jit(solution)/shard_map/all_to_all | solution.py:116
  23.0 26.9 %all-to-all-start.1 = ((bf16[16,140,128]{2,1,0:T(8,128)(2,1)}), bf16[16,140,128]{2,1,0:T(8,128)(2,1)S(1)}, u32[]{:S(2)}, u32[]{:S(2)}) async-start(bf16[16,140,128]{2,1,0:T(8,128)(2,1)} %broadcast_in_dim.7), calls=%async_computation.1 | async-start | bytes 1179648 | tf_op jit(solution)/shard_map/all_to_all | solution.py:116
  49.9 1.7 %copy-start = (bf16[2048,640]{1,0:T(8,128)(2,1)S(1)}, bf16[2048,640]{1,0:T(8,128)(2,1)}, u32[]{:S(2)}) copy-start(bf16[2048,640]{1,0:T(8,128)(2,1)} %get-tuple-element.41) | copy-start | bytes 7864324
  54.7 17.2 %all-to-all-start.2 = ((f32[140,16,40]{0,2,1:T(8,128)}), f32[140,16,40]{0,2,1:T(8,128)}, u32[]{:S(2)}, u32[]{:S(2)}) async-start(f32[140,16,40]{0,2,1:T(8,128)} %bitcast.72), calls=%async_computation.2 | async-start | bytes 1310720 | tf_op jit(solution)/shard_map/all_to_all | solution.py:122
  73.0 13.0 %copy-start.1 = (bf16[2048,640]{1,0:T(8,128)(2,1)S(1)}, bf16[2048,640]{1,0:T(8,128)(2,1)}, u32[]{:S(2)}) copy-start(bf16[2048,640]{1,0:T(8,128)(2,1)} %get-tuple-element.41) | copy-start | bytes 7864324

commit v7 on v6

--- a/solution.py
+++ b/solution.py
@@ -125,11 +125,9 @@
 
 def scatter_dir(part, sizes):
     rows, width = part.shape
-    split = part.reshape(rows, sizes[0], sizes[1] * width // (sizes[0] * sizes[1]))
-    received = lax.all_to_all(narrow_rows(split), DIR_AXES[0], 1, 1, tiled=True)
-    outer = jnp.sum(widen_rows(received), axis=1)
-    inner = outer.reshape(rows, sizes[1], width // (sizes[0] * sizes[1]))
-    received = lax.all_to_all(narrow_rows(inner), DIR_AXES[1], 1, 1, tiled=True)
+    size = sizes[0] * sizes[1]
+    split = part.reshape(rows, size, width // size)
+    received = lax.all_to_all(narrow_rows(split), DIR_AXES, 1, 1, tiled=True)
     return jnp.sum(widen_rows(received), axis=1)
 
 

time: 126 us -> 125 us (level)
    unnamed x12 -> x13, local copies, waits for them, and re-layouts: 3.08 us -> 3.19 us
    all_to_all x2 -> x1, blocking collectives: 30.2 us -> 30.3 us  [scatter_dir(): received = lax.all_to_all(narrow_rows(split), DIR_AXES, 1, 1, tiled=True)]
where the time goes in v7:
time: 125 us; the launch traced here: 124 us
  blocking collectives  41.7 us (33%)
  other arithmetic  26.6 us (21%)
  starting transfers between devices  19.7 us (16%)
  waiting for transfers between devices  17.3 us (14%)
  local copies, waits for them, and re-layouts  9.94 us (8%)
  matrix products  7.95 us (6%)
    all_to_all x1, blocking collectives, scatter_dir(): received = lax.all_to_all(narrow_rows(split), DIR_AXES, 1, 1, tiled=True)  30.3 us
    convert_element_type x1, other arithmetic, phase_tile(): jnp.cos(angles).astype(jnp.bfloat16)  22.5 us
    all_to_all x2, starting transfers between devices, gather_blocks(): return lax.all_to_all(spread, axis_name, 0, 0, tiled=True)  13.7 us
    all_to_all x1, blocking collectives, gather_blocks(): return lax.all_to_all(spread, axis_name, 0, 0, tiled=True)  11.4 us
    all_to_all x1, waiting for transfers between devices, scatter_sum(): received = lax.all_to_all(split, axis_name, 1, 1, tiled=True)  8.85 us
    all_to_all x2, waiting for transfers between devices, gather_blocks(): return lax.all_to_all(spread, axis_name, 0, 0, tiled=True)  8.5 us
    all_to_all x1, starting transfers between devices, scatter_sum(): received = lax.all_to_all(split, axis_name, 1, 1, tiled=True)  5.94 us
    dot_general x1, matrix products, adjoint_terms(): lax.dot_general(left_side, right_side, (((1,), (1,)), ((), ())), preferre...  4.87 us
  transfers between devices with their start and end apart: 3, of which 2 were waited for; matrix products, arithmetic and copies ran while one was open for 22% of the time, Pallas kernels for 0%

profile of v7, /device:TPU:32, one launch (start us, length us, event | category | flops | bytes accessed | tf_op | source)
XLA Modules:
  0.0 124.1 jit_solution(17198686846948490236)
XLA Ops:
  0.6 1.3 %broadcast_in_dim.6 = f32[16,3,128]{2,1,0:T(4,128)} broadcast(f32[3,128]{1,0:T(4,128)} %param.7), dimensions={1,2} | broadcast | bytes 26112 | tf_op jit(solution)/shard_map/broadcast_in_dim | solution.py:115
  1.9 10.1 %all-to-all-start = ((f32[16,3,128]{2,1,0:T(4,128)}), f32[16,3,128]{2,1,0:T(4,128)S(1)}, u32[]{:S(2)}, u32[]{:S(2)}) async-start(f32[16,3,128]{2,1,0:T(4,128)} %broadcast_in_dim.6), calls=%async_computation | async-start | bytes 65536 | tf_op jit(solution)/shard_map/all_to_all | solution.py:116
  12.1 0.7 fusion.69
  12.8 0.8 copy.14
  13.6 8.5 %all-to-all-done = f32[16,3,128]{2,1,0:T(4,128)S(1)} async-done(((f32[16,3,128]{2,1,0:T(4,128)}), f32[16,3,128]{2,1,0:T(4,128)S(1)}, u32[]{:S(2)}, u32[]{:S(2)}) %all-to-all-start) | async-done | bytes 24608 | tf_op jit(solution)/shard_map/all_to_all | solution.py:116
  22.1 0.9 broadcast_in_dim.7
  23.0 3.6 %all-to-all-start.1 = ((bf16[16,140,128]{2,1,0:T(8,128)(2,1)}), bf16[16,140,128]{2,1,0:T(8,128)(2,1)S(1)}, u32[]{:S(2)}, u32[]{:S(2)}) async-start(bf16[16,140,128]{2,1,0:T(8,128)(2,1)} %broadcast_in_dim.7), calls=%async_computation.1 | async-start | bytes 1179648 | tf_op jit(solution)/shard_map/all_to_all | solution.py:116
  26.6 0.7 cosine_multiply_fusion
  27.3 22.5 %cosine_convert_fusion = (bf16[2048,640]{1,0:T(8,128)(2,1)S(1)}, bf16[2048,640]{1,0:T(8,128)(2,1)}) fusion(f32[640]{0:T(1024)S(1)} %get-tuple-element.44, f32[2048]{0:T(1024)S(1)} %bitcast.88, f32[640]{0:T(1024)S(1)} %get-tuple-element.42, f32[2048]{0:T(1024)S(1)} %bitcast.89, f32[640]{0:T(1024)S(1)} %get-tuple-element.41, f32[2048]{0:T(1024)S(1)} %bitcast.87), kind=kLoop, calls=%fused_computation.9 | loop fusion | flops 9175040 | bytes 5275136 | tf_op jit(solution)/shard_map/convert_element_type | solution.py:22
  49.9 0.0 all-to-all-done.1
  49.9 0.0 copy-start
  49.9 0.1 fusion.62
  50.1 0.1 copy.25
  50.2 0.1 copy.24
  50.3 0.1 neg.6
  50.4 1.3 %copy-done = bf16[2048,640]{1,0:T(8,128)(2,1)S(1)} copy-done((bf16[2048,640]{1,0:T(8,128)(2,1)S(1)}, bf16[2048,640]{1,0:T(8,128)(2,1)}, u32[]{:S(2)}) %copy-start) | copy-done | bytes 2621464
  51.6 3.1 %fusion = f32[140,640]{0,1:T(8,128)} fusion(bf16[2048,640]{1,0:T(8,128)(2,1)S(1)} %copy-done, bf16[2048,640]{1,0:T(8,128)(2,1)S(1)} %get-tuple-element.36, bf16[70,2048]{1,0:T(8,128)(2,1)S(1)} %neg.6, bf16[70,2048]{1,0:T(8,128)(2,1)S(1)} %bitcast.71, bf16[70,2048]{1,0:T(8,128)(2,1)S(1)} %bitcast.66), kind=kOutput, calls=%fused_computation | convolution fusion | flops 749076480 | bytes 6461440 | tf_op jit(solution)/shard_map/dot_general | solution.py:33
  54.7 5.9 %all-to-all-start.2 = ((f32[140,16,40]{0,2,1:T(8,128)}), f32[140,16,40]{0,2,1:T(8,128)}, u32[]{:S(2)}, u32[]{:S(2)}) async-start(f32[140,16,40]{0,2,1:T(8,128)} %bitcast.77), calls=%async_computation.2 | async-start | bytes 1310720 | tf_op jit(solution)/shard_map/all_to_all | solution.py:122
  60.7 0.8 dynamic_slice.6
  61.4 1.4 %constant_dynamic-slice_fusion = (f32[2,1,70,40]{3,1,2,0:T(1,128)S(1)}, f32[2,1,70,40]{3,1,2,0:T(1,128)S(1)}) fusion(f32[2,2,70,640]{3,1,2,0:T(2,128)} %param.11, s32[]{:T(128)S(6)} %select_n.4, s32[]{:T(128)S(6)} %add.45), kind=kLoop, calls=%fused_computation.97 | loop fusion | bytes 89608 | tf_op jit(solution)/shard_map/slice | solution.py:53
  62.9 0.1 copy.22
  62.9 0.1 copy.23
  63.0 8.9 %all-to-all-done.2 = f32[140,16,40]{0,2,1:T(8,128)} async-done(((f32[140,16,40]{0,2,1:T(8,128)}), f32[140,16,40]{0,2,1:T(8,128)}, u32[]{:S(2)}, u32[]{:S(2)}) %all-to-all-start.2) | async-done | bytes 358432 | tf_op jit(solution)/shard_map/all_to_all | solution.py:122
  71.9 1.1 reduce_sum.81
  73.0 0.0 copy-start.1
  73.0 0.1 fusion.67
  73.1 0.1 fusion.52
  73.2 0.1 fusion.56
  73.3 0.1 multiply_convert_fusion.1
  73.4 0.1 pad_maximum_fusion.3
  73.5 11.4 %all_to_all.25 = bf16[16,140,40]{1,2,0:T(8,128)(2,1)S(1)} all-to-all(bf16[16,140,40]{1,2,0:T(8,128)(2,1)S(1)} %broadcast_in_dim.8), channel_id=1, replica_groups=mesh['y'=4,'z_lo'=2,'core'=2,'x'=4,'z_hi'=4] {'y','z_lo','core'}, dimensions={0} | all-to-all | bytes 358400 | tf_op jit(solution)/shard_map/all_to_all | solution.py:116
  84.9 0.1 fusion.63
  85.0 0.3 fusion.40
  85.3 0.1 fusion.66
  85.5 0.2 fusion.64
  85.6 0.4 maximum_negate_fusion
  86.0 0.0 copy-done.1
  86.0 4.9 %fusion.4 = f32[560,2048]{1,0:T(8,128)S(1)} fusion(bf16[2048,640]{1,0:T(8,128)(2,1)S(1)} %copy-done.1, bf16[2048,640]{1,0:T(8,128)(2,1)S(1)} %get-tuple-element.36, bf16[280,640]{0,1:T(8,128)(2,1)S(1)} %maximum_negate_fusion, bf16[70,640]{0,1:T(8,128)(2,1)S(1)} %get-tuple-element.29, bf16[70,640]{0,1:T(8,128)(2,1)S(1)} %get-tuple-element.48, ...), kind=kOutput, calls=%fused_computation.4 | convolution fusion | flops 2965135360 | bytes 10905600 | tf_op jit(solution)/shard_map/dot_general | solution.py:44
  90.9 0.7 fusion.44
  91.7 0.1 pad_maximum_fusion.1
  91.8 0.1 copy.26
  91.9 0.1 slice.186
  92.0 0.2 copy.18
  92.2 0.1 pad_maximum_fusion
  92.3 30.3 %all_to_all.26 = bf16[146,16,128]{2,0,1:T(8,128)(2,1)S(1)} all-to-all(bf16[146,16,128]{2,0,1:T(8,128)(2,1)S(1)} %pad_maximum_fusion), channel_id=1, replica_groups=mesh['y'=4,'z_lo'=2,'core'=2,'x'=4,'z_hi'=4] {'x','z_hi'}, dimensions={1} | all-to-all | bytes 1196032 | tf_op jit(solution)/shard_map/all_to_all | solution.py:130
  122.6 0.1 convert_element_type.61
  122.7 0.1 slice.181
  122.8 0.1 maximum_reduce_fusion
  122.8 0.6 slice.185
  123.4 0.7 copy.19
  (14 shorter events, 0.3 us)
Async XLA Ops:
  1.9 20.2 %all-to-all-start = ((f32[16,3,128]{2,1,0:T(4,128)}), f32[16,3,128]{2,1,0:T(4,128)S(1)}, u32[]{:S(2)}, u32[]{:S(2)}) async-start(f32[16,3,128]{2,1,0:T(4,128)} %broadcast_in_dim.6), calls=%async_computation | async-start | bytes 65536 | tf_op jit(solution)/shard_map/all_to_all | solution.py:116
  23.0 26.9 %all-to-all-start.1 = ((bf16[16,140,128]{2,1,0:T(8,128)(2,1)}), bf16[16,140,128]{2,1,0:T(8,128)(2,1)S(1)}, u32[]{:S(2)}, u32[]{:S(2)}) async-start(bf16[16,140,128]{2,1,0:T(8,128)(2,1)} %broadcast_in_dim.7), calls=%async_computation.1 | async-start | bytes 1179648 | tf_op jit(solution)/shard_map/all_to_all | solution.py:116
  49.9 1.7 %copy-start = (bf16[2048,640]{1,0:T(8,128)(2,1)S(1)}, bf16[2048,640]{1,0:T(8,128)(2,1)}, u32[]{:S(2)}) copy-start(bf16[2048,640]{1,0:T(8,128)(2,1)} %get-tuple-element.37) | copy-start | bytes 7864324
  54.7 17.2 %all-to-all-start.2 = ((f32[140,16,40]{0,2,1:T(8,128)}), f32[140,16,40]{0,2,1:T(8,128)}, u32[]{:S(2)}, u32[]{:S(2)}) async-start(f32[140,16,40]{0,2,1:T(8,128)} %bitcast.77), calls=%async_computation.2 | async-start | bytes 1310720 | tf_op jit(solution)/shard_map/all_to_all | solution.py:122
  73.0 13.0 %copy-start.1 = (bf16[2048,640]{1,0:T(8,128)(2,1)S(1)}, bf16[2048,640]{1,0:T(8,128)(2,1)}, u32[]{:S(2)}) copy-start(bf16[2048,640]{1,0:T(8,128)(2,1)} %get-tuple-element.37) | copy-start | bytes 7864324

commit v8 on v7

--- a/solution.py
+++ b/solution.py
@@ -3,6 +3,7 @@
 import jax
 import jax.numpy as jnp
 from jax import lax
+import numpy as np
 from jax.sharding import PartitionSpec as P
 
 C = 70
@@ -11,6 +12,29 @@
 def unit_vectors(polar, azimuth):
     sine_polar = jnp.sin(polar)
     return jnp.stack([sine_polar * jnp.cos(azimuth), sine_polar * jnp.sin(azimuth), jnp.cos(polar)])
+
+
+def sine_cosine(angles):
+    quarter = jnp.round(angles * np.float32(2.0 / np.pi))
+    reduced = angles - quarter * np.float32(1.5703125)
+    reduced = reduced - quarter * np.float32(4.837512969970703125e-4)
+    reduced = reduced - quarter * np.float32(7.54978995489188216e-8)
+    square = reduced * reduced
+    sine = reduced + reduced * square * (
+        np.float32(-1 / 6)
+        + square * (np.float32(1 / 120) + square * (np.float32(-1 / 5040) + square * np.float32(1 / 362880)))
+    )
+    cosine = np.float32(1) + square * (
+        np.float32(-0.5)
+        + square * (np.float32(1 / 24) + square * (np.float32(-1 / 720) + square * np.float32(1 / 40320)))
+    )
+    turn = quarter.astype(jnp.int32)
+    odd = (turn & 1) == 1
+    cos_base = jnp.where(odd, sine, cosine)
+    sin_base = jnp.where(odd, cosine, sine)
+    cos_value = jnp.where(((turn + 1) & 2) == 2, -cos_base, cos_base)
+    sin_value = jnp.where((turn & 2) == 2, -sin_base, sin_base)
+    return (cos_value, sin_value)
 
 
 def phase_tile(places, vectors):
@@ -19,7 +43,8 @@
         + places[1][:, None] * vectors[1][None, :]
         + places[2][:, None] * vectors[2][None, :]
     )
-    return (jnp.cos(angles).astype(jnp.bfloat16), jnp.sin(angles).astype(jnp.bfloat16))
+    cos_value, sin_value = sine_cosine(angles)
+    return (cos_value.astype(jnp.bfloat16), sin_value.astype(jnp.bfloat16))
 
 
 def field_terms(coef_block, cos_tile, sin_tile):

time: 125 us -> 115 us (0.920)
  other arithmetic: 26.6 us -> 13.4 us
  waiting for transfers between devices: 17.3 us -> 26.2 us
  blocking collectives: 41.7 us -> 35.8 us
    convert_element_type x1, other arithmetic: 22.5 us -> 9.33 us  [phase_tile(): return (cos_value.astype(jnp.bfloat16), sin_value.astype(jnp.bfloat16))]
    all_to_all x2, waiting for transfers between devices: 8.5 us -> 17.4 us  [gather_blocks(): return lax.all_to_all(spread, axis_name, 0, 0, tiled=True)]
    all_to_all x1, blocking collectives: 30.3 us -> 24.4 us  [scatter_dir(): received = lax.all_to_all(narrow_rows(split), DIR_AXES, 1, 1, tiled=True)]
  transfers between devices with their start and end apart: 3 -> 3, of which waited for: 2 -> 3; matrix products, arithmetic and copies ran while one was open for 22% -> 12% of each run, Pallas kernels for 0% -> 0%
where the time goes in v8:
time: 115 us; the launch traced here: 114 us
  blocking collectives  35.8 us (31%)
  waiting for transfers between devices  26.2 us (23%)
  starting transfers between devices  19.7 us (17%)
  other arithmetic  13.4 us (12%)
  local copies, waits for them, and re-layouts  9.94 us (9%)
  matrix products  7.95 us (7%)
    all_to_all x1, blocking collectives, scatter_dir(): received = lax.all_to_all(narrow_rows(split), DIR_AXES, 1, 1, tiled=True)  24.4 us
    all_to_all x2, waiting for transfers between devices, gather_blocks(): return lax.all_to_all(spread, axis_name, 0, 0, tiled=True)  17.4 us
    all_to_all x2, starting transfers between devices, gather_blocks(): return lax.all_to_all(spread, axis_name, 0, 0, tiled=True)  13.7 us
    all_to_all x1, blocking collectives, gather_blocks(): return lax.all_to_all(spread, axis_name, 0, 0, tiled=True)  11.4 us
    convert_element_type x1, other arithmetic, phase_tile(): return (cos_value.astype(jnp.bfloat16), sin_value.astype(jnp.bfloat16))  9.33 us
    all_to_all x1, waiting for transfers between devices, scatter_sum(): received = lax.all_to_all(split, axis_name, 1, 1, tiled=True)  8.85 us
    all_to_all x1, starting transfers between devices, scatter_sum(): received = lax.all_to_all(split, axis_name, 1, 1, tiled=True)  5.94 us
    dot_general x1, matrix products, adjoint_terms(): lax.dot_general(left_side, right_side, (((1,), (1,)), ((), ())), preferre...  4.87 us
  transfers between devices with their start and end apart: 3, of which 3 were waited for; matrix products, arithmetic and copies ran while one was open for 12% of the time, Pallas kernels for 0%

profile of v8, /device:TPU:32, one launch (start us, length us, event | category | flops | bytes accessed | tf_op | source)
XLA Modules:
  0.0 113.8 jit_solution(17630378881761829108)
XLA Ops:
  0.6 1.3 %broadcast_in_dim.6 = f32[16,3,128]{2,1,0:T(4,128)} broadcast(f32[3,128]{1,0:T(4,128)} %param.7), dimensions={1,2} | broadcast | bytes 26112 | tf_op jit(solution)/shard_map/broadcast_in_dim | solution.py:140
  1.9 10.1 %all-to-all-start = ((f32[16,3,128]{2,1,0:T(4,128)}), f32[16,3,128]{2,1,0:T(4,128)S(1)}, u32[]{:S(2)}, u32[]{:S(2)}) async-start(f32[16,3,128]{2,1,0:T(4,128)} %broadcast_in_dim.6), calls=%async_computation | async-start | bytes 65536 | tf_op jit(solution)/shard_map/all_to_all | solution.py:141
  12.1 0.7 fusion.80
  12.8 0.7 cosine_multiply_fusion
  13.5 0.8 copy.14
  14.3 7.8 %all-to-all-done = f32[16,3,128]{2,1,0:T(4,128)S(1)} async-done(((f32[16,3,128]{2,1,0:T(4,128)}), f32[16,3,128]{2,1,0:T(4,128)S(1)}, u32[]{:S(2)}, u32[]{:S(2)}) %all-to-all-start) | async-done | bytes 24608 | tf_op jit(solution)/shard_map/all_to_all | solution.py:141
  22.1 0.9 broadcast_in_dim.7
  23.0 3.6 %all-to-all-start.1 = ((bf16[16,140,128]{2,1,0:T(8,128)(2,1)}), bf16[16,140,128]{2,1,0:T(8,128)(2,1)S(1)}, u32[]{:S(2)}, u32[]{:S(2)}) async-start(bf16[16,140,128]{2,1,0:T(8,128)(2,1)} %broadcast_in_dim.7), calls=%async_computation.1 | async-start | bytes 1179648 | tf_op jit(solution)/shard_map/all_to_all | solution.py:141
  26.6 9.3 %fusion.9 = (bf16[2048,640]{1,0:T(8,128)(2,1)S(1)}, bf16[2048,640]{1,0:T(8,128)(2,1)}) fusion(f32[640]{0:T(1024)S(1)} %get-tuple-element.44, f32[2048]{0:T(1024)S(1)} %bitcast.88, f32[640]{0:T(1024)S(1)} %get-tuple-element.42, f32[2048]{0:T(1024)S(1)} %bitcast.89, f32[640]{0:T(1024)S(1)} %get-tuple-element.41, f32[2048]{0:T(1024)S(1)} %bitcast.87), kind=kLoop, calls=%fused_computation.19 | loop fusion | flops 61603840 | bytes 5275136 | tf_op jit(solution)/shard_map/convert_element_type | solution.py:47
  35.9 9.6 %all-to-all-done.1 = bf16[16,140,128]{2,1,0:T(8,128)(2,1)S(1)} async-done(((bf16[16,140,128]{2,1,0:T(8,128)(2,1)}), bf16[16,140,128]{2,1,0:T(8,128)(2,1)S(1)}, u32[]{:S(2)}, u32[]{:S(2)}) %all-to-all-start.1) | async-done | bytes 573472 | tf_op jit(solution)/shard_map/all_to_all | solution.py:141
  45.5 0.0 copy-start
  45.5 0.1 fusion.73
  45.7 0.1 copy.25
  45.9 0.1 copy.24
  46.0 0.1 neg.12
  46.0 1.3 %copy-done = bf16[2048,640]{1,0:T(8,128)(2,1)S(1)} copy-done((bf16[2048,640]{1,0:T(8,128)(2,1)S(1)}, bf16[2048,640]{1,0:T(8,128)(2,1)}, u32[]{:S(2)}) %copy-start) | copy-done | bytes 2621464
  47.3 3.1 %fusion.11 = f32[140,640]{0,1:T(8,128)} fusion(bf16[2048,640]{1,0:T(8,128)(2,1)S(1)} %copy-done, bf16[2048,640]{1,0:T(8,128)(2,1)S(1)} %get-tuple-element.36, bf16[70,2048]{1,0:T(8,128)(2,1)S(1)} %neg.12, bf16[70,2048]{1,0:T(8,128)(2,1)S(1)} %bitcast.71, bf16[70,2048]{1,0:T(8,128)(2,1)S(1)} %bitcast.66), kind=kOutput, calls=%fused_computation.21 | convolution fusion | flops 749076480 | bytes 6461440 | tf_op jit(solution)/shard_map/dot_general | solution.py:58
  50.4 5.9 %all-to-all-start.2 = ((f32[140,16,40]{0,2,1:T(8,128)}), f32[140,16,40]{0,2,1:T(8,128)}, u32[]{:S(2)}, u32[]{:S(2)}) async-start(f32[140,16,40]{0,2,1:T(8,128)} %bitcast.77), calls=%async_computation.2 | async-start | bytes 1310720 | tf_op jit(solution)/shard_map/all_to_all | solution.py:147
  56.3 0.8 dynamic_slice.6
  57.1 1.4 %constant_dynamic-slice_fusion = (f32[2,1,70,40]{3,1,2,0:T(1,128)S(1)}, f32[2,1,70,40]{3,1,2,0:T(1,128)S(1)}) fusion(f32[2,2,70,640]{3,1,2,0:T(2,128)} %param.11, s32[]{:T(128)S(6)} %select_n.17, s32[]{:T(128)S(6)} %add.109), kind=kLoop, calls=%fused_computation.121 | loop fusion | bytes 89608 | tf_op jit(solution)/shard_map/slice | solution.py:78
  58.5 0.1 copy.22
  58.6 0.1 copy.23
  58.7 8.9 %all-to-all-done.2 = f32[140,16,40]{0,2,1:T(8,128)} async-done(((f32[140,16,40]{0,2,1:T(8,128)}), f32[140,16,40]{0,2,1:T(8,128)}, u32[]{:S(2)}, u32[]{:S(2)}) %all-to-all-start.2) | async-done | bytes 358432 | tf_op jit(solution)/shard_map/all_to_all | solution.py:147
  67.5 1.1 %reduce_sum.81 = f32[140,40]{0,1:T(8,128)S(1)} reduce(f32[140,16,40]{0,2,1:T(8,128)} %all-to-all-done.2, f32[]{:T(128)} %constant.59.clone.1), dimensions={1}, to_apply=%region_0.1 | reduce | flops 84000 | bytes 380804 | tf_op jit(solution)/shard_map/reduce_sum | solution.py:148
  68.7 0.0 copy-start.1
  68.7 0.1 fusion.78
  68.7 0.1 fusion.63
  68.9 0.1 fusion.67
  69.0 0.1 multiply_convert_fusion.1
  69.0 0.1 pad_maximum_fusion.3
  69.1 11.4 %all_to_all.25 = bf16[16,140,40]{1,2,0:T(8,128)(2,1)S(1)} all-to-all(bf16[16,140,40]{1,2,0:T(8,128)(2,1)S(1)} %broadcast_in_dim.8), channel_id=1, replica_groups=mesh['y'=4,'z_lo'=2,'core'=2,'x'=4,'z_hi'=4] {'y','z_lo','core'}, dimensions={0} | all-to-all | bytes 358400 | tf_op jit(solution)/shard_map/all_to_all | solution.py:141
  80.5 0.1 fusion.74
  80.7 0.3 fusion.51
  81.0 0.1 fusion.77
  81.1 0.2 fusion.75
  81.3 0.4 maximum_negate_fusion
  81.7 0.0 copy-done.1
  81.7 4.9 %fusion.15 = f32[560,2048]{1,0:T(8,128)S(1)} fusion(bf16[2048,640]{1,0:T(8,128)(2,1)S(1)} %copy-done.1, bf16[2048,640]{1,0:T(8,128)(2,1)S(1)} %get-tuple-element.36, bf16[280,640]{0,1:T(8,128)(2,1)S(1)} %maximum_negate_fusion, bf16[70,640]{0,1:T(8,128)(2,1)S(1)} %get-tuple-element.29, bf16[70,640]{0,1:T(8,128)(2,1)S(1)} %get-tuple-element.48, ...), kind=kOutput, calls=%fused_computation.25 | convolution fusion | flops 2965135360 | bytes 10905600 | tf_op jit(solution)/shard_map/dot_general | solution.py:69
  86.6 0.6 fusion.55
  87.3 0.1 pad_maximum_fusion.1
  87.4 0.1 copy.26
  87.6 0.1 slice.186
  87.7 0.2 copy.18
  87.8 0.1 pad_maximum_fusion
  87.9 24.4 %all_to_all.26 = bf16[146,16,128]{2,0,1:T(8,128)(2,1)S(1)} all-to-all(bf16[146,16,128]{2,0,1:T(8,128)(2,1)S(1)} %pad_maximum_fusion), channel_id=1, replica_groups=mesh['y'=4,'z_lo'=2,'core'=2,'x'=4,'z_hi'=4] {'x','z_hi'}, dimensions={1} | all-to-all | bytes 1196032 | tf_op jit(solution)/shard_map/all_to_all | solution.py:155
  112.3 0.1 convert_element_type.65
  112.4 0.1 slice.181
  112.5 0.1 maximum_reduce_fusion
  112.5 0.6 slice.185
  113.1 0.7 copy.19
  (14 shorter events, 0.3 us)
Async XLA Ops:
  1.9 20.2 %all-to-all-start = ((f32[16,3,128]{2,1,0:T(4,128)}), f32[16,3,128]{2,1,0:T(4,128)S(1)}, u32[]{:S(2)}, u32[]{:S(2)}) async-start(f32[16,3,128]{2,1,0:T(4,128)} %broadcast_in_dim.6), calls=%async_computation | async-start | bytes 65536 | tf_op jit(solution)/shard_map/all_to_all | solution.py:141
  23.0 22.5 %all-to-all-start.1 = ((bf16[16,140,128]{2,1,0:T(8,128)(2,1)}), bf16[16,140,128]{2,1,0:T(8,128)(2,1)S(1)}, u32[]{:S(2)}, u32[]{:S(2)}) async-start(bf16[16,140,128]{2,1,0:T(8,128)(2,1)} %broadcast_in_dim.7), calls=%async_computation.1 | async-start | bytes 1179648 | tf_op jit(solution)/shard_map/all_to_all | solution.py:141
  45.5 1.7 %copy-start = (bf16[2048,640]{1,0:T(8,128)(2,1)S(1)}, bf16[2048,640]{1,0:T(8,128)(2,1)}, u32[]{:S(2)}) copy-start(bf16[2048,640]{1,0:T(8,128)(2,1)} %get-tuple-element.37) | copy-start | bytes 7864324
  50.4 17.2 %all-to-all-start.2 = ((f32[140,16,40]{0,2,1:T(8,128)}), f32[140,16,40]{0,2,1:T(8,128)}, u32[]{:S(2)}, u32[]{:S(2)}) async-start(f32[140,16,40]{0,2,1:T(8,128)} %bitcast.77), calls=%async_computation.2 | async-start | bytes 1310720 | tf_op jit(solution)/shard_map/all_to_all | solution.py:147
  68.7 13.0 %copy-start.1 = (bf16[2048,640]{1,0:T(8,128)(2,1)S(1)}, bf16[2048,640]{1,0:T(8,128)(2,1)}, u32[]{:S(2)}) copy-start(bf16[2048,640]{1,0:T(8,128)(2,1)} %get-tuple-element.37) | copy-start | bytes 7864324

commit v9 on v8

--- a/solution.py
+++ b/solution.py
@@ -174,11 +174,11 @@
     own_count = coefficients.shape[2]
     dir_size = dir_sizes[0] * dir_sizes[1]
     own_rows = coefficients.reshape(2 * C, own_count)
+    coef_blocks = gather_blocks(own_rows, DIR_AXES, dir_size)
+    domain_rows = jnp.moveaxis(coef_blocks, 0, 1).reshape(2 * C, dir_size * own_count)
+    positions, domain_rows = lax.optimization_barrier((positions, domain_rows))
     place_blocks = gather_blocks(positions, DIR_AXES, dir_size)
     domain_places = jnp.moveaxis(place_blocks, 0, 1).reshape(3, dir_size * own_count)
-    own_rows, domain_places = lax.optimization_barrier((own_rows, domain_places))
-    coef_blocks = gather_blocks(own_rows, DIR_AXES, dir_size)
-    domain_rows = jnp.moveaxis(coef_blocks, 0, 1).reshape(2 * C, dir_size * own_count)
     vectors = unit_vectors(polar, azimuth)
     cos_tile, sin_tile = phase_tile(domain_places, vectors)
     partial_fields = field_terms(domain_rows, cos_tile, sin_tile)

time: 115 us -> 123 us (1.070)
  waiting for transfers between devices: 26.2 us -> 36.1 us
  local copies, waits for them, and re-layouts: 9.94 us -> 8.03 us
    all_to_all x2, waiting for transfers between devices: 17.4 us -> 27.2 us  [gather_blocks(): return lax.all_to_all(spread, axis_name, 0, 0, tiled=True)]
    unnamed x13 -> x17, local copies, waits for them, and re-layouts: 3.19 us -> 2 us
  transfers between devices with their start and end apart: 3 -> 3, of which waited for: 3 -> 3; matrix products, arithmetic and copies ran while one was open for 12% -> 4% of each run, Pallas kernels for 0% -> 0%
where the time goes in v9:
time: 123 us; the launch traced here: 122 us
  waiting for transfers between devices  36.1 us (29%)
  blocking collectives  35.2 us (29%)
  starting transfers between devices  19.9 us (16%)
  other arithmetic  13.7 us (11%)
  local copies, waits for them, and re-layouts  8.03 us (7%)
  matrix products  7.96 us (6%)
    all_to_all x2, waiting for transfers between devices, gather_blocks(): return lax.all_to_all(spread, axis_name, 0, 0, tiled=True)  27.2 us
    all_to_all x1, blocking collectives, scatter_dir(): received = lax.all_to_all(narrow_rows(split), DIR_AXES, 1, 1, tiled=True)  23.8 us
    all_to_all x2, starting transfers between devices, gather_blocks(): return lax.all_to_all(spread, axis_name, 0, 0, tiled=True)  13.8 us
    all_to_all x1, blocking collectives, gather_blocks(): return lax.all_to_all(spread, axis_name, 0, 0, tiled=True)  11.4 us
    all_to_all x1, waiting for transfers between devices, scatter_sum(): received = lax.all_to_all(split, axis_name, 1, 1, tiled=True)  8.85 us
    convert_element_type x1, other arithmetic, phase_tile(): return (cos_value.astype(jnp.bfloat16), sin_value.astype(jnp.bfloat16))  8.75 us
    all_to_all x1, starting transfers between devices, scatter_sum(): received = lax.all_to_all(split, axis_name, 1, 1, tiled=True)  6.11 us
    dot_general x1, matrix products, adjoint_terms(): lax.dot_general(left_side, right_side, (((1,), (1,)), ((), ())), preferre...  4.88 us
  transfers between devices with their start and end apart: 3, of which 3 were waited for; matrix products, arithmetic and copies ran while one was open for 4% of the time, Pallas kernels for 0%

profile of v9, /device:TPU:32, one launch (start us, length us, event | category | flops | bytes accessed | tf_op | source)
XLA Modules:
  0.0 121.8 jit_solution(11865914434424668468)
XLA Ops:
  0.6 0.0 copy-start.4
  0.6 0.8 copy.14
  1.4 0.9 broadcast_in_dim.9
  2.3 10.1 %all-to-all-start = ((bf16[16,140,128]{2,1,0:T(8,128)(2,1)}), bf16[16,140,128]{2,1,0:T(8,128)(2,1)S(1)}, u32[]{:S(2)}, u32[]{:S(2)}) async-start(bf16[16,140,128]{2,1,0:T(8,128)(2,1)} %broadcast_in_dim.9), calls=%async_computation | async-start | bytes 1179648 | tf_op jit(solution)/shard_map/all_to_all | solution.py:141
  12.5 0.7 fusion.80
  13.2 0.7 cosine_multiply_fusion
  13.9 18.1 %all-to-all-done = bf16[16,140,128]{2,1,0:T(8,128)(2,1)S(1)} async-done(((bf16[16,140,128]{2,1,0:T(8,128)(2,1)}), bf16[16,140,128]{2,1,0:T(8,128)(2,1)S(1)}, u32[]{:S(2)}, u32[]{:S(2)}) %all-to-all-start) | async-done | bytes 573472 | tf_op jit(solution)/shard_map/all_to_all | solution.py:141
  32.0 0.1 copy.15
  32.2 0.1 pad.37
  32.3 0.2 copy.23
  32.5 0.0 copy-done.4
  32.5 0.6 broadcast_in_dim.10
  33.1 3.7 %all-to-all-start.1 = ((f32[16,3,128]{2,1,0:T(4,128)}), f32[16,3,128]{2,1,0:T(4,128)S(1)}, u32[]{:S(2)}, u32[]{:S(2)}) async-start(f32[16,3,128]{2,1,0:T(4,128)} %broadcast_in_dim.10), calls=%async_computation.1 | async-start | bytes 65536 | tf_op jit(solution)/shard_map/all_to_all | solution.py:141
  36.8 0.9 fusion.73
  37.7 9.1 %all-to-all-done.1 = f32[16,3,128]{2,1,0:T(4,128)S(1)} async-done(((f32[16,3,128]{2,1,0:T(4,128)}), f32[16,3,128]{2,1,0:T(4,128)S(1)}, u32[]{:S(2)}, u32[]{:S(2)}) %all-to-all-start.1) | async-done | bytes 24608 | tf_op jit(solution)/shard_map/all_to_all | solution.py:141
  46.8 0.0 copy-start.2
  46.8 0.0 copy-start.3
  46.9 8.7 %fusion.9 = (bf16[2048,640]{1,0:T(8,128)(2,1)S(1)}, bf16[2048,640]{1,0:T(8,128)(2,1)S(1)}) fusion(f32[640]{0:T(1024)S(1)} %get-tuple-element.45, f32[2048]{0:T(1024)S(1)} %bitcast.79, f32[640]{0:T(1024)S(1)} %get-tuple-element.43, f32[2048]{0:T(1024)S(1)} %bitcast.80, f32[640]{0:T(1024)S(1)} %get-tuple-element.42, f32[2048]{0:T(1024)S(1)} %bitcast.78), kind=kLoop, calls=%fused_computation.19 | loop fusion | flops 61603840 | bytes 5275136 | tf_op jit(solution)/shard_map/convert_element_type | solution.py:47
  55.6 0.0 copy-start
  55.6 0.0 copy-done.2
  55.6 0.0 copy-done.3
  55.7 3.1 %fusion.11 = f32[140,640]{0,1:T(8,128)} fusion(bf16[2048,640]{1,0:T(8,128)(2,1)S(1)} %get-tuple-element.38, bf16[2048,640]{1,0:T(8,128)(2,1)S(1)} %get-tuple-element.37, bf16[70,2048]{1,0:T(8,128)(2,1)S(1)} %copy-done.2, bf16[70,2048]{1,0:T(8,128)(2,1)S(1)} %copy-done.3, bf16[70,2048]{1,0:T(8,128)(2,1)S(1)} %get-tuple-element.21), kind=kOutput, calls=%fused_computation.21 | convolution fusion | flops 749076480 | bytes 6461440 | tf_op jit(solution)/shard_map/dot_general | solution.py:58
  58.7 0.0 copy-done
  58.7 6.1 %all-to-all-start.2 = ((f32[140,16,40]{0,2,1:T(8,128)}), f32[140,16,40]{0,2,1:T(8,128)}, u32[]{:S(2)}, u32[]{:S(2)}) async-start(f32[140,16,40]{0,2,1:T(8,128)} %bitcast.68), calls=%async_computation.2 | async-start | bytes 1310720 | tf_op jit(solution)/shard_map/all_to_all | solution.py:147
  64.8 0.8 dynamic_slice.6
  65.6 1.4 %constant_dynamic-slice_fusion = (f32[2,1,70,40]{3,1,2,0:T(1,128)S(1)}, f32[2,1,70,40]{3,1,2,0:T(1,128)S(1)}) fusion(f32[2,2,70,640]{3,1,2,0:T(2,128)} %param.11, s32[]{:T(128)S(6)} %select_n.17, s32[]{:T(128)S(6)} %add.109), kind=kLoop, calls=%fused_computation.121 | loop fusion | bytes 89608 | tf_op jit(solution)/shard_map/slice | solution.py:78
  67.0 0.1 copy.21
  67.1 0.1 copy.22
  67.2 8.9 %all-to-all-done.2 = f32[140,16,40]{0,2,1:T(8,128)} async-done(((f32[140,16,40]{0,2,1:T(8,128)}), f32[140,16,40]{0,2,1:T(8,128)}, u32[]{:S(2)}, u32[]{:S(2)}) %all-to-all-start.2) | async-done | bytes 358432 | tf_op jit(solution)/shard_map/all_to_all | solution.py:147
  76.1 1.1 reduce_sum.81
  77.2 0.0 copy-start.1
  77.2 0.1 fusion.78
  77.3 0.1 fusion.63
  77.4 0.1 fusion.67
  77.5 0.1 multiply_convert_fusion.1
  77.6 0.1 pad_maximum_fusion.3
  77.7 11.4 %all_to_all.25 = bf16[16,140,40]{1,2,0:T(8,128)(2,1)S(1)} all-to-all(bf16[16,140,40]{1,2,0:T(8,128)(2,1)S(1)} %broadcast_in_dim.11), channel_id=1, replica_groups=mesh['y'=4,'z_lo'=2,'core'=2,'x'=4,'z_hi'=4] {'y','z_lo','core'}, dimensions={0} | all-to-all | bytes 358400 | tf_op jit(solution)/shard_map/all_to_all | solution.py:141
  89.1 0.1 fusion.74
  89.2 0.3 fusion.51
  89.5 0.1 fusion.77
  89.6 0.2 fusion.75
  89.8 0.4 maximum_negate_fusion
  90.2 0.0 copy-done.1
  90.2 4.9 %fusion.15 = f32[560,2048]{1,0:T(8,128)S(1)} fusion(bf16[2048,640]{1,0:T(8,128)(2,1)S(1)} %copy-done.1, bf16[2048,640]{1,0:T(8,128)(2,1)S(1)} %get-tuple-element.37, bf16[280,640]{0,1:T(8,128)(2,1)S(1)} %maximum_negate_fusion, bf16[70,640]{0,1:T(8,128)(2,1)S(1)} %get-tuple-element.30, bf16[70,640]{0,1:T(8,128)(2,1)S(1)} %get-tuple-element.49, ...), kind=kOutput, calls=%fused_computation.25 | convolution fusion | flops 2965135360 | bytes 10905600 | tf_op jit(solution)/shard_map/dot_general | solution.py:69
  95.1 0.7 fusion.55
  95.9 0.1 pad_maximum_fusion.1
  96.0 0.1 copy.24
  96.1 0.1 slice.182
  96.2 0.2 copy.17
  96.4 0.1 pad_maximum_fusion
  96.5 23.8 %all_to_all.26 = bf16[146,16,128]{2,0,1:T(8,128)(2,1)S(1)} all-to-all(bf16[146,16,128]{2,0,1:T(8,128)(2,1)S(1)} %pad_maximum_fusion), channel_id=1, replica_groups=mesh['y'=4,'z_lo'=2,'core'=2,'x'=4,'z_hi'=4] {'x','z_hi'}, dimensions={1} | all-to-all | bytes 1196032 | tf_op jit(solution)/shard_map/all_to_all | solution.py:155
  120.3 0.1 convert_element_type.65
  120.4 0.1 slice.177
  120.5 0.1 maximum_reduce_fusion
  120.6 0.6 slice.181
  121.2 0.7 copy.18
  (10 shorter events, 0.2 us)
Async XLA Ops:
  0.6 31.8 %copy-start.4 = (f32[3,128]{1,0:T(4,128)S(1)}, f32[3,128]{1,0:T(4,128)}, u32[]{:S(2)}) copy-start(f32[3,128]{1,0:T(4,128)} %param.7) | copy-start | bytes 4612
  2.3 29.7 %all-to-all-start = ((bf16[16,140,128]{2,1,0:T(8,128)(2,1)}), bf16[16,140,128]{2,1,0:T(8,128)(2,1)S(1)}, u32[]{:S(2)}, u32[]{:S(2)}) async-start(bf16[16,140,128]{2,1,0:T(8,128)(2,1)} %broadcast_in_dim.9), calls=%async_computation | async-start | bytes 1179648 | tf_op jit(solution)/shard_map/all_to_all | solution.py:141
  33.1 13.7 %all-to-all-start.1 = ((f32[16,3,128]{2,1,0:T(4,128)}), f32[16,3,128]{2,1,0:T(4,128)S(1)}, u32[]{:S(2)}, u32[]{:S(2)}) async-start(f32[16,3,128]{2,1,0:T(4,128)} %broadcast_in_dim.10), calls=%async_computation.1 | async-start | bytes 65536 | tf_op jit(solution)/shard_map/all_to_all | solution.py:141
  46.8 8.8 %copy-start.2 = (bf16[70,2048]{1,0:T(8,128)(2,1)S(1)}, bf16[70,2048]{1,0:T(8,128)(2,1)}, u32[]{:S(2)}) copy-start(bf16[70,2048]{1,0:T(8,128)(2,1)} %get-tuple-element.22) | copy-start | bytes 860164
  46.8 8.8 %copy-start.3 = (bf16[70,2048]{1,0:T(8,128)(2,1)S(1)}, bf16[70,2048]{1,0:T(8,128)(2,1)}, u32[]{:S(2)}) copy-start(bf16[70,2048]{1,0:T(8,128)(2,1)} %get-tuple-element.23) | copy-start | bytes 860164
  55.6 3.1 %copy-start = (bf16[2048,640]{1,0:T(8,128)(2,1)}, bf16[2048,640]{1,0:T(8,128)(2,1)S(1)}, u32[]{:S(2)}) copy-start(bf16[2048,640]{1,0:T(8,128)(2,1)S(1)} %get-tuple-element.38) | copy-start | bytes 7864324
  58.7 17.3 %all-to-all-start.2 = ((f32[140,16,40]{0,2,1:T(8,128)}), f32[140,16,40]{0,2,1:T(8,128)}, u32[]{:S(2)}, u32[]{:S(2)}) async-start(f32[140,16,40]{0,2,1:T(8,128)} %bitcast.68), calls=%async_computation.2 | async-start | bytes 1310720 | tf_op jit(solution)/shard_map/all_to_all | solution.py:147
  77.2 13.0 %copy-start.1 = (bf16[2048,640]{1,0:T(8,128)(2,1)S(1)}, bf16[2048,640]{1,0:T(8,128)(2,1)}, u32[]{:S(2)}) copy-start(bf16[2048,640]{1,0:T(8,128)(2,1)} %copy-done) | copy-start | bytes 7864324

commit v10 on v8

--- a/solution.py
+++ b/solution.py
@@ -184,13 +184,19 @@
     partial_fields = field_terms(domain_rows, cos_tile, sin_tile)
     dir_count = polar.shape[0]
     slice_width = dir_count // dom_size
-    fields_slice = scatter_sum(partial_fields, DOM_AXES, dom_size)
+    flat_fields = jnp.transpose(
+        partial_fields.reshape(2 * C, dom_size, slice_width), (1, 0, 2)
+    ).reshape(dom_size, 2 * C * slice_width)
+    received_fields = lax.all_to_all(flat_fields, DOM_AXES, 0, 0, tiled=True)
+    fields_slice = jnp.sum(received_fields, axis=0).reshape(2 * C, slice_width)
     offset = lax.axis_index(DOM_AXES) * slice_width
     farmap_slice = lax.dynamic_slice_in_dim(farmap, offset, slice_width, 3)
     weights_slice = lax.dynamic_slice_in_dim(weights, offset, slice_width, 0)
     adjoint_slice = cotangent_rows(fields_slice, farmap_slice, weights_slice)
-    adjoint_blocks = gather_blocks(adjoint_slice, DOM_AXES, dom_size)
-    adjoint = jnp.moveaxis(adjoint_blocks, 0, 1).reshape(2 * C, dir_count)
+    adjoint_blocks = gather_blocks(adjoint_slice.reshape(2 * C * slice_width), DOM_AXES, dom_size)
+    adjoint = jnp.transpose(
+        adjoint_blocks.reshape(dom_size, 2 * C, slice_width), (1, 0, 2)
+    ).reshape(2 * C, dir_count)
     stacked = stacked_rows(adjoint, vectors)
     coef_part, place_part = gradients(adjoint_terms(stacked, cos_tile, sin_tile), domain_rows)
     part = jnp.concatenate([coef_part, place_part], axis=0)

time: 115 us -> 120 us (1.043)
  local copies, waits for them, and re-layouts: 9.94 us -> 18.7 us
  waiting for transfers between devices: 26.2 us -> 22.9 us
  blocking collectives: 35.8 us -> 33.4 us
  other arithmetic: 13.4 us -> 15.2 us
    all_to_all x1, waiting for transfers between devices: 8.85 us -> 5.56 us  [body(): received_fields = lax.all_to_all(flat_fields, DOM_AXES, 0, 0, tiled=True)]
    reshape x0 -> x2, local copies, waits for them, and re-layouts: none -> 3.05 us  [body(): adjoint_blocks.reshape(dom_size, 2 * C, slice_width)]
    all_to_all x1, blocking collectives: 11.4 us -> 9.4 us  [gather_blocks(): return lax.all_to_all(spread, axis_name, 0, 0, tiled=True)]
    all_to_all x0 -> x1, local copies, waits for them, and re-layouts: none -> 1.91 us  [body(): received_fields = lax.all_to_all(flat_fields, DOM_AXES, 0, 0, tiled=True)]
    broadcast_in_dim x0 -> x1, other arithmetic: none -> 1.7 us  [gather_blocks(): spread = jnp.broadcast_to(block[None], (size,) + block.shape)]
    transpose x0 -> x1, local copies, waits for them, and re-layouts: none -> 1.51 us  [body(): jnp.transpose(partial_fields.reshape(2 * C, dom_size, slice_width), (1, 0...]
    unnamed x13 -> x19, local copies, waits for them, and re-layouts: 3.19 us -> 4.26 us
    broadcast_in_dim x3 -> x4, local copies, waits for them, and re-layouts: 2.23 us -> 2.92 us  [gather_blocks(): spread = jnp.broadcast_to(block[None], (size,) + block.shape)]
where the time goes in v10:
time: 120 us; the launch traced here: 119 us
  blocking collectives  33.4 us (28%)
  waiting for transfers between devices  22.9 us (19%)
  starting transfers between devices  19.7 us (16%)
  local copies, waits for them, and re-layouts  18.7 us (16%)
  other arithmetic  15.2 us (13%)
  matrix products  7.83 us (7%)
    all_to_all x1, blocking collectives, scatter_dir(): received = lax.all_to_all(narrow_rows(split), DIR_AXES, 1, 1, tiled=True)  24 us
    all_to_all x2, waiting for transfers between devices, gather_blocks(): return lax.all_to_all(spread, axis_name, 0, 0, tiled=True)  17.4 us
    all_to_all x2, starting transfers between devices, gather_blocks(): return lax.all_to_all(spread, axis_name, 0, 0, tiled=True)  13.7 us
    all_to_all x1, blocking collectives, gather_blocks(): return lax.all_to_all(spread, axis_name, 0, 0, tiled=True)  9.4 us
    convert_element_type x1, other arithmetic, phase_tile(): return (cos_value.astype(jnp.bfloat16), sin_value.astype(jnp.bfloat16))  9.33 us
    all_to_all x1, starting transfers between devices, body(): received_fields = lax.all_to_all(flat_fields, DOM_AXES, 0, 0, tiled=True)  5.94 us
    all_to_all x1, waiting for transfers between devices, body(): received_fields = lax.all_to_all(flat_fields, DOM_AXES, 0, 0, tiled=True)  5.56 us
    dot_general x1, matrix products, adjoint_terms(): lax.dot_general(left_side, right_side, (((1,), (1,)), ((), ())), preferre...  4.76 us
  transfers between devices with their start and end apart: 3, of which 3 were waited for; matrix products, arithmetic and copies ran while one was open for 12% of the time, Pallas kernels for 0%

profile of v10, /device:TPU:32, one launch (start us, length us, event | category | flops | bytes accessed | tf_op | source)
XLA Modules:
  0.0 118.7 jit_solution(5341020483761513782)
XLA Ops:
  0.6 1.3 %broadcast_in_dim.6 = f32[16,3,128]{2,1,0:T(4,128)} broadcast(f32[3,128]{1,0:T(4,128)} %param.7), dimensions={1,2} | broadcast | bytes 26112 | tf_op jit(solution)/shard_map/broadcast_in_dim | solution.py:140
  1.9 10.1 %all-to-all-start = ((f32[16,3,128]{2,1,0:T(4,128)}), f32[16,3,128]{2,1,0:T(4,128)S(1)}, u32[]{:S(2)}, u32[]{:S(2)}) async-start(f32[16,3,128]{2,1,0:T(4,128)} %broadcast_in_dim.6), calls=%async_computation | async-start | bytes 65536 | tf_op jit(solution)/shard_map/all_to_all | solution.py:141
  12.1 0.7 fusion.80
  12.8 0.7 cosine_multiply_fusion
  13.5 0.8 copy.35
  14.3 7.8 %all-to-all-done = f32[16,3,128]{2,1,0:T(4,128)S(1)} async-done(((f32[16,3,128]{2,1,0:T(4,128)}), f32[16,3,128]{2,1,0:T(4,128)S(1)}, u32[]{:S(2)}, u32[]{:S(2)}) %all-to-all-start) | async-done | bytes 24608 | tf_op jit(solution)/shard_map/all_to_all | solution.py:141
  22.1 0.9 broadcast_in_dim.7
  23.0 3.6 %all-to-all-start.1 = ((bf16[16,140,128]{2,1,0:T(8,128)(2,1)}), bf16[16,140,128]{2,1,0:T(8,128)(2,1)S(1)}, u32[]{:S(2)}, u32[]{:S(2)}) async-start(bf16[16,140,128]{2,1,0:T(8,128)(2,1)} %broadcast_in_dim.7), calls=%async_computation.1 | async-start | bytes 1179648 | tf_op jit(solution)/shard_map/all_to_all | solution.py:141
  26.6 9.3 %fusion.9 = (bf16[2048,640]{1,0:T(8,128)(2,1)S(1)}, bf16[2048,640]{1,0:T(8,128)(2,1)}) fusion(f32[640]{0:T(1024)S(1)} %get-tuple-element.46, f32[2048]{0:T(1024)S(1)} %bitcast.90, f32[640]{0:T(1024)S(1)} %get-tuple-element.44, f32[2048]{0:T(1024)S(1)} %bitcast.91, f32[640]{0:T(1024)S(1)} %get-tuple-element.43, f32[2048]{0:T(1024)S(1)} %bitcast.89), kind=kLoop, calls=%fused_computation.19 | loop fusion | flops 61603840 | bytes 5275136 | tf_op jit(solution)/shard_map/convert_element_type | solution.py:47
  35.9 9.6 %all-to-all-done.1 = bf16[16,140,128]{2,1,0:T(8,128)(2,1)S(1)} async-done(((bf16[16,140,128]{2,1,0:T(8,128)(2,1)}), bf16[16,140,128]{2,1,0:T(8,128)(2,1)S(1)}, u32[]{:S(2)}, u32[]{:S(2)}) %all-to-all-start.1) | async-done | bytes 573472 | tf_op jit(solution)/shard_map/all_to_all | solution.py:141
  45.6 0.1 fusion.73
  45.7 0.1 copy.52
  45.9 0.1 copy.51
  46.0 0.1 neg.12
  46.0 1.3 %copy-done.2 = bf16[2048,640]{1,0:T(8,128)(2,1)S(1)} copy-done((bf16[2048,640]{1,0:T(8,128)(2,1)S(1)}, bf16[2048,640]{1,0:T(8,128)(2,1)}, u32[]{:S(2)}) %copy-start.2) | copy-done | bytes 2621464
  47.3 3.1 %fusion.11 = f32[140,640]{0,1:T(8,128)} fusion(bf16[2048,640]{1,0:T(8,128)(2,1)S(1)} %copy-done.2, bf16[2048,640]{1,0:T(8,128)(2,1)S(1)} %get-tuple-element.36, bf16[70,2048]{1,0:T(8,128)(2,1)S(1)} %neg.12, bf16[70,2048]{1,0:T(8,128)(2,1)S(1)} %bitcast.73, bf16[70,2048]{1,0:T(8,128)(2,1)S(1)} %bitcast.68), kind=kOutput, calls=%fused_computation.21 | convolution fusion | flops 749076480 | bytes 6461440 | tf_op jit(solution)/shard_map/dot_general | solution.py:58
  50.4 1.5 %copy.39 = f32[16,140,40]{2,1,0:T(8,128)S(1)} copy(f32[16,140,40]{1,2,0:T(8,128)} %bitcast.77) | data formatting | bytes 716800 | tf_op jit(solution)/shard_map/transpose | solution.py:187
  51.9 1.9 %all_to_all.25 = f32[16,1,5600]{2,1,0:T(1,128)} reshape(f32[16,140,40]{2,1,0:T(8,128)S(1)} %copy.39) | data formatting | bytes 716800 | tf_op jit(solution)/shard_map/all_to_all | solution.py:190
  53.8 5.9 %all-to-all-start.2 = ((f32[16,1,5600]{2,1,0:T(1,128)}), f32[16,1,5600]{2,1,0:T(1,128)S(1)}, u32[]{:S(2)}, u32[]{:S(2)}) async-start(f32[16,1,5600]{2,1,0:T(1,128)} %all_to_all.25), calls=%async_computation.2 | async-start | bytes 720896 | tf_op jit(solution)/shard_map/all_to_all | solution.py:190
  59.7 0.8 dynamic_slice.6
  60.5 1.4 %constant_dynamic-slice_fusion = (f32[2,1,70,40]{3,1,2,0:T(1,128)S(1)}, f32[2,1,70,40]{3,1,2,0:T(1,128)S(1)}) fusion(f32[2,2,70,640]{3,1,2,0:T(2,128)} %param.11, s32[]{:T(128)S(6)} %select_n.17, s32[]{:T(128)S(6)} %add.110), kind=kLoop, calls=%fused_computation.121 | loop fusion | bytes 89608 | tf_op jit(solution)/shard_map/slice | solution.py:78
  61.9 0.1 copy.49
  62.0 0.1 copy.50
  62.1 5.6 %all-to-all-done.2 = f32[16,1,5600]{2,1,0:T(1,128)S(1)} async-done(((f32[16,1,5600]{2,1,0:T(1,128)}), f32[16,1,5600]{2,1,0:T(1,128)S(1)}, u32[]{:S(2)}, u32[]{:S(2)}) %all-to-all-start.2) | async-done | bytes 358432 | tf_op jit(solution)/shard_map/all_to_all | solution.py:190
  67.6 0.2 reduce_sum.81
  67.9 0.1 fusion.79
  68.0 0.1 mul.328
  68.0 0.1 copy.41
  68.1 0.1 mul.331
  68.2 0.1 copy.42
  68.3 0.1 fusion.63
  68.4 0.1 fusion.67
  68.5 0.1 multiply_convert_fusion.1
  68.6 0.1 pad_maximum_fusion.3
  68.7 0.1 copy.43
  68.8 0.1 convert_element_type.57
  68.9 0.2 broadcast_in_dim.8
  69.1 0.5 broadcast.64
  69.6 1.7 %reduce.2 = bf16[16,5600]{1,0:T(8,128)(2,1)S(1)} reduce(bf16[16,1,5600]{2,1,0:T(2,128)(2,1)S(1)} %broadcast_in_dim.8, bf16[]{:T(256)} %broadcast.64), dimensions={1}, to_apply=%broadcast_in_dim.8.reduce_sub_computation | reduce | bytes 358402 | tf_op jit(solution)/shard_map/broadcast_in_dim | solution.py:140
  71.3 0.2 reshape.128
  71.5 9.4 %all_to_all.31 = bf16[16,2,2800]{2,1,0:T(2,128)(2,1)S(1)} all-to-all(bf16[16,2,2800]{2,1,0:T(2,128)(2,1)S(1)} %reshape.128), channel_id=1, replica_groups=mesh['y'=4,'z_lo'=2,'core'=2,'x'=4,'z_hi'=4] {'y','z_lo','core'}, dimensions={0} | all-to-all | bytes 358400 | tf_op jit(solution)/shard_map/all_to_all | solution.py:141
  80.9 0.3 reshape.129
  81.2 1.1 reduce.1
  82.3 1.7 %reshape.124 = bf16[16,140,40]{2,1,0:T(8,128)(2,1)} reshape(bf16[16,5600]{1,0:T(8,128)(2,1)S(1)} %reduce.1) | data formatting | bytes 358400 | tf_op jit(solution)/shard_map/reshape | solution.py:198
  84.0 1.4 %copy.44 = bf16[16,140,40]{1,2,0:T(8,128)(2,1)S(1)} copy(bf16[16,140,40]{2,1,0:T(8,128)(2,1)} %reshape.124) | data formatting | bytes 358400 | tf_op jit(solution)/shard_map/reshape | solution.py:198
  85.4 0.3 fusion.51
  85.7 0.1 fusion.74
  85.8 0.1 fusion.77
  85.9 0.2 fusion.75
  86.1 0.4 maximum_negate_fusion
  86.5 0.6 copy-done.3
  87.1 4.8 %fusion.15 = f32[560,2048]{1,0:T(8,128)S(1)} fusion(bf16[2048,640]{1,0:T(8,128)(2,1)S(1)} %copy-done.3, bf16[2048,640]{1,0:T(8,128)(2,1)S(1)} %copy-done.1, bf16[280,640]{0,1:T(8,128)(2,1)S(1)} %maximum_negate_fusion, bf16[70,640]{0,1:T(8,128)(2,1)S(1)} %get-tuple-element.31, bf16[70,640]{0,1:T(8,128)(2,1)S(1)} %get-tuple-element.50, ...), kind=kOutput, calls=%fused_computation.25 | convolution fusion | flops 2965135360 | bytes 10905600 | tf_op jit(solution)/shard_map/dot_general | solution.py:69
  91.9 0.7 fusion.55
  92.6 0.1 pad_maximum_fusion.1
  92.7 0.1 copy.53
  92.9 0.1 slice.204
  93.0 0.2 copy.45
  93.1 0.1 pad_maximum_fusion
  93.2 24.0 %all_to_all.32 = bf16[146,16,128]{2,0,1:T(8,128)(2,1)S(1)} all-to-all(bf16[146,16,128]{2,0,1:T(8,128)(2,1)S(1)} %pad_maximum_fusion), channel_id=1, replica_groups=mesh['y'=4,'z_lo'=2,'core'=2,'x'=4,'z_hi'=4] {'x','z_hi'}, dimensions={1} | all-to-all | bytes 1196032 | tf_op jit(solution)/shard_map/all_to_all | solution.py:155
  117.2 0.1 convert_element_type.69
  117.3 0.1 slice.199
  117.4 0.1 maximum_reduce_fusion
  117.5 0.6 slice.203
  118.1 0.7 copy.46
  (19 shorter events, 0.3 us)
Async XLA Ops:
  1.9 20.2 %all-to-all-start = ((f32[16,3,128]{2,1,0:T(4,128)}), f32[16,3,128]{2,1,0:T(4,128)S(1)}, u32[]{:S(2)}, u32[]{:S(2)}) async-start(f32[16,3,128]{2,1,0:T(4,128)} %broadcast_in_dim.6), calls=%async_computation | async-start | bytes 65536 | tf_op jit(solution)/shard_map/all_to_all | solution.py:141
  23.0 22.5 %all-to-all-start.1 = ((bf16[16,140,128]{2,1,0:T(8,128)(2,1)}), bf16[16,140,128]{2,1,0:T(8,128)(2,1)S(1)}, u32[]{:S(2)}, u32[]{:S(2)}) async-start(bf16[16,140,128]{2,1,0:T(8,128)(2,1)} %broadcast_in_dim.7), calls=%async_computation.1 | async-start | bytes 1179648 | tf_op jit(solution)/shard_map/all_to_all | solution.py:141
  35.9 14.4 %copy-start = (bf16[2048,640]{1,0:T(8,128)(2,1)}, bf16[2048,640]{1,0:T(8,128)(2,1)S(1)}, u32[]{:S(2)}) copy-start(bf16[2048,640]{1,0:T(8,128)(2,1)S(1)} %get-tuple-element.36) | copy-start | bytes 7864324
  45.5 1.7 %copy-start.2 = (bf16[2048,640]{1,0:T(8,128)(2,1)S(1)}, bf16[2048,640]{1,0:T(8,128)(2,1)}, u32[]{:S(2)}) copy-start(bf16[2048,640]{1,0:T(8,128)(2,1)} %get-tuple-element.37) | copy-start | bytes 7864324
  53.8 13.8 %all-to-all-start.2 = ((f32[16,1,5600]{2,1,0:T(1,128)}), f32[16,1,5600]{2,1,0:T(1,128)S(1)}, u32[]{:S(2)}, u32[]{:S(2)}) async-start(f32[16,1,5600]{2,1,0:T(1,128)} %all_to_all.25), calls=%async_computation.2 | async-start | bytes 720896 | tf_op jit(solution)/shard_map/all_to_all | solution.py:190
  82.3 4.2 %copy-start.1 = (bf16[2048,640]{1,0:T(8,128)(2,1)S(1)}, bf16[2048,640]{1,0:T(8,128)(2,1)}, u32[]{:S(2)}) copy-start(bf16[2048,640]{1,0:T(8,128)(2,1)} %copy-done) | copy-start | bytes 7864324
  85.4 1.8 %copy-start.3 = (bf16[2048,640]{1,0:T(8,128)(2,1)S(1)}, bf16[2048,640]{1,0:T(8,128)(2,1)}, u32[]{:S(2)}) copy-start(bf16[2048,640]{1,0:T(8,128)(2,1)} %get-tuple-element.37) | copy-start | bytes 7864324

commit v11 on v8

--- a/solution.py
+++ b/solution.py
@@ -141,11 +141,11 @@
     return lax.all_to_all(spread, axis_name, 0, 0, tiled=True)
 
 
-def scatter_sum(part, axis_name, size):
+def scatter_sum(part, axis_name, size, sum_type=None):
     rows, width = part.shape
     split = part.reshape(rows, size, width // size)
     received = lax.all_to_all(split, axis_name, 1, 1, tiled=True)
-    return jnp.sum(received, axis=1)
+    return jnp.sum(received.astype(sum_type or received.dtype), axis=1)
 
 
 def scatter_dir(part, sizes):
@@ -184,7 +184,7 @@
     partial_fields = field_terms(domain_rows, cos_tile, sin_tile)
     dir_count = polar.shape[0]
     slice_width = dir_count // dom_size
-    fields_slice = scatter_sum(partial_fields, DOM_AXES, dom_size)
+    fields_slice = scatter_sum(partial_fields.astype(jnp.bfloat16), DOM_AXES, dom_size, jnp.float32)
     offset = lax.axis_index(DOM_AXES) * slice_width
     farmap_slice = lax.dynamic_slice_in_dim(farmap, offset, slice_width, 3)
     weights_slice = lax.dynamic_slice_in_dim(weights, offset, slice_width, 0)

time: 115 us -> 111 us (0.965)
  waiting for transfers between devices: 26.2 us -> 18.9 us
  local copies, waits for them, and re-layouts: 9.94 us -> 14.5 us
  matrix products: 7.95 us -> 5.88 us
    all_to_all x1, waiting for transfers between devices: 8.85 us -> 1.5 us  [scatter_sum(): received = lax.all_to_all(split, axis_name, 1, 1, tiled=True)]
    unnamed x13, local copies, waits for them, and re-layouts: 3.19 us -> 6.18 us
    dot_general x1, matrix products: 3.08 us -> 1.11 us  [field_terms(): return jnp.dot(left_side, right_side, preferred_element_type=jnp.float32)]
  transfers between devices with their start and end apart: 3 -> 3, of which waited for: 3 -> 3; matrix products, arithmetic and copies ran while one was open for 12% -> 16% of each run, Pallas kernels for 0% -> 0%
where the time goes in v11:
time: 111 us; the launch traced here: 110 us
  blocking collectives  36 us (32%)
  starting transfers between devices  19.7 us (18%)
  waiting for transfers between devices  18.9 us (17%)
  local copies, waits for them, and re-layouts  14.5 us (13%)
  other arithmetic  14.1 us (13%)
  matrix products  5.88 us (5%)
    all_to_all x1, blocking collectives, scatter_dir(): received = lax.all_to_all(narrow_rows(split), DIR_AXES, 1, 1, tiled=True)  24.3 us
    all_to_all x2, waiting for transfers between devices, gather_blocks(): return lax.all_to_all(spread, axis_name, 0, 0, tiled=True)  17.4 us
    all_to_all x2, starting transfers between devices, gather_blocks(): return lax.all_to_all(spread, axis_name, 0, 0, tiled=True)  13.7 us
    all_to_all x1, blocking collectives, gather_blocks(): return lax.all_to_all(spread, axis_name, 0, 0, tiled=True)  11.6 us
    convert_element_type x1, other arithmetic, phase_tile(): return (cos_value.astype(jnp.bfloat16), sin_value.astype(jnp.bfloat16))  9.33 us
    unnamed x13, local copies, waits for them, and re-layouts  6.18 us
    all_to_all x1, starting transfers between devices, scatter_sum(): received = lax.all_to_all(split, axis_name, 1, 1, tiled=True)  5.94 us
    dot_general x1, matrix products, adjoint_terms(): lax.dot_general(left_side, right_side, (((1,), (1,)), ((), ())), preferre...  4.78 us
  transfers between devices with their start and end apart: 3, of which 3 were waited for; matrix products, arithmetic and copies ran while one was open for 16% of the time, Pallas kernels for 0%

profile of v11, /device:TPU:32, one launch (start us, length us, event | category | flops | bytes accessed | tf_op | source)
XLA Modules:
  0.0 109.8 jit_solution(1348649333050070629)
XLA Ops:
  0.6 1.3 %broadcast_in_dim.6 = f32[16,3,128]{2,1,0:T(4,128)} broadcast(f32[3,128]{1,0:T(4,128)} %param.7), dimensions={1,2} | broadcast | bytes 26112 | tf_op jit(solution)/shard_map/broadcast_in_dim | solution.py:140
  1.9 10.1 %all-to-all-start = ((f32[16,3,128]{2,1,0:T(4,128)}), f32[16,3,128]{2,1,0:T(4,128)S(1)}, u32[]{:S(2)}, u32[]{:S(2)}) async-start(f32[16,3,128]{2,1,0:T(4,128)} %broadcast_in_dim.6), calls=%async_computation | async-start | bytes 65536 | tf_op jit(solution)/shard_map/all_to_all | solution.py:141
  12.1 0.7 fusion.85
  12.8 0.7 cosine_multiply_fusion
  13.5 0.8 copy.14
  14.3 7.8 %all-to-all-done = f32[16,3,128]{2,1,0:T(4,128)S(1)} async-done(((f32[16,3,128]{2,1,0:T(4,128)}), f32[16,3,128]{2,1,0:T(4,128)S(1)}, u32[]{:S(2)}, u32[]{:S(2)}) %all-to-all-start) | async-done | bytes 24608 | tf_op jit(solution)/shard_map/all_to_all | solution.py:141
  22.1 0.9 broadcast_in_dim.7
  23.0 3.6 %all-to-all-start.1 = ((bf16[16,140,128]{2,1,0:T(8,128)(2,1)}), bf16[16,140,128]{2,1,0:T(8,128)(2,1)S(1)}, u32[]{:S(2)}, u32[]{:S(2)}) async-start(bf16[16,140,128]{2,1,0:T(8,128)(2,1)} %broadcast_in_dim.7), calls=%async_computation.1 | async-start | bytes 1179648 | tf_op jit(solution)/shard_map/all_to_all | solution.py:141
  26.6 9.3 %fusion.9 = (bf16[2048,640]{1,0:T(8,128)(2,1)S(1)}, bf16[2048,640]{1,0:T(8,128)(2,1)}) fusion(f32[640]{0:T(1024)S(1)} %get-tuple-element.44, f32[2048]{0:T(1024)S(1)} %bitcast.88, f32[640]{0:T(1024)S(1)} %get-tuple-element.42, f32[2048]{0:T(1024)S(1)} %bitcast.89, f32[640]{0:T(1024)S(1)} %get-tuple-element.41, f32[2048]{0:T(1024)S(1)} %bitcast.87), kind=kLoop, calls=%fused_computation.19 | loop fusion | flops 61603840 | bytes 5275136 | tf_op jit(solution)/shard_map/convert_element_type | solution.py:47
  35.9 9.6 %all-to-all-done.1 = bf16[16,140,128]{2,1,0:T(8,128)(2,1)S(1)} async-done(((bf16[16,140,128]{2,1,0:T(8,128)(2,1)}), bf16[16,140,128]{2,1,0:T(8,128)(2,1)S(1)}, u32[]{:S(2)}, u32[]{:S(2)}) %all-to-all-start.1) | async-done | bytes 573472 | tf_op jit(solution)/shard_map/all_to_all | solution.py:141
  45.5 0.0 copy-start
  45.5 0.1 fusion.78
  45.7 0.1 copy.24
  45.9 0.1 copy.23
  46.0 0.1 neg.12
  46.0 1.3 %copy-done = bf16[2048,640]{1,0:T(8,128)(2,1)S(1)} copy-done((bf16[2048,640]{1,0:T(8,128)(2,1)S(1)}, bf16[2048,640]{1,0:T(8,128)(2,1)}, u32[]{:S(2)}) %copy-start) | copy-done | bytes 2621464
  47.3 1.1 %fusion.51 = bf16[140,640]{1,0:T(8,128)(2,1)S(1)} fusion(bf16[2048,640]{1,0:T(8,128)(2,1)S(1)} %copy-done, bf16[2048,640]{1,0:T(8,128)(2,1)S(1)} %get-tuple-element.36, bf16[70,2048]{1,0:T(8,128)(2,1)S(1)} %neg.12, bf16[70,2048]{1,0:T(8,128)(2,1)S(1)} %bitcast.72, bf16[70,2048]{1,0:T(8,128)(2,1)S(1)} %bitcast.66), kind=kOutput, calls=%fused_computation.68 | convolution fusion | flops 749166080 | bytes 6282240 | tf_op jit(solution)/shard_map/dot_general | solution.py:58
  48.4 0.9 copy.17
  49.3 5.9 %all-to-all-start.2 = ((bf16[140,16,40]{0,2,1:T(8,128)(2,1)}), bf16[140,16,40]{0,2,1:T(8,128)(2,1)S(1)}, u32[]{:S(2)}, u32[]{:S(2)}) async-start(bf16[140,16,40]{0,2,1:T(8,128)(2,1)} %bitcast.71), calls=%async_computation.2 | async-start | bytes 655360 | tf_op jit(solution)/shard_map/all_to_all | solution.py:147
  55.2 0.8 dynamic_slice.6
  56.0 2.1 %constant_dynamic-slice_fusion = (f32[2,1,70,40]{3,1,2,0:T(1,128)}, f32[2,1,70,40]{3,1,2,0:T(1,128)}) fusion(f32[2,2,70,640]{3,1,2,0:T(2,128)} %param.11, s32[]{:T(128)S(6)} %select_n.17, s32[]{:T(128)S(6)} %add.109), kind=kLoop, calls=%fused_computation.123 | loop fusion | bytes 89608 | tf_op jit(solution)/shard_map/slice | solution.py:78
  58.1 1.6 %copy.21 = f32[2,1,70,40]{2,3,0,1:T(8,128)} copy(f32[2,1,70,40]{3,1,2,0:T(1,128)} %get-tuple-element.19) | data formatting | bytes 44800
  59.7 1.6 %copy.22 = f32[2,1,70,40]{2,3,0,1:T(8,128)} copy(f32[2,1,70,40]{3,1,2,0:T(1,128)} %get-tuple-element.20) | data formatting | bytes 44800
  61.3 1.5 %all-to-all-done.2 = bf16[140,16,40]{0,2,1:T(8,128)(2,1)S(1)} async-done(((bf16[140,16,40]{0,2,1:T(8,128)(2,1)}), bf16[140,16,40]{0,2,1:T(8,128)(2,1)S(1)}, u32[]{:S(2)}, u32[]{:S(2)}) %all-to-all-start.2) | async-done | bytes 179232 | tf_op jit(solution)/shard_map/all_to_all | solution.py:147
  62.8 0.1 convert_reduce_fusion
  62.8 0.0 copy-start.1
  62.8 0.1 fusion.83
  62.9 1.1 fusion.68
  64.0 0.9 fusion.72
  64.9 0.1 multiply_convert_fusion.1
  64.9 0.1 pad_maximum_fusion.3
  65.1 11.6 %all_to_all.25 = bf16[16,140,40]{1,2,0:T(8,128)(2,1)S(1)} all-to-all(bf16[16,140,40]{1,2,0:T(8,128)(2,1)S(1)} %broadcast_in_dim.8), channel_id=1, replica_groups=mesh['y'=4,'z_lo'=2,'core'=2,'x'=4,'z_hi'=4] {'y','z_lo','core'}, dimensions={0} | all-to-all | bytes 358400 | tf_op jit(solution)/shard_map/all_to_all | solution.py:141
  76.7 0.1 fusion.79
  76.8 0.3 fusion.56
  77.1 0.1 fusion.82
  77.2 0.2 fusion.80
  77.4 0.4 maximum_negate_fusion
  77.8 0.0 copy-done.1
  77.8 4.8 %fusion.15 = f32[560,2048]{1,0:T(8,128)S(1)} fusion(bf16[2048,640]{1,0:T(8,128)(2,1)S(1)} %copy-done.1, bf16[2048,640]{1,0:T(8,128)(2,1)S(1)} %get-tuple-element.36, bf16[280,640]{0,1:T(8,128)(2,1)S(1)} %maximum_negate_fusion, bf16[70,640]{0,1:T(8,128)(2,1)S(1)} %get-tuple-element.29, bf16[70,640]{0,1:T(8,128)(2,1)S(1)} %get-tuple-element.48, ...), kind=kOutput, calls=%fused_computation.25 | convolution fusion | flops 2965135360 | bytes 10905600 | tf_op jit(solution)/shard_map/dot_general | solution.py:69
  82.6 0.6 fusion.60
  83.4 0.1 pad_maximum_fusion.1
  83.5 0.1 copy.25
  83.6 0.1 slice.186
  83.7 0.2 copy.18
  83.8 0.1 pad_maximum_fusion
  83.9 24.3 %all_to_all.26 = bf16[146,16,128]{2,0,1:T(8,128)(2,1)S(1)} all-to-all(bf16[146,16,128]{2,0,1:T(8,128)(2,1)S(1)} %pad_maximum_fusion), channel_id=1, replica_groups=mesh['y'=4,'z_lo'=2,'core'=2,'x'=4,'z_hi'=4] {'x','z_hi'}, dimensions={1} | all-to-all | bytes 1196032 | tf_op jit(solution)/shard_map/all_to_all | solution.py:155
  108.3 0.1 convert_element_type.73
  108.4 0.1 slice.181
  108.5 0.1 maximum_reduce_fusion
  108.5 0.6 slice.185
  109.1 0.7 copy.19
  (14 shorter events, 0.3 us)
Async XLA Ops:
  1.9 20.2 %all-to-all-start = ((f32[16,3,128]{2,1,0:T(4,128)}), f32[16,3,128]{2,1,0:T(4,128)S(1)}, u32[]{:S(2)}, u32[]{:S(2)}) async-start(f32[16,3,128]{2,1,0:T(4,128)} %broadcast_in_dim.6), calls=%async_computation | async-start | bytes 65536 | tf_op jit(solution)/shard_map/all_to_all | solution.py:141
  23.0 22.5 %all-to-all-start.1 = ((bf16[16,140,128]{2,1,0:T(8,128)(2,1)}), bf16[16,140,128]{2,1,0:T(8,128)(2,1)S(1)}, u32[]{:S(2)}, u32[]{:S(2)}) async-start(bf16[16,140,128]{2,1,0:T(8,128)(2,1)} %broadcast_in_dim.7), calls=%async_computation.1 | async-start | bytes 1179648 | tf_op jit(solution)/shard_map/all_to_all | solution.py:141
  45.5 1.7 %copy-start = (bf16[2048,640]{1,0:T(8,128)(2,1)S(1)}, bf16[2048,640]{1,0:T(8,128)(2,1)}, u32[]{:S(2)}) copy-start(bf16[2048,640]{1,0:T(8,128)(2,1)} %get-tuple-element.37) | copy-start | bytes 7864324
  49.3 13.5 %all-to-all-start.2 = ((bf16[140,16,40]{0,2,1:T(8,128)(2,1)}), bf16[140,16,40]{0,2,1:T(8,128)(2,1)S(1)}, u32[]{:S(2)}, u32[]{:S(2)}) async-start(bf16[140,16,40]{0,2,1:T(8,128)(2,1)} %bitcast.71), calls=%async_computation.2 | async-start | bytes 655360 | tf_op jit(solution)/shard_map/all_to_all | solution.py:147
  62.8 15.0 %copy-start.1 = (bf16[2048,640]{1,0:T(8,128)(2,1)S(1)}, bf16[2048,640]{1,0:T(8,128)(2,1)}, u32[]{:S(2)}) copy-start(bf16[2048,640]{1,0:T(8,128)(2,1)} %get-tuple-element.37) | copy-start | bytes 7864324
